TPU v7x, 256 devices: a whole 4x4x8 slice. The times are simulated.
256 devices in a mesh: row: 32 (over y, z), col: 8 (over x, core).
Axes of the slice: x: 4, y: 4, z: 8, core: 2. Of those that a mesh axis runs over, the one named last changes fastest.
Arguments:
- responses: bfloat16 [4096, 2, 3, 2048], P(('col', 'row')), may hold values from -6 to 6
- labels: int32 [2048], replicated, may hold values from 0 to 15
- conductivity: float32 [16], replicated, may hold values from 0.05 to 2
- permittivity: float32 [16], replicated, may hold values from 0.1 to 1.6
Outputs:
- noise_cov: float32 [2, 4096, 4096], P(None, 'row', 'col')
- energy_gram: float32 [2, 4096, 4096], P(None, 'row', 'col')
All inputs are finite; a program needn't handle non-finite values.
Results may differ from a plain program's by a relative error of at most 0.0021.
Values may be sent and summed in bfloat16 or wider, within the bound.
No kernel may reach another device: no remote copies, remote signals or barrier semaphores. Data moves between devices by JAX's collectives and lax.ppermute only.
A program may use at most 128 MiB of HBM per device.

v0:
```python
import jax
import jax.numpy as jnp
from jax import lax
from jax.sharding import PartitionSpec as P


def broadcast(block, axis, holder):
    block = jnp.where(lax.axis_index(axis) == holder, block, jnp.zeros_like(block))
    return lax.psum(block, axis)


def tile_products(row_fields, right_fields, vox_labels, conductivity, permittivity, scale_factor):
    classes = jnp.arange(conductivity.shape[0], dtype=jnp.int32)
    onehot = (vox_labels[None, :] == classes[:, None]).astype(jnp.float32)
    cond_voxel = jnp.sum(onehot * conductivity[:, None], axis=0) * scale_factor
    perm_voxel = jnp.sum(onehot * permittivity[:, None], axis=0) * scale_factor
    fields = row_fields.astype(jnp.float32)
    vox_here = row_fields.shape[3]
    row_total = row_fields.shape[0]

    def weighted(weight_vec):
        scaled = fields * weight_vec[None, None, None, :]
        crossed = jnp.concatenate([-scaled[:, 1:2], scaled[:, 0:1]], axis=1)
        return (scaled.astype(jnp.bfloat16), crossed.astype(jnp.bfloat16))

    sig_plain, sig_cross = weighted(cond_voxel)
    eps_plain, eps_cross = weighted(perm_voxel)
    left_stack = jnp.concatenate([sig_plain, sig_cross, eps_plain, eps_cross], axis=0)
    left_stack = left_stack.reshape(4 * row_total, 6 * vox_here)
    right_flat = right_fields.reshape(right_fields.shape[0], 6 * vox_here)
    products = lax.dot_general(
        left_stack, right_flat, (((1,), (1,)), ((), ())), preferred_element_type=jnp.float32
    )
    return products.reshape(4, row_total, right_fields.shape[0])


def body(responses, labels, conductivity, permittivity):
    nb_dev = responses.shape[0]
    vox_total = labels.shape[0]
    row_count = lax.axis_size("row")
    col_count = lax.axis_size("col")
    row_block = nb_dev * col_count
    row_index = lax.axis_index("row")
    scale_factor = 1.0 / jnp.sqrt(jnp.float32(6 * vox_total))
    columns = lax.all_gather(responses, "row", axis=0, tiled=True)
    row_ratio = row_count // col_count
    own_rows = lax.dynamic_slice_in_dim(columns, row_index % row_ratio * row_block, row_block, 0)
    row_fields = broadcast(own_rows, "col", row_index // row_ratio)
    products = tile_products(row_fields, columns, labels, conductivity, permittivity, scale_factor)
    noise_cov = products[0:2]
    energy_gram = products[2:4]
    return (noise_cov, energy_gram)


def solution(mesh):
    in_specs = (P(("col", "row"), None, None, None), P(), P(), P())
    out_specs = (P(None, "row", "col"), P(None, "row", "col"))
    return jax.shard_map(body, mesh=mesh, in_specs=in_specs, out_specs=out_specs, check_vma=False)
```

profile of v0, /device:TPU:8, one launch (start us, length us, event | category | flops | bytes accessed | tf_op | source)
XLA Modules:
  0.0 240.6 jit_solution(9226071765441624125)
XLA Ops:
  7.2 0.0 copy-start.4
  7.2 0.0 copy-start.3
  7.2 0.0 copy-start.2
  7.2 0.0 all-gather.2.cloned.1.call-start
  7.2 1.9 copy.7
  9.1 0.0 all-gather.2.cloned.1.call-update
  9.1 0.0 all-reduce.2.cloned.1.call-start
  9.2 123.3 %all-gather.2.cloned.1.call-done = bf16[512,2,3,2048]{3,0,2,1:T(8,128)(2,1)} async-done(((bf16[16,2,3,2048]{3,0,2,1:T(8,128)(2,1)}), bf16[512,2,3,2048]{3,0,2,1:T(8,128)(2,1)}) %all-gather.2.cloned.1.call-update) | async-done | bytes 12582928 | tf_op jit(solution)/shard_map/all_gather | solution.py:45
  132.5 4.5 %dynamic-slice_select_fusion = bf16[128,2,3,2048]{3,0,2,1:T(8,128)(2,1)} fusion(bf16[512,2,3,2048]{3,0,2,1:T(8,128)(2,1)} %all-gather.2.cloned.1.call-done, s32[]{:T(128)S(6)} %select_n.25, pred[]{:T(512)S(6)} %eq.18), kind=kLoop, calls=%fused_computation.18 | loop fusion | flops 1572864 | bytes 6291461 | tf_op jit(solution)/shard_map/jit(_where)/select_n | solution.py:8
  137.0 0.0 all-reduce.2.cloned.1.call-update
  137.0 0.0 copy-done.4
  137.0 0.0 copy-done.3
  137.1 0.0 copy-done.2
  137.1 0.1 select_reduce_fusion.1
  137.2 72.5 %all-reduce.2.cloned.1.call-done = bf16[128,2,3,2048]{3,0,2,1:T(8,128)(2,1)} async-done(((bf16[128,2,3,2048]{3,0,2,1:T(8,128)(2,1)}), bf16[128,2,3,2048]{3,0,2,1:T(8,128)(2,1)}) %all-reduce.2.cloned.1.call-update) | async-done | bytes 3145744 | tf_op jit(solution)/shard_map/psum | solution.py:9
  209.7 6.8 %convert_multiply_fusion.1 = (f32[128,2,3,2048]{3,0,2,1:T(8,128)S(1)}, bf16[128,2,3,2048]{3,0,2,1:T(8,128)(2,1)}, bf16[128,2,3,2048]{3,0,2,1:T(8,128)(2,1)}, f32[128,2,3,2048]{3,0,2,1:T(8,128)S(1)}) fusion(bf16[128,2,3,2048]{3,0,2,1:T(8,128)(2,1)} %all-reduce.2.cloned.1.call-done, f32[2048]{0:T(1024)S(1)} %get-tuple-element.13, f32[2048]{0:T(1024)S(1)} %get-tuple-element.12), kind=kLoop, calls=%fused_computation.13 | loop fusion | flops 7864320 | bytes 22036480 | tf_op jit(solution)/shard_map/mul | solution.py:22
  216.5 0.0 copy-start
  216.5 0.0 copy-start.1
  216.5 0.2 fusion.13
  216.7 0.2 fusion.12
  217.0 1.4 copy-done
  218.4 0.2 slice.35
  218.5 0.8 copy-done.1
  219.3 0.2 slice.37
  219.5 13.2 %fusion.14 = f32[512,512]{1,0:T(8,128)S(1)} fusion(bf16[512,2,3,2048]{3,0,2,1:T(8,128)(2,1)} %all-gather.2.cloned.1.call-done, bf16[128,1,3,2048]{3,0,2,1:T(8,128)(2,1)S(1)} %slice.37, bf16[128,1,3,2048]{3,0,2,1:T(8,128)(2,1)S(1)} %fusion.12, bf16[128,2,3,2048]{3,0,2,1:T(8,128)(2,1)S(1)} %copy-done.1, bf16[128,1,3,2048]{3,0,2,1:T(8,128)(2,1)S(1)} %slice.35, ...), kind=kOutput, calls=%fused_computation.19 | convolution fusion | flops 6517948416 | bytes 26214400 | tf_op jit(solution)/shard_map/dot_general | solution.py:31
  232.7 1.0 fusion.20
  (1 shorter events, 0.0 us)
Async XLA Ops:
  7.2 129.9 %copy-start.4 = (f32[16]{0:T(128)S(1)}, f32[16]{0:T(128)}, u32[]{:S(2)}) copy-start(f32[16]{0:T(128)} %param.7) | copy-start | bytes 196
  7.2 129.9 %copy-start.3 = (f32[16]{0:T(128)S(1)}, f32[16]{0:T(128)}, u32[]{:S(2)}) copy-start(f32[16]{0:T(128)} %param.6) | copy-start | bytes 196
  7.2 129.9 %copy-start.2 = (s32[2048]{0:T(1024)S(1)}, s32[2048]{0:T(1024)}, u32[]{:S(2)}) copy-start(s32[2048]{0:T(1024)} %param.5) | copy-start | bytes 24580
  7.2 125.3 %all-gather.2.cloned.1.call-start = ((), (), s32[]{:S(2)}) async-start(), calls=%async_computation | async-start | bytes 12976128 | tf_op jit(solution)/shard_map/all_gather | solution.py:45
  9.1 200.5 %all-reduce.2.cloned.1.call-start = ((), (), s32[]{:S(2)}) async-start(), calls=%async_computation.1 | async-start | bytes 6291456 | tf_op jit(solution)/shard_map/psum | solution.py:9
  216.5 1.9 copy-start
  216.5 2.8 %copy-start.1 = (bf16[128,2,3,2048]{3,0,2,1:T(8,128)(2,1)S(1)}, bf16[128,2,3,2048]{3,0,2,1:T(8,128)(2,1)}, u32[]{:S(2)}) copy-start(bf16[128,2,3,2048]{3,0,2,1:T(8,128)(2,1)} %get-tuple-element.8) | copy-start | bytes 9437188
Sparse Core Ops, SparseCore 0:
  11.2 121.3 all-gather.1
  137.2 72.4 all-reduce.1
where the time goes:
time: 241 us
  waiting for transfers between devices  196 us (81%)
  between operations  14.2 us (6%)
  matrix products  13.2 us (5%)
  other arithmetic  11.9 us (5%)
  local copies, waits for them, and re-layouts  5.42 us (2%)
    all_gather x1, waiting for transfers between devices, body(): columns = lax.all_gather(responses, 'row', axis=0, tiled=True)  123 us
    psum x1, waiting for transfers between devices, broadcast(): return lax.psum(block, axis)  72.5 us
    dot_general x1, matrix products, tile_products(): lax.dot_general(left_stack, right_flat, (((1,), (1,)), ((), ())), preferr...  13.2 us
    mul x1, other arithmetic, weighted(): scaled = fields * weight_vec[None, None, None, :]  6.83 us
  transfers between devices with their start and end apart: 2, of which 2 were waited for; matrix products, arithmetic and copies ran while one was open for 0% of the time, Pallas kernels for 0%

commit v1 on v0

v1 whole, which is shorter than its diff:
```python
import jax
import jax.numpy as jnp
from jax import lax
from jax.experimental import pallas as pl
from jax.experimental.pallas import tpu as pltpu
from jax.sharding import PartitionSpec as P

NY, NZ, NX, NC = 4, 8, 4, 2
NQ = 512
KQ = 6 * NQ
BF = jnp.bfloat16
F32 = jnp.float32
VMEM_LIMIT = 56 * 1024 * 1024

BATCHES = ((0, 7, 1), (6, 2), (5, 3, 4))


def row_permute(v, move):
    pairs = []
    for y in range(NY):
        for z in range(NZ):
            y2, z2 = move(y, z)
            pairs.append((y * NZ + z, y2 % NY * NZ + z2 % NZ))
    return lax.ppermute(v, "row", pairs)


def col_permute(v, move):
    pairs = []
    for x in range(NX):
        for c in range(NC):
            x2, c2 = move(x, c)
            pairs.append((x * NC + c, x2 % NX * NC + c2 % NC))
    return lax.ppermute(v, "col", pairs)


def all_permute(v, move):
    pairs = []
    for y in range(NY):
        for z in range(NZ):
            for x in range(NX):
                for c in range(NC):
                    y2, z2, x2, c2 = move(y, z, x, c)
                    pairs.append((((y * NZ + z) * NX + x) * NC + c, ((y2 * NZ + z2) * NX + x2) * NC + c2))
    return lax.ppermute(v, ("row", "col"), pairs)


def pick(stack, i):
    return lax.dynamic_index_in_dim(stack, i, 0, keepdims=False)


def prep_kernel(pos_ref, w_ref, *refs):
    ins, out_ref = refs[:-1], refs[-1]
    y, c = pos_ref[0], pos_ref[1]
    half = len(ins) // 2
    for lane in range(2):
        lane_row = 64 * (c if lane == 0 else 1 - c)
        t = 0
        for ref in ins[lane * half:(lane + 1) * half]:
            for j in range(ref.shape[0]):
                off = pl.multiple_of(lane_row + 16 * lax.rem(y - t + NY, NY), 16)
                for m in range(6):
                    v = ref[j, m].astype(F32)
                    for k in range(2):
                        out_ref[k, pl.ds(off, 16), m * NQ:(m + 1) * NQ] = (v * w_ref[k:k + 1]).astype(BF)
                t += 1


def prep(pos, w, own, other):
    args = (*own, *other)
    return pl.pallas_call(
        prep_kernel,
        out_shape=jax.ShapeDtypeStruct((2, 128, KQ), BF),
        in_specs=[pl.BlockSpec(memory_space=pltpu.SMEM)] + [pl.BlockSpec(memory_space=pltpu.VMEM)] * (1 + len(args)),
        out_specs=pl.BlockSpec(memory_space=pltpu.VMEM),
        compiler_params=pltpu.CompilerParams(vmem_limit_bytes=VMEM_LIMIT),
        name="weigh",
    )(pos, w, *args)


def batch_kernel(n, counts, pos_ref, *refs):
    npieces = len(counts)
    pieces = refs[:npieces]
    lhs = refs[npieces:npieces + 4]
    outs = refs[npieces + 4:npieces + 8]
    rhs, left, sems = refs[npieces + 8:]
    y = pos_ref[0]
    copies = [pltpu.make_async_copy(lhs[r], left.at[r], sems.at[r]) for r in range(4)]
    for cp in copies:
        cp.start()
    nc = 64 * n
    p, t = 0, 0
    for ref, cnt in zip(pieces, counts):
        for j in range(cnt):
            ys = lax.rem(y - t + NY, NY)
            off = pl.multiple_of(ys * (16 * n) + 16 * p, 16)
            off2 = pl.multiple_of(nc + ys * (16 * n) + 16 * p, 16)
            for m in range(3):
                re = ref[j, m]
                im = ref[j, m + 3]
                rhs[pl.ds(off, 16), m * NQ:(m + 1) * NQ] = re
                rhs[pl.ds(off, 16), (m + 3) * NQ:(m + 4) * NQ] = im
                rhs[pl.ds(off2, 16), m * NQ:(m + 1) * NQ] = im
                rhs[pl.ds(off2, 16), (m + 3) * NQ:(m + 4) * NQ] = -re
            t += 1
        if t == NY:
            p, t = p + 1, 0
    for r in range(4):
        copies[r].wait()
        a = left[r].reshape(256, KQ)
        res = lax.dot_general(a, rhs[...], (((1,), (1,)), ((), ())), preferred_element_type=F32)
        s = pos_ref[2 + r]
        for k in range(4):
            @pl.when(s == k)
            def _():
                outs[k][...] = res.astype(outs[k].dtype)


def batch(pos, pieces, lhs, n):
    counts = tuple(v.shape[0] for v in pieces)
    width = 128 * n
    flops = 2 * 1024 * width * KQ
    return pl.pallas_call(
        lambda *refs: batch_kernel(n, counts, *refs),
        out_shape=[jax.ShapeDtypeStruct((256, width), F32 if k == 0 else BF) for k in range(4)],
        in_specs=[pl.BlockSpec(memory_space=pltpu.SMEM)] + [pl.BlockSpec(memory_space=pltpu.VMEM)] * len(pieces)
        + [pl.BlockSpec(memory_space=pl.ANY)] * 4,
        out_specs=[pl.BlockSpec(memory_space=pltpu.VMEM)] * 4,
        scratch_shapes=[pltpu.VMEM((width, KQ), BF), pltpu.VMEM((4, 2, 128, KQ), BF), pltpu.SemaphoreType.DMA((4,))],
        compiler_params=pltpu.CompilerParams(vmem_limit_bytes=VMEM_LIMIT),
        cost_estimate=pl.CostEstimate(flops=flops, transcendentals=0, bytes_accessed=8 << 20),
        name="partial_gram",
    )(pos, *pieces, *lhs)


def final_kernel(nb, *refs):
    parts = refs[:4 * nb]
    sels = refs[4 * nb:5 * nb]
    noise_ref, energy_ref = refs[5 * nb:]
    total = None
    for b in range(nb):
        own, *rest = parts[4 * b:4 * b + 4]
        v = own[...]
        for r in rest:
            v = v + r[...].astype(F32)
        hi = v.astype(BF)
        lo = (v - hi.astype(F32)).astype(BF)
        sel = sels[b][...]
        for u in (hi, lo):
            d = jnp.dot(u, sel, preferred_element_type=F32)
            total = d if total is None else total + d
    for e in range(2):
        noise_ref[e] = total[0:128, e * 512:(e + 1) * 512]
        energy_ref[e] = total[128:256, e * 512:(e + 1) * 512]


def final(parts, sels):
    nb = len(sels)
    shape = jax.ShapeDtypeStruct((2, 128, 512), F32)
    return pl.pallas_call(
        lambda *refs: final_kernel(nb, *refs),
        out_shape=[shape, shape],
        in_specs=[pl.BlockSpec(memory_space=pltpu.VMEM)] * (5 * nb),
        out_specs=[pl.BlockSpec(memory_space=pltpu.VMEM)] * 2,
        compiler_params=pltpu.CompilerParams(vmem_limit_bytes=VMEM_LIMIT),
        name="collect",
    )(*[v for four in parts for v in four], *sels)


def selection(offsets, z):
    n = len(offsets)
    e = jnp.arange(2)[:, None, None, None]
    ys = jnp.arange(NY)[None, :, None, None]
    zs = ((z + jnp.array(offsets, jnp.int32)) % NZ)[None, None, :, None]
    i = jnp.arange(16)[None, None, None, :]
    target = (512 * e + 128 * ys + 16 * zs + i).reshape(128 * n, 1)
    return (target == jnp.arange(1024)[None, :]).astype(BF)


def body(responses, labels, conductivity, permittivity):
    row = lax.axis_index("row")
    col = lax.axis_index("col")
    y, z = row // NZ, row % NZ
    x, c = col // NC, col % NC
    pos = jnp.stack([y, c] + [(x + r - y) % NY for r in range(4)]).astype(jnp.int32)

    classes = jnp.arange(conductivity.shape[0], dtype=jnp.int32)
    labels_q = lax.dynamic_slice_in_dim(labels, y * NQ, NQ, 0)
    onehot = (labels_q[None, :] == classes[:, None]).astype(F32)
    scale = 1.0 / jnp.sqrt(jnp.float32(6 * labels.shape[0]))
    w = jnp.stack([jnp.sum(onehot * t[:, None], axis=0) * scale for t in (conductivity, permittivity)])
    sels = [selection(o, z) for o in BATCHES]

    quarters = responses.reshape(16, 2, 3, NY, NQ).transpose(3, 1, 2, 0, 4).reshape(NY, 6, 16, NQ)

    sent = [pick(quarters, (y + s) % NY) for s in range(NY)]
    cols = jnp.stack([sent[0]] + [row_permute(sent[s], lambda a, b, s=s: (a + s, b)) for s in (1, 2, 3)])
    mine = jnp.stack([
        all_permute(pick(quarters, (z + t) % NY), lambda y, z, x, c, t=t: ((z + t) % NY, NY * c + y, x, z // 4))
        for t in range(4)
    ])

    up = row_permute(cols, lambda a, b: (a, b + 1))
    down = row_permute(cols, lambda a, b: (a, b - 1))
    left = col_permute(mine, lambda a, b: (a + 1, b))
    right = col_permute(mine, lambda a, b: (a - 1, b))
    far1 = col_permute(left[:2], lambda a, b: (a + 1, b))
    far2 = col_permute(right[2:], lambda a, b: (a - 1, b))
    up2 = row_permute(up, lambda a, b: (a, b + 1))
    down2 = row_permute(down, lambda a, b: (a, b - 1))

    def swap(v):
        return col_permute(v, lambda a, b: (a, 1 - b))

    lhs = [prep(pos, w, own, [swap(v) for v in own]) for own in ([mine], [right], [far1, far2], [left])]
    up3 = row_permute(up2, lambda a, b: (a, b + 1))
    down3 = row_permute(down2, lambda a, b: (a, b - 1))
    up4 = row_permute(up3[:2], lambda a, b: (a, b + 1))
    down4 = row_permute(down3[2:], lambda a, b: (a, b - 1))

    parts = []
    for pieces, offsets in zip(([cols, up, down], [up2, down2], [up3, down3, up4, down4]), BATCHES):
        outs = batch(pos, pieces, lhs, len(offsets))
        parts.append([outs[0]] + [row_permute(outs[s], lambda a, b, s=s: (a + s, b)) for s in (1, 2, 3)])
    return tuple(final(parts, sels))


def solution(mesh):
    in_specs = (P(("col", "row"), None, None, None), P(), P(), P())
    out_specs = (P(None, "row", "col"), P(None, "row", "col"))
    return jax.shard_map(body, mesh=mesh, in_specs=in_specs, out_specs=out_specs, check_vma=False)
```

time: 241 us -> 132 us (0.55)
  waiting for transfers between devices: 196 us -> 12.4 us
  starting transfers between devices: 0.08 us -> 60.3 us
  Pallas kernels: 0 us -> 38.1 us
  matrix products: 13.2 us -> 0 us
  between operations: 14.2 us -> 1.26 us
  other arithmetic: 11.9 us -> 6.99 us
  local copies, waits for them, and re-layouts: 5.42 us -> 10.3 us
    all_gather x1 -> x0, waiting for transfers between devices: 123 us -> none  [body(): columns = lax.all_gather(responses, 'row', axis=0, tiled=True)]
    psum x1 -> x0, waiting for transfers between devices: 72.5 us -> none  [broadcast(): return lax.psum(block, axis)]
    ppermute x0 -> x33, starting transfers between devices: none -> 60.3 us  [the longest x20 37.5 us: row_permute(): return lax.ppermute(v, 'row', pairs)]
    pallas_call x0 -> x8, Pallas kernels: none -> 38.1 us  [the longest x3 23.1 us: batch(): pl.pallas_call(lambda *refs: batch_kernel(n, counts, *refs), out_shape=[j...]
    dot_general x1 -> x0, matrix products: 13.2 us -> none  [tile_products(): lax.dot_general(left_stack, right_flat, (((1,), (1,)), ((), ())), preferr...]
    ppermute x0 -> x33, waiting for transfers between devices: none -> 12.4 us  [the longest x20 11 us: row_permute(): return lax.ppermute(v, 'row', pairs)]
    mul x2 -> x5, other arithmetic: 6.83 us -> 0.61 us  [the longest x1 0.58 us: body(): jnp.sum(onehot * t[:, None], axis=0) * scale]
    select_n x1 -> x0, other arithmetic: 4.46 us -> none  [broadcast(): jnp.where(lax.axis_index(axis) == holder, block, jnp.zeros_like(block))]
  transfers between devices with their start and end apart: 2 -> 33, of which waited for: 2 -> 9; matrix products, arithmetic and copies ran while one was open for 0% -> 10% of each run, Pallas kernels for 0% -> 26%
where the time goes in v1:
time: 132 us; the launch traced here: 129 us
  starting transfers between devices  60.3 us (46%)
  Pallas kernels  38.1 us (29%)
  waiting for transfers between devices  12.4 us (9%)
  local copies, waits for them, and re-layouts  10.3 us (8%)
  other arithmetic  6.99 us (5%)
    ppermute x20, starting transfers between devices, row_permute(): return lax.ppermute(v, 'row', pairs)  37.5 us
    pallas_call x3, Pallas kernels, batch(): pl.pallas_call(lambda *refs: batch_kernel(n, counts, *refs), out_shape=[j...  23.1 us
    ppermute x9, starting transfers between devices, col_permute(): return lax.ppermute(v, 'col', pairs)  12.6 us
    ppermute x20, waiting for transfers between devices, row_permute(): return lax.ppermute(v, 'row', pairs)  11 us
    ppermute x4, starting transfers between devices, all_permute(): return lax.ppermute(v, ('row', 'col'), pairs)  10.2 us
    pallas_call x4, Pallas kernels, prep(): pl.pallas_call(prep_kernel, out_shape=jax.ShapeDtypeStruct((2, 128, KQ),...  10.1 us
    pallas_call x1, Pallas kernels, final(): pl.pallas_call(lambda *refs: final_kernel(nb, *refs), out_shape=[shape, s...  4.89 us
    convert_element_type x3, other arithmetic, selection(): return (target == jnp.arange(1024)[None, :]).astype(BF)  3.88 us
  transfers between devices with their start and end apart: 33, of which 9 were waited for; matrix products, arithmetic and copies ran while one was open for 10% of the time, Pallas kernels for 26%

profile of v1, /device:TPU:8, one launch (start us, length us, event | category | flops | bytes accessed | tf_op | source)
XLA Modules:
  0.0 129.3 jit_solution(2730763453207464481)
XLA Ops:
  2.4 2.3 %collective-permute-start.2 = (bf16[6,16,512]{2,1,0:T(8,128)(2,1)S(1)}, bf16[6,16,512]{2,1,0:T(8,128)(2,1)S(1)}, u32[]{:S(2)}, u32[]{:S(2)}) collective-permute-start(bf16[6,16,512]{2,1,0:T(8,128)(2,1)S(1)} %get-tuple-element.32), channel_id=1, source_target_pairs={{0,192},{8,200},{16,208},{24,216},{32,224},{40,232},{48,240},{56,2... | collective-permute-start | bytes 294920 | tf_op jit(solution)/shard_map/ppermute | solution.py:24
  5.5 1.9 %collective-permute-start = (bf16[6,16,512]{2,1,0:T(8,128)(2,1)S(1)}, bf16[6,16,512]{2,1,0:T(8,128)(2,1)S(1)}, u32[]{:S(2)}, u32[]{:S(2)}) collective-permute-start(bf16[6,16,512]{2,1,0:T(8,128)(2,1)S(1)} %get-tuple-element.34), channel_id=1, source_target_pairs={{0,64},{8,72},{16,80},{24,88},{32,96},{40,104},{48,112},{56,120},{... | collective-permute-start | bytes 294920 | tf_op jit(solution)/shard_map/ppermute | solution.py:24
  7.4 2.6 %collective-permute-start.8 = (bf16[6,16,512]{2,1,0:T(8,128)(2,1)S(1)}, bf16[6,16,512]{2,1,0:T(8,128)(2,1)S(1)}, u32[]{:S(2)}, u32[]{:S(2)}) collective-permute-start(bf16[6,16,512]{2,1,0:T(8,128)(2,1)S(1)} %get-tuple-element.29), channel_id=1, source_target_pairs={{0,192},{1,224},{2,194},{3,226},{4,196},{5,228},{6,198},{7,230},{8... | collective-permute-start | bytes 294920 | tf_op jit(solution)/shard_map/ppermute | solution.py:44
  10.0 1.7 %collective-permute-start.7 = (bf16[6,16,512]{2,1,0:T(8,128)(2,1)S(1)}, bf16[6,16,512]{2,1,0:T(8,128)(2,1)S(1)}, u32[]{:S(2)}, u32[]{:S(2)}) collective-permute-start(bf16[6,16,512]{2,1,0:T(8,128)(2,1)S(1)} %get-tuple-element.30), channel_id=1, source_target_pairs={{0,128},{1,160},{2,130},{3,162},{4,132},{5,164},{6,134},{7,166},{8... | collective-permute-start | bytes 294920 | tf_op jit(solution)/shard_map/ppermute | solution.py:44
  13.1 2.5 %collective-permute-start.6 = (bf16[6,16,512]{2,1,0:T(8,128)(2,1)S(1)}, bf16[6,16,512]{2,1,0:T(8,128)(2,1)S(1)}, u32[]{:S(2)}, u32[]{:S(2)}) collective-permute-start(bf16[6,16,512]{2,1,0:T(8,128)(2,1)S(1)} %get-tuple-element.31), channel_id=1, source_target_pairs={{0,64},{1,96},{2,66},{3,98},{4,68},{5,100},{6,70},{7,102},{8,128},... | collective-permute-start | bytes 294920 | tf_op jit(solution)/shard_map/ppermute | solution.py:44
  15.6 3.3 %collective-permute-start.5 = (bf16[6,16,512]{2,1,0:T(8,128)(2,1)S(1)}, bf16[6,16,512]{2,1,0:T(8,128)(2,1)S(1)}, u32[]{:S(2)}, u32[]{:S(2)}) collective-permute-start(bf16[6,16,512]{2,1,0:T(8,128)(2,1)S(1)} %get-tuple-element.28), channel_id=1, source_target_pairs={{0,0},{1,32},{2,2},{3,34},{4,4},{5,36},{6,6},{7,38},{8,64},{9,96},... | collective-permute-start | bytes 294920 | tf_op jit(solution)/shard_map/ppermute | solution.py:44
  19.2 8.1 %collective-permute-start.4 = (bf16[4,6,16,512]{3,2,1,0:T(8,128)(2,1)S(1)}, bf16[4,6,16,512]{3,2,1,0:T(8,128)(2,1)}, u32[]{:S(2)}, u32[]{:S(2)}) collective-permute-start(bf16[4,6,16,512]{3,2,1,0:T(8,128)(2,1)S(1)} %pad_maximum_fusion.refs_1_), channel_id=1, source_target_pairs={{0,56},{8,0},{16,8},{24,16},{32,24},{40,32},{48,40},{56,48},{64,12... | collective-permute-start | bytes 1179656 | tf_op jit(solution)/shard_map/ppermute | solution.py:24
  29.0 5.0 %collective-permute-start.9 = (bf16[4,6,16,512]{3,2,1,0:T(8,128)(2,1)S(1)}, bf16[4,6,16,512]{3,2,1,0:T(8,128)(2,1)S(1)}, u32[]{:S(2)}, u32[]{:S(2)}) collective-permute-start(bf16[4,6,16,512]{3,2,1,0:T(8,128)(2,1)S(1)} %pad_maximum_fusion.1.refs_0_), channel_id=1, source_target_pairs={{0,1},{1,0},{2,3},{3,2},{4,5},{5,4},{6,7},{7,6},{8,9},{9,8},{10,11... | collective-permute-start | bytes 1179656 | tf_op jit(solution)/shard_map/ppermute | solution.py:33
  34.0 1.7 %collective-permute-start.10 = (bf16[4,6,16,512]{3,2,1,0:T(8,128)(2,1)S(1)}, bf16[4,6,16,512]{3,2,1,0:T(8,128)(2,1)S(1)}, u32[]{:S(2)}, u32[]{:S(2)}) collective-permute-start(bf16[4,6,16,512]{3,2,1,0:T(8,128)(2,1)S(1)} %pad_maximum_fusion.1.refs_0_), channel_id=1, source_target_pairs={{0,6},{1,7},{2,0},{3,1},{4,2},{5,3},{6,4},{7,5},{8,14},{9,15},{10,... | collective-permute-start | bytes 1179656 | tf_op jit(solution)/shard_map/ppermute | solution.py:33
  35.7 3.0 %collective-permute-done.3.refs_2_ = bf16[4,6,16,512]{3,2,1,0:T(8,128)(2,1)} collective-permute-done((bf16[4,6,16,512]{3,2,1,0:T(8,128)(2,1)S(1)}, bf16[4,6,16,512]{3,2,1,0:T(8,128)(2,1)}, u32[]{:S(2)}, u32[]{:S(2)}) %collective-permute-start.3) | collective-permute-done | bytes 393248 | tf_op jit(solution)/shard_map/ppermute | solution.py:24
  38.7 3.2 %collective-permute-start.22 = (bf16[4,6,16,512]{3,2,1,0:T(8,128)(2,1)}, bf16[4,6,16,512]{3,2,1,0:T(8,128)(2,1)S(1)}, u32[]{:S(2)}, u32[]{:S(2)}) collective-permute-start(bf16[4,6,16,512]{3,2,1,0:T(8,128)(2,1)} %collective-permute-done.4.refs_3_), channel_id=1, source_target_pairs={{0,56},{8,0},{16,8},{24,16},{32,24},{40,32},{48,40},{56,48},{64,12... | collective-permute-start | bytes 1179656 | tf_op jit(solution)/shard_map/ppermute | solution.py:24
  42.0 1.6 %collective-permute-start.13 = (bf16[2,6,16,512]{3,2,1,0:T(8,128)(2,1)S(1)}, bf16[2,6,16,512]{3,2,1,0:T(8,128)(2,1)}, u32[]{:S(2)}, u32[]{:S(2)}) collective-permute-start(bf16[2,6,16,512]{3,2,1,0:T(8,128)(2,1)S(1)} %slice.16), channel_id=1, source_target_pairs={{0,2},{1,3},{2,4},{3,5},{4,6},{5,7},{6,0},{7,1},{8,10},{9,11},{10,... | collective-permute-start | bytes 589832 | tf_op jit(solution)/shard_map/ppermute | solution.py:33
  45.9 3.0 %collective-permute-start.14 = (bf16[2,6,16,512]{3,2,1,0:T(8,128)(2,1)}, bf16[2,6,16,512]{3,2,1,0:T(8,128)(2,1)}, u32[]{:S(2)}, u32[]{:S(2)}) collective-permute-start(bf16[2,6,16,512]{3,2,1,0:T(8,128)(2,1)} %slice.17), channel_id=1, source_target_pairs={{0,6},{1,7},{2,0},{3,1},{4,2},{5,3},{6,4},{7,5},{8,14},{9,15},{10,... | collective-permute-start | bytes 589832 | tf_op jit(solution)/shard_map/ppermute | solution.py:33
  50.9 2.2 %collective-permute-start.27 = (bf16[4,6,16,512]{3,2,1,0:T(8,128)(2,1)S(1)}, bf16[4,6,16,512]{3,2,1,0:T(8,128)(2,1)}, u32[]{:S(2)}, u32[]{:S(2)}) collective-permute-start(bf16[4,6,16,512]{3,2,1,0:T(8,128)(2,1)S(1)} %collective-permute-done.22.refs_2_), channel_id=1, source_target_pairs={{0,56},{8,0},{16,8},{24,16},{32,24},{40,32},{48,40},{56,48},{64,12... | collective-permute-start | bytes 1179656 | tf_op jit(solution)/shard_map/ppermute | solution.py:24
  58.1 1.8 %fusion.1.refs_14_ = bf16[384,1024]{1,0:T(8,128)(2,1)} fusion(s32[384]{0:T(512)} %add.352), kind=kLoop, calls=%fused_computation.3 | loop fusion | flops 786432 | bytes 787968 | tf_op jit(solution)/shard_map/convert_element_type | solution.py:176
  59.9 2.5 %weigh.4.refs_4_.refs_3_.refs_5_ = bf16[2,128,3072]{2,1,0:T(8,128)(2,1)} custom-call(s32[6]{0:T(128)} %stack.60.pos_ref.refs_0_, f32[2,512]{1,0:T(2,128)} %pad_maximum_fusion.2.w_ref, bf16[4,6,16,512]{3,2,1,0:T(8,128)(2,1)} %copy-done, bf16[4,6,16,512]{3,2,1,0:T(8,128)(2,1)} %copy-done.6), custom_call_target="tpu_custom_call" | custom-call | tf_op jit(solution)/shard_map/weigh/pallas_call | solution.py:70
  62.5 2.5 %weigh.5.refs_5_.refs_4_.refs_6_ = bf16[2,128,3072]{2,1,0:T(8,128)(2,1)} custom-call(s32[6]{0:T(128)} %stack.60.pos_ref.refs_0_, f32[2,512]{1,0:T(2,128)} %pad_maximum_fusion.2.w_ref, bf16[4,6,16,512]{3,2,1,0:T(8,128)(2,1)} %copy-done.2, bf16[4,6,16,512]{3,2,1,0:T(8,128)(2,1)} %copy-done.7), custom_call_target="tpu_custom_call" | custom-call | tf_op jit(solution)/shard_map/weigh/pallas_call | solution.py:70
  65.7 2.5 %weigh.7.refs_7_.refs_6_.refs_8_ = bf16[2,128,3072]{2,1,0:T(8,128)(2,1)} custom-call(s32[6]{0:T(128)} %stack.60.pos_ref.refs_0_, f32[2,512]{1,0:T(2,128)} %pad_maximum_fusion.2.w_ref, bf16[4,6,16,512]{3,2,1,0:T(8,128)(2,1)} %copy-done.1, bf16[4,6,16,512]{3,2,1,0:T(8,128)(2,1)} %copy-done.8), custom_call_target="tpu_custom_call" | custom-call | tf_op jit(solution)/shard_map/weigh/pallas_call | solution.py:70
  69.5 2.6 %weigh.6.refs_6_.refs_5_.refs_7_ = bf16[2,128,3072]{2,1,0:T(8,128)(2,1)} custom-call(s32[6]{0:T(128)} %stack.60.pos_ref.refs_0_, f32[2,512]{1,0:T(2,128)} %pad_maximum_fusion.2.w_ref, bf16[2,6,16,512]{3,2,1,0:T(8,128)(2,1)} %collective-permute-done.13.refs_0_, bf16[2,6,16,512]{3,2,1,0:T(8,128)(2,1)} %collective-permute-done.14.refs_1_, ...), custom_call_target="tpu_custom_call" | custom-call | tf_op jit(solution)/shard_map/weigh/pallas_call | solution.py:70
  74.2 3.3 %collective-permute-start.29 = (bf16[2,6,16,512]{3,2,1,0:T(8,128)(2,1)S(1)}, bf16[2,6,16,512]{3,2,1,0:T(8,128)(2,1)S(1)}, u32[]{:S(2)}, u32[]{:S(2)}) collective-permute-start(bf16[2,6,16,512]{3,2,1,0:T(8,128)(2,1)S(1)} %slice.19), channel_id=1, source_target_pairs={{0,56},{8,0},{16,8},{24,16},{32,24},{40,32},{48,40},{56,48},{64,12... | collective-permute-start | bytes 589832 | tf_op jit(solution)/shard_map/ppermute | solution.py:24
  77.4 7.7 %partial_gram.3 = (f32[256,384]{1,0:T(8,128)}, bf16[256,384]{1,0:T(8,128)(2,1)}, bf16[256,384]{1,0:T(8,128)(2,1)}, bf16[256,384]{1,0:T(8,128)(2,1)}) custom-call(s32[6]{0:T(128)} %stack.60.pos_ref.refs_0_, bf16[4,6,16,512]{3,2,1,0:T(8,128)(2,1)} %copy-done.5, bf16[4,6,16,512]{3,2,1,0:T(8,128)(2,1)} %collective-permute-done.3.refs_2_, ...), custom_call_target="tpu_custom_call" | custom-call | flops 2415919104 | bytes 8388608 | tf_op jit(solution)/shard_map/partial_gram/pallas_call | solution.py:122
  85.2 2.7 %collective-permute-start.18 = (bf16[256,384]{1,0:T(8,128)(2,1)}, bf16[256,384]{1,0:T(8,128)(2,1)S(1)}, u32[]{:S(2)}, u32[]{:S(2)}) collective-permute-start(bf16[256,384]{1,0:T(8,128)(2,1)} %get-tuple-element.15), channel_id=1, source_target_pairs={{0,64},{8,72},{16,80},{24,88},{32,96},{40,104},{48,112},{56,120},{... | collective-permute-start | bytes 589832 | tf_op jit(solution)/shard_map/ppermute | solution.py:24
  87.8 3.5 %collective-permute-start.19 = (bf16[256,384]{1,0:T(8,128)(2,1)}, bf16[256,384]{1,0:T(8,128)(2,1)S(1)}, u32[]{:S(2)}, u32[]{:S(2)}) collective-permute-start(bf16[256,384]{1,0:T(8,128)(2,1)} %get-tuple-element.16), channel_id=1, source_target_pairs={{0,128},{8,136},{16,144},{24,152},{32,160},{40,168},{48,176},{56,1... | collective-permute-start | bytes 589832 | tf_op jit(solution)/shard_map/ppermute | solution.py:24
  91.3 7.6 %partial_gram.4 = (f32[256,256]{1,0:T(8,128)}, bf16[256,256]{1,0:T(8,128)(2,1)}, bf16[256,256]{1,0:T(8,128)(2,1)}, bf16[256,256]{1,0:T(8,128)(2,1)}) custom-call(s32[6]{0:T(128)} %stack.60.pos_ref.refs_0_, bf16[4,6,16,512]{3,2,1,0:T(8,128)(2,1)} %copy-done.3, bf16[4,6,16,512]{3,2,1,0:T(8,128)(2,1)} %copy-done.4, ...), custom_call_target="tpu_custom_call" | custom-call | flops 1610612736 | bytes 8388608 | tf_op jit(solution)/shard_map/partial_gram/pallas_call | solution.py:122
  99.1 2.0 %collective-permute-start.24 = (bf16[256,256]{1,0:T(8,128)(2,1)}, bf16[256,256]{1,0:T(8,128)(2,1)S(1)}, u32[]{:S(2)}, u32[]{:S(2)}) collective-permute-start(bf16[256,256]{1,0:T(8,128)(2,1)} %get-tuple-element.20), channel_id=1, source_target_pairs={{0,128},{8,136},{16,144},{24,152},{32,160},{40,168},{48,176},{56,1... | collective-permute-start | bytes 393224 | tf_op jit(solution)/shard_map/ppermute | solution.py:24
  101.8 7.7 %partial_gram.5 = (f32[256,384]{1,0:T(8,128)}, bf16[256,384]{1,0:T(8,128)(2,1)}, bf16[256,384]{1,0:T(8,128)(2,1)}, bf16[256,384]{1,0:T(8,128)(2,1)}) custom-call(s32[6]{0:T(128)} %stack.60.pos_ref.refs_0_, bf16[4,6,16,512]{3,2,1,0:T(8,128)(2,1)} %collective-permute-done.26.refs_1_, bf16[4,6,16,512]{3,2,1,0:T(8,128)(2,1)} %collective-permute-done.27.refs_2_, ...), custom_call_target="tpu_custom_call" | custom-call | flops 2415919104 | bytes 8388608 | tf_op jit(solution)/shard_map/partial_gram/pallas_call | solution.py:122
  109.6 2.2 %collective-permute-start.20 = (bf16[256,384]{1,0:T(8,128)(2,1)S(1)}, bf16[256,384]{1,0:T(8,128)(2,1)S(1)}, u32[]{:S(2)}, u32[]{:S(2)}) collective-permute-start(bf16[256,384]{1,0:T(8,128)(2,1)S(1)} %copy-done.25), channel_id=1, source_target_pairs={{0,192},{8,200},{16,208},{24,216},{32,224},{40,232},{48,240},{56,2... | collective-permute-start | bytes 589832 | tf_op jit(solution)/shard_map/ppermute | solution.py:24
  111.8 3.4 %collective-permute-start.31 = (bf16[256,384]{1,0:T(8,128)(2,1)}, bf16[256,384]{1,0:T(8,128)(2,1)S(1)}, u32[]{:S(2)}, u32[]{:S(2)}) collective-permute-start(bf16[256,384]{1,0:T(8,128)(2,1)} %get-tuple-element.24), channel_id=1, source_target_pairs={{0,128},{8,136},{16,144},{24,152},{32,160},{40,168},{48,176},{56,1... | collective-permute-start | bytes 589832 | tf_op jit(solution)/shard_map/ppermute | solution.py:24
  117.2 1.8 %collective-permute-done.30.refs_9_ = bf16[256,384]{1,0:T(8,128)(2,1)S(1)} collective-permute-done((bf16[256,384]{1,0:T(8,128)(2,1)}, bf16[256,384]{1,0:T(8,128)(2,1)S(1)}, u32[]{:S(2)}, u32[]{:S(2)}) %collective-permute-start.30) | collective-permute-done | bytes 196640 | tf_op jit(solution)/shard_map/ppermute | solution.py:24
  119.1 3.1 %collective-permute-done.31.refs_10_ = bf16[256,384]{1,0:T(8,128)(2,1)S(1)} collective-permute-done((bf16[256,384]{1,0:T(8,128)(2,1)}, bf16[256,384]{1,0:T(8,128)(2,1)S(1)}, u32[]{:S(2)}, u32[]{:S(2)}) %collective-permute-start.31) | collective-permute-done | bytes 196640 | tf_op jit(solution)/shard_map/ppermute | solution.py:24
  122.2 1.6 %collective-permute-done.32.refs_11_ = bf16[256,384]{1,0:T(8,128)(2,1)S(1)} collective-permute-done((bf16[256,384]{1,0:T(8,128)(2,1)}, bf16[256,384]{1,0:T(8,128)(2,1)S(1)}, u32[]{:S(2)}, u32[]{:S(2)}) %collective-permute-start.32) | collective-permute-done | bytes 196640 | tf_op jit(solution)/shard_map/ppermute | solution.py:24
  124.4 4.9 %collect.1 = (f32[2,128,512]{2,1,0:T(8,128)}, f32[2,128,512]{2,1,0:T(8,128)}) custom-call(f32[256,384]{1,0:T(8,128)} %get-tuple-element.14.refs_0_, bf16[256,384]{1,0:T(8,128)(2,1)} %copy-done.9, bf16[256,384]{1,0:T(8,128)(2,1)} %copy-done.10, bf16[256,384]{1,0:T(8,128)(2,1)} %copy-done.11, f32[256,256]{1,0:T(8,128)} %get-tuple-element.18.refs_4_, ...), custom_call_target="tpu_custom_call" | custom-call | tf_op jit(solution)/shard_map/collect/pallas_call | solution.py:159
  (130 shorter events, 22.6 us)
Async XLA Ops:
  2.4 10.8 %collective-permute-start.2 = (bf16[6,16,512]{2,1,0:T(8,128)(2,1)S(1)}, bf16[6,16,512]{2,1,0:T(8,128)(2,1)S(1)}, u32[]{:S(2)}, u32[]{:S(2)}) collective-permute-start(bf16[6,16,512]{2,1,0:T(8,128)(2,1)S(1)} %get-tuple-element.32), channel_id=1, source_target_pairs={{0,192},{8,200},{16,208},{24,216},{32,224},{40,232},{48,240},{56,2... | collective-permute-start | bytes 294920 | tf_op jit(solution)/shard_map/ppermute | solution.py:24
  4.6 11.0 %collective-permute-start.1 = (bf16[6,16,512]{2,1,0:T(8,128)(2,1)S(1)}, bf16[6,16,512]{2,1,0:T(8,128)(2,1)S(1)}, u32[]{:S(2)}, u32[]{:S(2)}) collective-permute-start(bf16[6,16,512]{2,1,0:T(8,128)(2,1)S(1)} %get-tuple-element.33), channel_id=1, source_target_pairs={{0,128},{8,136},{16,144},{24,152},{32,160},{40,168},{48,176},{56,1... | collective-permute-start | bytes 294920 | tf_op jit(solution)/shard_map/ppermute | solution.py:24
  5.5 13.5 %collective-permute-start = (bf16[6,16,512]{2,1,0:T(8,128)(2,1)S(1)}, bf16[6,16,512]{2,1,0:T(8,128)(2,1)S(1)}, u32[]{:S(2)}, u32[]{:S(2)}) collective-permute-start(bf16[6,16,512]{2,1,0:T(8,128)(2,1)S(1)} %get-tuple-element.34), channel_id=1, source_target_pairs={{0,64},{8,72},{16,80},{24,88},{32,96},{40,104},{48,112},{56,120},{... | collective-permute-start | bytes 294920 | tf_op jit(solution)/shard_map/ppermute | solution.py:24
  7.4 11.8 %collective-permute-start.8 = (bf16[6,16,512]{2,1,0:T(8,128)(2,1)S(1)}, bf16[6,16,512]{2,1,0:T(8,128)(2,1)S(1)}, u32[]{:S(2)}, u32[]{:S(2)}) collective-permute-start(bf16[6,16,512]{2,1,0:T(8,128)(2,1)S(1)} %get-tuple-element.29), channel_id=1, source_target_pairs={{0,192},{1,224},{2,194},{3,226},{4,196},{5,228},{6,198},{7,230},{8... | collective-permute-start | bytes 294920 | tf_op jit(solution)/shard_map/ppermute | solution.py:44
  10.0 17.4 %collective-permute-start.7 = (bf16[6,16,512]{2,1,0:T(8,128)(2,1)S(1)}, bf16[6,16,512]{2,1,0:T(8,128)(2,1)S(1)}, u32[]{:S(2)}, u32[]{:S(2)}) collective-permute-start(bf16[6,16,512]{2,1,0:T(8,128)(2,1)S(1)} %get-tuple-element.30), channel_id=1, source_target_pairs={{0,128},{1,160},{2,130},{3,162},{4,132},{5,164},{6,134},{7,166},{8... | collective-permute-start | bytes 294920 | tf_op jit(solution)/shard_map/ppermute | solution.py:44
  13.1 14.9 %collective-permute-start.6 = (bf16[6,16,512]{2,1,0:T(8,128)(2,1)S(1)}, bf16[6,16,512]{2,1,0:T(8,128)(2,1)S(1)}, u32[]{:S(2)}, u32[]{:S(2)}) collective-permute-start(bf16[6,16,512]{2,1,0:T(8,128)(2,1)S(1)} %get-tuple-element.31), channel_id=1, source_target_pairs={{0,64},{1,96},{2,66},{3,98},{4,68},{5,100},{6,70},{7,102},{8,128},... | collective-permute-start | bytes 294920 | tf_op jit(solution)/shard_map/ppermute | solution.py:44
  15.6 12.4 %collective-permute-start.5 = (bf16[6,16,512]{2,1,0:T(8,128)(2,1)S(1)}, bf16[6,16,512]{2,1,0:T(8,128)(2,1)S(1)}, u32[]{:S(2)}, u32[]{:S(2)}) collective-permute-start(bf16[6,16,512]{2,1,0:T(8,128)(2,1)S(1)} %get-tuple-element.28), channel_id=1, source_target_pairs={{0,0},{1,32},{2,2},{3,34},{4,4},{5,36},{6,6},{7,38},{8,64},{9,96},... | collective-permute-start | bytes 294920 | tf_op jit(solution)/shard_map/ppermute | solution.py:44
  19.1 19.6 %collective-permute-start.3 = (bf16[4,6,16,512]{3,2,1,0:T(8,128)(2,1)S(1)}, bf16[4,6,16,512]{3,2,1,0:T(8,128)(2,1)}, u32[]{:S(2)}, u32[]{:S(2)}) collective-permute-start(bf16[4,6,16,512]{3,2,1,0:T(8,128)(2,1)S(1)} %pad_maximum_fusion.refs_1_), channel_id=1, source_target_pairs={{0,8},{8,16},{16,24},{24,32},{32,40},{40,48},{48,56},{56,0},{64,72... | collective-permute-start | bytes 1179656 | tf_op jit(solution)/shard_map/ppermute | solution.py:24
  19.2 19.5 %collective-permute-start.4 = (bf16[4,6,16,512]{3,2,1,0:T(8,128)(2,1)S(1)}, bf16[4,6,16,512]{3,2,1,0:T(8,128)(2,1)}, u32[]{:S(2)}, u32[]{:S(2)}) collective-permute-start(bf16[4,6,16,512]{3,2,1,0:T(8,128)(2,1)S(1)} %pad_maximum_fusion.refs_1_), channel_id=1, source_target_pairs={{0,56},{8,0},{16,8},{24,16},{32,24},{40,32},{48,40},{56,48},{64,12... | collective-permute-start | bytes 1179656 | tf_op jit(solution)/shard_map/ppermute | solution.py:24
  28.1 13.9 %collective-permute-start.12 = (bf16[4,6,16,512]{3,2,1,0:T(8,128)(2,1)S(1)}, bf16[4,6,16,512]{3,2,1,0:T(8,128)(2,1)S(1)}, u32[]{:S(2)}, u32[]{:S(2)}) collective-permute-start(bf16[4,6,16,512]{3,2,1,0:T(8,128)(2,1)S(1)} %pad_maximum_fusion.1.refs_0_), channel_id=1, source_target_pairs={{0,2},{1,3},{2,4},{3,5},{4,6},{5,7},{6,0},{7,1},{8,10},{9,11},{10,... | collective-permute-start | bytes 1179656 | tf_op jit(solution)/shard_map/ppermute | solution.py:33
  29.0 16.9 %collective-permute-start.9 = (bf16[4,6,16,512]{3,2,1,0:T(8,128)(2,1)S(1)}, bf16[4,6,16,512]{3,2,1,0:T(8,128)(2,1)S(1)}, u32[]{:S(2)}, u32[]{:S(2)}) collective-permute-start(bf16[4,6,16,512]{3,2,1,0:T(8,128)(2,1)S(1)} %pad_maximum_fusion.1.refs_0_), channel_id=1, source_target_pairs={{0,1},{1,0},{2,3},{3,2},{4,5},{5,4},{6,7},{7,6},{8,9},{9,8},{10,11... | collective-permute-start | bytes 1179656 | tf_op jit(solution)/shard_map/ppermute | solution.py:33
  34.0 11.1 %collective-permute-start.10 = (bf16[4,6,16,512]{3,2,1,0:T(8,128)(2,1)S(1)}, bf16[4,6,16,512]{3,2,1,0:T(8,128)(2,1)S(1)}, u32[]{:S(2)}, u32[]{:S(2)}) collective-permute-start(bf16[4,6,16,512]{3,2,1,0:T(8,128)(2,1)S(1)} %pad_maximum_fusion.1.refs_0_), channel_id=1, source_target_pairs={{0,6},{1,7},{2,0},{3,1},{4,2},{5,3},{6,4},{7,5},{8,14},{9,15},{10,... | collective-permute-start | bytes 1179656 | tf_op jit(solution)/shard_map/ppermute | solution.py:33
  38.7 11.1 %collective-permute-start.21 = (bf16[4,6,16,512]{3,2,1,0:T(8,128)(2,1)}, bf16[4,6,16,512]{3,2,1,0:T(8,128)(2,1)S(1)}, u32[]{:S(2)}, u32[]{:S(2)}) collective-permute-start(bf16[4,6,16,512]{3,2,1,0:T(8,128)(2,1)} %collective-permute-done.3.refs_2_), channel_id=1, source_target_pairs={{0,8},{8,16},{16,24},{24,32},{32,40},{40,48},{48,56},{56,0},{64,72... | collective-permute-start | bytes 1179656 | tf_op jit(solution)/shard_map/ppermute | solution.py:24
  38.7 12.2 %collective-permute-start.22 = (bf16[4,6,16,512]{3,2,1,0:T(8,128)(2,1)}, bf16[4,6,16,512]{3,2,1,0:T(8,128)(2,1)S(1)}, u32[]{:S(2)}, u32[]{:S(2)}) collective-permute-start(bf16[4,6,16,512]{3,2,1,0:T(8,128)(2,1)} %collective-permute-done.4.refs_3_), channel_id=1, source_target_pairs={{0,56},{8,0},{16,8},{24,16},{32,24},{40,32},{48,40},{56,48},{64,12... | collective-permute-start | bytes 1179656 | tf_op jit(solution)/shard_map/ppermute | solution.py:24
  42.0 7.4 %collective-permute-start.13 = (bf16[2,6,16,512]{3,2,1,0:T(8,128)(2,1)S(1)}, bf16[2,6,16,512]{3,2,1,0:T(8,128)(2,1)}, u32[]{:S(2)}, u32[]{:S(2)}) collective-permute-start(bf16[2,6,16,512]{3,2,1,0:T(8,128)(2,1)S(1)} %slice.16), channel_id=1, source_target_pairs={{0,2},{1,3},{2,4},{3,5},{4,6},{5,7},{6,0},{7,1},{8,10},{9,11},{10,... | collective-permute-start | bytes 589832 | tf_op jit(solution)/shard_map/ppermute | solution.py:33
  45.1 12.5 %collective-permute-start.11 = (bf16[4,6,16,512]{3,2,1,0:T(8,128)(2,1)S(1)}, bf16[4,6,16,512]{3,2,1,0:T(8,128)(2,1)S(1)}, u32[]{:S(2)}, u32[]{:S(2)}) collective-permute-start(bf16[4,6,16,512]{3,2,1,0:T(8,128)(2,1)S(1)} %collective-permute-done.10.refs_0_), channel_id=1, source_target_pairs={{0,1},{1,0},{2,3},{3,2},{4,5},{5,4},{6,7},{7,6},{8,9},{9,8},{10,11... | collective-permute-start | bytes 1179656 | tf_op jit(solution)/shard_map/ppermute | solution.py:33
  45.9 11.6 %collective-permute-start.14 = (bf16[2,6,16,512]{3,2,1,0:T(8,128)(2,1)}, bf16[2,6,16,512]{3,2,1,0:T(8,128)(2,1)}, u32[]{:S(2)}, u32[]{:S(2)}) collective-permute-start(bf16[2,6,16,512]{3,2,1,0:T(8,128)(2,1)} %slice.17), channel_id=1, source_target_pairs={{0,6},{1,7},{2,0},{3,1},{4,2},{5,3},{6,4},{7,5},{8,14},{9,15},{10,... | collective-permute-start | bytes 589832 | tf_op jit(solution)/shard_map/ppermute | solution.py:33
  49.4 15.5 %collective-permute-start.17 = (bf16[4,6,16,512]{3,2,1,0:T(8,128)(2,1)S(1)}, bf16[4,6,16,512]{3,2,1,0:T(8,128)(2,1)S(1)}, u32[]{:S(2)}, u32[]{:S(2)}) collective-permute-start(bf16[4,6,16,512]{3,2,1,0:T(8,128)(2,1)S(1)} %collective-permute-done.12.refs_0_), channel_id=1, source_target_pairs={{0,1},{1,0},{2,3},{3,2},{4,5},{5,4},{6,7},{7,6},{8,9},{9,8},{10,11... | collective-permute-start | bytes 1179656 | tf_op jit(solution)/shard_map/ppermute | solution.py:33
  49.8 22.3 %collective-permute-start.26 = (bf16[4,6,16,512]{3,2,1,0:T(8,128)(2,1)S(1)}, bf16[4,6,16,512]{3,2,1,0:T(8,128)(2,1)}, u32[]{:S(2)}, u32[]{:S(2)}) collective-permute-start(bf16[4,6,16,512]{3,2,1,0:T(8,128)(2,1)S(1)} %collective-permute-done.21.refs_1_), channel_id=1, source_target_pairs={{0,8},{8,16},{16,24},{24,32},{32,40},{40,48},{48,56},{56,0},{64,72... | collective-permute-start | bytes 1179656 | tf_op jit(solution)/shard_map/ppermute | solution.py:24
  50.9 22.3 %collective-permute-start.27 = (bf16[4,6,16,512]{3,2,1,0:T(8,128)(2,1)S(1)}, bf16[4,6,16,512]{3,2,1,0:T(8,128)(2,1)}, u32[]{:S(2)}, u32[]{:S(2)}) collective-permute-start(bf16[4,6,16,512]{3,2,1,0:T(8,128)(2,1)S(1)} %collective-permute-done.22.refs_2_), channel_id=1, source_target_pairs={{0,56},{8,0},{16,8},{24,16},{32,24},{40,32},{48,40},{56,48},{64,12... | collective-permute-start | bytes 1179656 | tf_op jit(solution)/shard_map/ppermute | solution.py:24
  57.5 10.6 %collective-permute-start.15 = (bf16[2,6,16,512]{3,2,1,0:T(8,128)(2,1)}, bf16[2,6,16,512]{3,2,1,0:T(8,128)(2,1)S(1)}, u32[]{:S(2)}, u32[]{:S(2)}) collective-permute-start(bf16[2,6,16,512]{3,2,1,0:T(8,128)(2,1)} %collective-permute-done.13.refs_0_), channel_id=1, source_target_pairs={{0,1},{1,0},{2,3},{3,2},{4,5},{5,4},{6,7},{7,6},{8,9},{9,8},{10,11... | collective-permute-start | bytes 589832 | tf_op jit(solution)/shard_map/ppermute | solution.py:33
  57.6 10.6 %collective-permute-start.16 = (bf16[2,6,16,512]{3,2,1,0:T(8,128)(2,1)}, bf16[2,6,16,512]{3,2,1,0:T(8,128)(2,1)S(1)}, u32[]{:S(2)}, u32[]{:S(2)}) collective-permute-start(bf16[2,6,16,512]{3,2,1,0:T(8,128)(2,1)} %collective-permute-done.14.refs_1_), channel_id=1, source_target_pairs={{0,1},{1,0},{2,3},{3,2},{4,5},{5,4},{6,7},{7,6},{8,9},{9,8},{10,11... | collective-permute-start | bytes 589832 | tf_op jit(solution)/shard_map/ppermute | solution.py:33
  73.1 25.9 %collective-permute-start.28 = (bf16[2,6,16,512]{3,2,1,0:T(8,128)(2,1)S(1)}, bf16[2,6,16,512]{3,2,1,0:T(8,128)(2,1)S(1)}, u32[]{:S(2)}, u32[]{:S(2)}) collective-permute-start(bf16[2,6,16,512]{3,2,1,0:T(8,128)(2,1)S(1)} %slice.18), channel_id=1, source_target_pairs={{0,8},{8,16},{16,24},{24,32},{32,40},{40,48},{48,56},{56,0},{64,72... | collective-permute-start | bytes 589832 | tf_op jit(solution)/shard_map/ppermute | solution.py:24
  74.2 26.9 %collective-permute-start.29 = (bf16[2,6,16,512]{3,2,1,0:T(8,128)(2,1)S(1)}, bf16[2,6,16,512]{3,2,1,0:T(8,128)(2,1)S(1)}, u32[]{:S(2)}, u32[]{:S(2)}) collective-permute-start(bf16[2,6,16,512]{3,2,1,0:T(8,128)(2,1)S(1)} %slice.19), channel_id=1, source_target_pairs={{0,56},{8,0},{16,8},{24,16},{32,24},{40,32},{48,40},{56,48},{64,12... | collective-permute-start | bytes 589832 | tf_op jit(solution)/shard_map/ppermute | solution.py:24
  85.2 30.0 %collective-permute-start.18 = (bf16[256,384]{1,0:T(8,128)(2,1)}, bf16[256,384]{1,0:T(8,128)(2,1)S(1)}, u32[]{:S(2)}, u32[]{:S(2)}) collective-permute-start(bf16[256,384]{1,0:T(8,128)(2,1)} %get-tuple-element.15), channel_id=1, source_target_pairs={{0,64},{8,72},{16,80},{24,88},{32,96},{40,104},{48,112},{56,120},{... | collective-permute-start | bytes 589832 | tf_op jit(solution)/shard_map/ppermute | solution.py:24
  87.8 28.3 %collective-permute-start.19 = (bf16[256,384]{1,0:T(8,128)(2,1)}, bf16[256,384]{1,0:T(8,128)(2,1)S(1)}, u32[]{:S(2)}, u32[]{:S(2)}) collective-permute-start(bf16[256,384]{1,0:T(8,128)(2,1)} %get-tuple-element.16), channel_id=1, source_target_pairs={{0,128},{8,136},{16,144},{24,152},{32,160},{40,168},{48,176},{56,1... | collective-permute-start | bytes 589832 | tf_op jit(solution)/shard_map/ppermute | solution.py:24
  98.9 10.6 %collective-permute-start.23 = (bf16[256,256]{1,0:T(8,128)(2,1)}, bf16[256,256]{1,0:T(8,128)(2,1)S(1)}, u32[]{:S(2)}, u32[]{:S(2)}) collective-permute-start(bf16[256,256]{1,0:T(8,128)(2,1)} %get-tuple-element.19), channel_id=1, source_target_pairs={{0,64},{8,72},{16,80},{24,88},{32,96},{40,104},{48,112},{56,120},{... | collective-permute-start | bytes 393224 | tf_op jit(solution)/shard_map/ppermute | solution.py:24
  99.1 12.7 %collective-permute-start.24 = (bf16[256,256]{1,0:T(8,128)(2,1)}, bf16[256,256]{1,0:T(8,128)(2,1)S(1)}, u32[]{:S(2)}, u32[]{:S(2)}) collective-permute-start(bf16[256,256]{1,0:T(8,128)(2,1)} %get-tuple-element.20), channel_id=1, source_target_pairs={{0,128},{8,136},{16,144},{24,152},{32,160},{40,168},{48,176},{56,1... | collective-permute-start | bytes 393224 | tf_op jit(solution)/shard_map/ppermute | solution.py:24
  101.1 10.7 %collective-permute-start.25 = (bf16[256,256]{1,0:T(8,128)(2,1)}, bf16[256,256]{1,0:T(8,128)(2,1)S(1)}, u32[]{:S(2)}, u32[]{:S(2)}) collective-permute-start(bf16[256,256]{1,0:T(8,128)(2,1)} %get-tuple-element.21), channel_id=1, source_target_pairs={{0,192},{8,200},{16,208},{24,216},{32,224},{40,232},{48,240},{56,2... | collective-permute-start | bytes 393224 | tf_op jit(solution)/shard_map/ppermute | solution.py:24
  109.6 7.6 %collective-permute-start.20 = (bf16[256,384]{1,0:T(8,128)(2,1)S(1)}, bf16[256,384]{1,0:T(8,128)(2,1)S(1)}, u32[]{:S(2)}, u32[]{:S(2)}) collective-permute-start(bf16[256,384]{1,0:T(8,128)(2,1)S(1)} %copy-done.25), channel_id=1, source_target_pairs={{0,192},{8,200},{16,208},{24,216},{32,224},{40,232},{48,240},{56,2... | collective-permute-start | bytes 589832 | tf_op jit(solution)/shard_map/ppermute | solution.py:24
  111.8 10.4 %collective-permute-start.31 = (bf16[256,384]{1,0:T(8,128)(2,1)}, bf16[256,384]{1,0:T(8,128)(2,1)S(1)}, u32[]{:S(2)}, u32[]{:S(2)}) collective-permute-start(bf16[256,384]{1,0:T(8,128)(2,1)} %get-tuple-element.24), channel_id=1, source_target_pairs={{0,128},{8,136},{16,144},{24,152},{32,160},{40,168},{48,176},{56,1... | collective-permute-start | bytes 589832 | tf_op jit(solution)/shard_map/ppermute | solution.py:24
  115.2 8.6 %collective-permute-start.32 = (bf16[256,384]{1,0:T(8,128)(2,1)}, bf16[256,384]{1,0:T(8,128)(2,1)S(1)}, u32[]{:S(2)}, u32[]{:S(2)}) collective-permute-start(bf16[256,384]{1,0:T(8,128)(2,1)} %get-tuple-element.25), channel_id=1, source_target_pairs={{0,192},{8,200},{16,208},{24,216},{32,224},{40,232},{48,240},{56,2... | collective-permute-start | bytes 589832 | tf_op jit(solution)/shard_map/ppermute | solution.py:24
  (30 other events, 393.3 us)

commit v2 on v1

v2 whole, which is shorter than its diff:
```python
import jax
import jax.numpy as jnp
import numpy as np
from jax import lax
from jax.experimental import pallas as pl
from jax.experimental.pallas import tpu as pltpu
from jax.sharding import PartitionSpec as P

NY, NZ, NX, NC = 4, 8, 4, 2
NQ = 512
KQ = 6 * NQ
BF = jnp.bfloat16
F32 = jnp.float32
VMEM_LIMIT = 24 * 1024 * 1024
SCALE = np.float32(1) / np.sqrt(np.float32(6 * 2048))
LHS_TYPE = pltpu.VMEM((2, 128, KQ), BF)

BATCHES = ((0, 7, 1, 6), (2, 5), (3, 4))


def row_permute(v, move):
    pairs = []
    for y in range(NY):
        for z in range(NZ):
            y2, z2 = move(y, z)
            pairs.append((y * NZ + z, y2 % NY * NZ + z2 % NZ))
    return lax.ppermute(v, "row", pairs)


def col_permute(v, move):
    pairs = []
    for x in range(NX):
        for c in range(NC):
            x2, c2 = move(x, c)
            pairs.append((x * NC + c, x2 % NX * NC + c2 % NC))
    return lax.ppermute(v, "col", pairs)


def all_permute(v, move):
    pairs = []
    for y in range(NY):
        for z in range(NZ):
            for x in range(NX):
                for c in range(NC):
                    y2, z2, x2, c2 = move(y, z, x, c)
                    pairs.append((((y * NZ + z) * NX + x) * NC + c, ((y2 * NZ + z2) * NX + x2) * NC + c2))
    return lax.ppermute(v, ("row", "col"), pairs)


def pick(stack, i):
    return lax.dynamic_index_in_dim(stack, i, 0, keepdims=False)


def place():
    row, col = lax.axis_index("row"), lax.axis_index("col")
    return row // NZ, row % NZ, col // NC, col % NC


SMEM_SPEC = pl.BlockSpec(memory_space=pltpu.SMEM)
VMEM_SPEC = pl.BlockSpec(memory_space=pltpu.VMEM)


def weigh_kernel(count, tab0_ref, tab1_ref, labels_ref, *refs):
    ins, out_ref = refs[:-1], refs[-1]
    y, _, _, c = place()
    labels = labels_ref[0:1, pl.ds(pl.multiple_of(y * NQ, NQ), NQ)]
    weights = []
    for tab in (tab0_ref, tab1_ref):
        w = jnp.zeros((1, NQ), F32)
        for k in range(count):
            w = jnp.where(labels == k, tab[k], w)
        weights.append(w * SCALE)
    half = len(ins) // 2
    for lane in range(2):
        lane_row = 64 * (c if lane == 0 else 1 - c)
        t = 0
        for ref in ins[lane * half:(lane + 1) * half]:
            for j in range(ref.shape[0]):
                off = pl.multiple_of(lane_row + 16 * lax.rem(y - t + NY, NY), 16)
                for m in range(6):
                    v = ref[j, m].astype(F32)
                    for k in range(2):
                        out_ref[k, pl.ds(off, 16), m * NQ:(m + 1) * NQ] = (v * weights[k]).astype(BF)
                t += 1


def weigh(tables, labels, own, other):
    args = (*own, *other)
    count = tables[0].shape[0]
    return pl.pallas_call(
        lambda *refs: weigh_kernel(count, *refs),
        out_shape=LHS_TYPE,
        in_specs=[SMEM_SPEC] * 2 + [VMEM_SPEC] * (1 + len(args)),
        out_specs=VMEM_SPEC,
        compiler_params=pltpu.CompilerParams(vmem_limit_bytes=VMEM_LIMIT),
        cost_estimate=pl.CostEstimate(flops=4 << 20, transcendentals=0, bytes_accessed=3 << 20),
        name="weigh",
    )(*tables, labels, *args)


def batch_kernel(n, counts, *refs):
    npieces = len(counts)
    pieces = refs[:npieces]
    lhs = refs[npieces:npieces + 4]
    outs = refs[npieces + 4:npieces + 8]
    rhs = refs[npieces + 8]
    y, _, x, _ = place()
    nc = 64 * n
    p, t = 0, 0
    for ref, cnt in zip(pieces, counts):
        for j in range(cnt):
            ys = lax.rem(y - t + NY, NY)
            off = pl.multiple_of(ys * (16 * n) + 16 * p, 16)
            off2 = pl.multiple_of(nc + ys * (16 * n) + 16 * p, 16)
            for m in range(3):
                re = ref[j, m]
                im = ref[j, m + 3]
                rhs[pl.ds(off, 16), m * NQ:(m + 1) * NQ] = re
                rhs[pl.ds(off, 16), (m + 3) * NQ:(m + 4) * NQ] = im
                rhs[pl.ds(off2, 16), m * NQ:(m + 1) * NQ] = im
                rhs[pl.ds(off2, 16), (m + 3) * NQ:(m + 4) * NQ] = -re
            t += 1
        if t == NY:
            p, t = p + 1, 0
    for r in range(4):
        a = lhs[r][...].reshape(256, KQ)
        res = lax.dot_general(a, rhs[...], (((1,), (1,)), ((), ())), preferred_element_type=F32)
        s = lax.rem(x + r - y + NY, NY)
        for k in range(4):
            @pl.when(s == k)
            def _():
                outs[k][...] = res.astype(outs[k].dtype)


def batch(pieces, lhs, n):
    counts = tuple(v.shape[0] for v in pieces)
    width = 128 * n
    flops = 2 * 1024 * width * KQ
    return pl.pallas_call(
        lambda *refs: batch_kernel(n, counts, *refs),
        out_shape=[jax.ShapeDtypeStruct((256, width), F32 if k == 0 else BF) for k in range(4)],
        in_specs=[VMEM_SPEC] * (len(pieces) + 4),
        out_specs=[VMEM_SPEC] * 4,
        scratch_shapes=[pltpu.VMEM((width, KQ), BF)],
        compiler_params=pltpu.CompilerParams(vmem_limit_bytes=VMEM_LIMIT),
        cost_estimate=pl.CostEstimate(flops=flops, transcendentals=0, bytes_accessed=4 << 20),
        name="partial_gram",
    )(*pieces, *lhs)


def order_kernel(out_ref):
    _, z, _, _ = place()
    base = 0
    for offsets in BATCHES:
        n = len(offsets)
        k = lax.broadcasted_iota(jnp.int32, (64 * n, NQ), 0)
        j = lax.broadcasted_iota(jnp.int32, (64 * n, NQ), 1)
        p = (k // 16) % n
        zs = jnp.full(k.shape, lax.rem(z + offsets[0], NZ))
        for q in range(1, n):
            zs = jnp.where(p == q, lax.rem(z + offsets[q], NZ), zs)
        target = 128 * (k // (16 * n)) + 16 * zs + k % 16
        out_ref[base:base + 64 * n] = (target == j).astype(F32).astype(BF)
        base += 64 * n


def collect_kernel(nb, *refs):
    parts = refs[:4 * nb]
    order_ref, noise_ref, energy_ref = refs[4 * nb:]
    total = [None, None]
    base = 0
    for b in range(nb):
        own, *rest = parts[4 * b:4 * b + 4]
        width = own.shape[1] // 2
        sel = order_ref[base:base + width]
        base += width
        for e in range(2):
            v = own[:, e * width:(e + 1) * width]
            for r in rest:
                v = v + r[:, e * width:(e + 1) * width].astype(F32)
            hi = v.astype(BF)
            lo = (v - hi.astype(F32)).astype(BF)
            d = jnp.dot(jnp.concatenate([hi, lo], axis=0), sel, preferred_element_type=F32)
            total[e] = d if total[e] is None else total[e] + d
    for e in range(2):
        d = total[e][0:256] + total[e][256:512]
        noise_ref[e] = d[0:128]
        energy_ref[e] = d[128:256]


def collect(parts):
    nb = len(BATCHES)
    order = pl.pallas_call(
        order_kernel,
        out_shape=jax.ShapeDtypeStruct((NQ, NQ), BF),
        out_specs=VMEM_SPEC,
        compiler_params=pltpu.CompilerParams(vmem_limit_bytes=VMEM_LIMIT),
        name="order",
    )()
    shape = jax.ShapeDtypeStruct((2, 128, 512), F32)
    return pl.pallas_call(
        lambda *refs: collect_kernel(nb, *refs),
        out_shape=[shape, shape],
        in_specs=[VMEM_SPEC] * (4 * nb + 1),
        out_specs=[VMEM_SPEC] * 2,
        compiler_params=pltpu.CompilerParams(vmem_limit_bytes=VMEM_LIMIT),
        name="collect",
    )(*[v for four in parts for v in four], order)


def body(responses, labels, conductivity, permittivity):
    y, _, _, c = place()
    tables = (conductivity, permittivity)
    labels = labels.reshape(1, labels.shape[0])
    quarters = responses.reshape(16, 2, 3, NY, NQ).transpose(3, 1, 2, 0, 4).reshape(NY, 6, 16, NQ)

    def along_y(v):
        got = [pick(v, y)]
        got += [row_permute(pick(v, (y + s) % NY), lambda a, b, s=s: (a + s, b)) for s in (1, 2, 3)]
        return jnp.stack(got)

    def one_way(first, second):
        return jnp.where(c == 0, first, second)

    cols = along_y(quarters)
    moved = all_permute(quarters, lambda y, z, x, c: (z % NY, NY * c + y, x, z // NY))
    up = row_permute(cols, lambda a, b: (a, b + 1))
    down = row_permute(cols, lambda a, b: (a, b - 1))
    mine = along_y(moved)
    left = col_permute(mine, lambda a, b: (a + 1, b))
    right = col_permute(mine, lambda a, b: (a - 1, b))
    far = col_permute(one_way(left, right), lambda a, b: (a + 1 - 2 * b, b))
    up2 = row_permute(up, lambda a, b: (a, b + 1))
    down2 = row_permute(down, lambda a, b: (a, b - 1))

    def swap(v):
        return col_permute(v, lambda a, b: (a, 1 - b))

    lhs = [weigh(tables, labels, [own], [swap(own)]) for own in (mine, right, far, left)]
    up3 = row_permute(up2, lambda a, b: (a, b + 1))
    down3 = row_permute(down2, lambda a, b: (a, b - 1))
    last = all_permute(one_way(up3, down3), lambda y, z, x, c: (y, (z + 1 - 2 * c) % NZ, x, c))

    parts = []
    for pieces, offsets in zip(([cols, up, down, up2], [down2, up3], [down3, last]), BATCHES):
        outs = batch(pieces, lhs, len(offsets))
        parts.append([outs[0]] + [row_permute(outs[s], lambda a, b, s=s: (a + s, b)) for s in (2, 1, 3)])
    return tuple(collect(parts))


def solution(mesh):
    in_specs = (P(("col", "row"), None, None, None), P(), P(), P())
    out_specs = (P(None, "row", "col"), P(None, "row", "col"))
    return jax.shard_map(body, mesh=mesh, in_specs=in_specs, out_specs=out_specs, check_vma=False)
```

time: 132 us -> 104 us (0.79)
  waiting for transfers between devices: 12.4 us -> 36.3 us
  Pallas kernels: 38.1 us -> 17.9 us
  starting transfers between devices: 60.3 us -> 45.9 us
  local copies, waits for them, and re-layouts: 10.3 us -> 1.45 us
  other arithmetic: 6.99 us -> 0.19 us
    ppermute x4 -> x2, waiting for transfers between devices: 0.73 us -> 13.2 us  [all_permute(): return lax.ppermute(v, ('row', 'col'), pairs)]
    pallas_call x3, Pallas kernels: 23.1 us -> 12.7 us  [batch(): pl.pallas_call(lambda *refs: batch_kernel(n, counts, *refs), out_shape=[j...]
    pallas_call x5 -> x6, Pallas kernels: 15 us -> 5.25 us  [the longest x4 3.19 us: weigh(): pl.pallas_call(lambda *refs: weigh_kernel(count, *refs), out_shape=LHS_TY...]
    ppermute x9 -> x7, starting transfers between devices: 12.6 us -> 3.44 us  [col_permute(): return lax.ppermute(v, 'col', pairs)]
    ppermute x20 -> x21, waiting for transfers between devices: 11 us -> 18.7 us  [row_permute(): return lax.ppermute(v, 'row', pairs)]
    ppermute x4 -> x2, starting transfers between devices: 10.2 us -> 5.28 us  [all_permute(): return lax.ppermute(v, ('row', 'col'), pairs)]
    convert_element_type x3 -> x0, other arithmetic: 3.88 us -> none  [selection(): return (target == jnp.arange(1024)[None, :]).astype(BF)]
    ppermute x9 -> x7, waiting for transfers between devices: 0.64 us -> 4.44 us  [col_permute(): return lax.ppermute(v, 'col', pairs)]
  transfers between devices with their start and end apart: 33 -> 30, of which waited for: 9 -> 9; matrix products, arithmetic and copies ran while one was open for 10% -> 0% of each run, Pallas kernels for 26% -> 16%
where the time goes in v2:
time: 104 us; the launch traced here: 103 us
  starting transfers between devices  45.9 us (44%)
  waiting for transfers between devices  36.3 us (35%)
  Pallas kernels  17.9 us (17%)
  local copies, waits for them, and re-layouts  1.45 us (1%)
    ppermute x21, starting transfers between devices, row_permute(): return lax.ppermute(v, 'row', pairs)  37.1 us
    ppermute x21, waiting for transfers between devices, row_permute(): return lax.ppermute(v, 'row', pairs)  18.7 us
    ppermute x2, waiting for transfers between devices, all_permute(): return lax.ppermute(v, ('row', 'col'), pairs)  13.2 us
    pallas_call x3, Pallas kernels, batch(): pl.pallas_call(lambda *refs: batch_kernel(n, counts, *refs), out_shape=[j...  12.7 us
    ppermute x2, starting transfers between devices, all_permute(): return lax.ppermute(v, ('row', 'col'), pairs)  5.28 us
    ppermute x7, waiting for transfers between devices, col_permute(): return lax.ppermute(v, 'col', pairs)  4.44 us
    ppermute x7, starting transfers between devices, col_permute(): return lax.ppermute(v, 'col', pairs)  3.44 us
    pallas_call x4, Pallas kernels, weigh(): pl.pallas_call(lambda *refs: weigh_kernel(count, *refs), out_shape=LHS_TY...  3.19 us
  transfers between devices with their start and end apart: 30, of which 9 were waited for; matrix products, arithmetic and copies ran while one was open for 0% of the time, Pallas kernels for 16%

profile of v2, /device:TPU:8, one launch (start us, length us, event | category | flops | bytes accessed | tf_op | source)
XLA Modules:
  0.0 102.7 jit_solution(11854607475999090679)
XLA Ops:
  0.6 1.2 %reshape.13 = bf16[16,2,3,4,512]{4,3,1,2,0:T(4,128)(2,1)S(1)} reshape(bf16[16,2,3,2048]{3,1,2,0:T(2,128)(2,1)} %param.4) | data formatting | bytes 786432 | tf_op jit(solution)/shard_map/reshape | solution.py:215
  2.0 3.7 %collective-permute-start.6 = (bf16[4,6,16,512]{3,2,1,0:T(8,128)(2,1)S(1)}, bf16[4,6,16,512]{3,2,1,0:T(8,128)(2,1)S(1)}, u32[]{:S(2)}, u32[]{:S(2)}) collective-permute-start(bf16[4,6,16,512]{3,2,1,0:T(8,128)(2,1)S(1)} %bitcast.28), channel_id=1, source_target_pairs={{0,0},{1,32},{2,2},{3,34},{4,4},{5,36},{6,6},{7,38},{8,64},{9,96},... | collective-permute-start | bytes 1179656 | tf_op jit(solution)/shard_map/ppermute | solution.py:47
  5.9 4.9 %collective-permute-start.1 = (bf16[6,16,512]{2,1,0:T(8,128)(2,1)S(1)}, bf16[6,16,512]{2,1,0:T(8,128)(2,1)S(1)}, u32[]{:S(2)}, u32[]{:S(2)}) collective-permute-start(bf16[6,16,512]{2,1,0:T(8,128)(2,1)S(1)} %get-tuple-element.32), channel_id=1, source_target_pairs={{0,128},{8,136},{16,144},{24,152},{32,160},{40,168},{48,176},{56,1... | collective-permute-start | bytes 294920 | tf_op jit(solution)/shard_map/ppermute | solution.py:27
  10.8 2.5 %collective-permute-start = (bf16[6,16,512]{2,1,0:T(8,128)(2,1)S(1)}, bf16[6,16,512]{2,1,0:T(8,128)(2,1)S(1)}, u32[]{:S(2)}, u32[]{:S(2)}) collective-permute-start(bf16[6,16,512]{2,1,0:T(8,128)(2,1)S(1)} %get-tuple-element.33), channel_id=1, source_target_pairs={{0,64},{8,72},{16,80},{24,88},{32,96},{40,104},{48,112},{56,120},{... | collective-permute-start | bytes 294920 | tf_op jit(solution)/shard_map/ppermute | solution.py:27
  13.3 13.2 %collective-permute-done.6 = bf16[4,6,16,512]{3,2,1,0:T(8,128)(2,1)S(1)} collective-permute-done((bf16[4,6,16,512]{3,2,1,0:T(8,128)(2,1)S(1)}, bf16[4,6,16,512]{3,2,1,0:T(8,128)(2,1)S(1)}, u32[]{:S(2)}, u32[]{:S(2)}) %collective-permute-start.6) | collective-permute-done | bytes 393248 | tf_op jit(solution)/shard_map/ppermute | solution.py:47
  26.7 1.9 %collective-permute-start.8 = (bf16[6,16,512]{2,1,0:T(8,128)(2,1)S(1)}, bf16[6,16,512]{2,1,0:T(8,128)(2,1)S(1)}, u32[]{:S(2)}, u32[]{:S(2)}) collective-permute-start(bf16[6,16,512]{2,1,0:T(8,128)(2,1)S(1)} %get-tuple-element.28), channel_id=1, source_target_pairs={{0,128},{8,136},{16,144},{24,152},{32,160},{40,168},{48,176},{56,1... | collective-permute-start | bytes 294920 | tf_op jit(solution)/shard_map/ppermute | solution.py:27
  28.7 5.8 %collective-permute-start.3 = (bf16[4,6,16,512]{3,2,1,0:T(8,128)(2,1)S(1)}, bf16[4,6,16,512]{3,2,1,0:T(8,128)(2,1)S(1)}, u32[]{:S(2)}, u32[]{:S(2)}) collective-permute-start(bf16[4,6,16,512]{3,2,1,0:T(8,128)(2,1)S(1)} %pad_maximum_fusion.refs_0_), channel_id=1, source_target_pairs={{0,8},{8,16},{16,24},{24,32},{32,40},{40,48},{48,56},{56,0},{64,72... | collective-permute-start | bytes 1179656 | tf_op jit(solution)/shard_map/ppermute | solution.py:27
  34.5 1.8 %collective-permute-start.4 = (bf16[4,6,16,512]{3,2,1,0:T(8,128)(2,1)S(1)}, bf16[4,6,16,512]{3,2,1,0:T(8,128)(2,1)S(1)}, u32[]{:S(2)}, u32[]{:S(2)}) collective-permute-start(bf16[4,6,16,512]{3,2,1,0:T(8,128)(2,1)S(1)} %pad_maximum_fusion.refs_0_), channel_id=1, source_target_pairs={{0,56},{8,0},{16,8},{24,16},{32,24},{40,32},{48,40},{56,48},{64,12... | collective-permute-start | bytes 1179656 | tf_op jit(solution)/shard_map/ppermute | solution.py:27
  36.4 2.8 %collective-permute-start.11 = (bf16[4,6,16,512]{3,2,1,0:T(8,128)(2,1)S(1)}, bf16[4,6,16,512]{3,2,1,0:T(8,128)(2,1)S(1)}, u32[]{:S(2)}, u32[]{:S(2)}) collective-permute-start(bf16[4,6,16,512]{3,2,1,0:T(8,128)(2,1)S(1)} %pad_maximum_fusion.1.refs_3_), channel_id=1, source_target_pairs={{0,6},{1,7},{2,0},{3,1},{4,2},{5,3},{6,4},{7,5},{8,14},{9,15},{10,... | collective-permute-start | bytes 1179656 | tf_op jit(solution)/shard_map/ppermute | solution.py:36
  39.3 5.4 %collective-permute-done.3.refs_1_ = bf16[4,6,16,512]{3,2,1,0:T(8,128)(2,1)S(1)} collective-permute-done((bf16[4,6,16,512]{3,2,1,0:T(8,128)(2,1)S(1)}, bf16[4,6,16,512]{3,2,1,0:T(8,128)(2,1)S(1)}, u32[]{:S(2)}, u32[]{:S(2)}) %collective-permute-start.3) | collective-permute-done | bytes 393248 | tf_op jit(solution)/shard_map/ppermute | solution.py:27
  44.7 3.2 %collective-permute-start.20 = (bf16[4,6,16,512]{3,2,1,0:T(8,128)(2,1)S(1)}, bf16[4,6,16,512]{3,2,1,0:T(8,128)(2,1)S(1)}, u32[]{:S(2)}, u32[]{:S(2)}) collective-permute-start(bf16[4,6,16,512]{3,2,1,0:T(8,128)(2,1)S(1)} %collective-permute-done.4.refs_2_), channel_id=1, source_target_pairs={{0,56},{8,0},{16,8},{24,16},{32,24},{40,32},{48,40},{56,48},{64,12... | collective-permute-start | bytes 1179656 | tf_op jit(solution)/shard_map/ppermute | solution.py:27
  47.9 3.3 %collective-permute-done.13.refs_3_ = bf16[4,6,16,512]{3,2,1,0:T(8,128)(2,1)S(1)} collective-permute-done((bf16[4,6,16,512]{3,2,1,0:T(8,128)(2,1)S(1)}, bf16[4,6,16,512]{3,2,1,0:T(8,128)(2,1)S(1)}, u32[]{:S(2)}, u32[]{:S(2)}) %collective-permute-start.13) | collective-permute-done | bytes 393248 | tf_op jit(solution)/shard_map/ppermute | solution.py:36
  51.3 4.1 %collective-permute-done.5.refs_3_ = bf16[4,6,16,512]{3,2,1,0:T(8,128)(2,1)S(1)} collective-permute-done((bf16[4,6,16,512]{3,2,1,0:T(8,128)(2,1)S(1)}, bf16[4,6,16,512]{3,2,1,0:T(8,128)(2,1)S(1)}, u32[]{:S(2)}, u32[]{:S(2)}) %collective-permute-start.5) | collective-permute-done | bytes 393248 | tf_op jit(solution)/shard_map/ppermute | solution.py:27
  55.4 3.2 %collective-permute-start.25 = (bf16[4,6,16,512]{3,2,1,0:T(8,128)(2,1)S(1)}, bf16[4,6,16,512]{3,2,1,0:T(8,128)(2,1)S(1)}, u32[]{:S(2)}, u32[]{:S(2)}) collective-permute-start(bf16[4,6,16,512]{3,2,1,0:T(8,128)(2,1)S(1)} %collective-permute-done.20.refs_0_), channel_id=1, source_target_pairs={{0,56},{8,0},{16,8},{24,16},{32,24},{40,32},{48,40},{56,48},{64,12... | collective-permute-start | bytes 1179656 | tf_op jit(solution)/shard_map/ppermute | solution.py:27
  59.2 1.1 %collective-permute-done.14.refs_3_ = bf16[4,6,16,512]{3,2,1,0:T(8,128)(2,1)S(1)} collective-permute-done((bf16[4,6,16,512]{3,2,1,0:T(8,128)(2,1)S(1)}, bf16[4,6,16,512]{3,2,1,0:T(8,128)(2,1)S(1)}, u32[]{:S(2)}, u32[]{:S(2)}) %collective-permute-start.14) | collective-permute-done | bytes 393248 | tf_op jit(solution)/shard_map/ppermute | solution.py:36
  60.3 0.8 weigh.4.refs_4_.refs_2_
  61.1 4.1 %collective-permute-done.21.refs_1_ = bf16[4,6,16,512]{3,2,1,0:T(8,128)(2,1)S(1)} collective-permute-done((bf16[4,6,16,512]{3,2,1,0:T(8,128)(2,1)S(1)}, bf16[4,6,16,512]{3,2,1,0:T(8,128)(2,1)S(1)}, u32[]{:S(2)}, u32[]{:S(2)}) %collective-permute-start.21) | collective-permute-done | bytes 393248 | tf_op jit(solution)/shard_map/ppermute | solution.py:27
  65.3 1.6 %collective-permute-start.26 = (bf16[4,6,16,512]{3,2,1,0:T(8,128)(2,1)S(1)}, bf16[4,6,16,512]{3,2,1,0:T(8,128)(2,1)S(1)}, u32[]{:S(2)}, u32[]{:S(2)}) collective-permute-start(bf16[4,6,16,512]{3,2,1,0:T(8,128)(2,1)S(1)} %broadcast_select_fusion), channel_id=1, source_target_pairs={{0,8},{1,57},{2,10},{3,59},{4,12},{5,61},{6,14},{7,63},{8,16},{9,1... | collective-permute-start | bytes 1179656 | tf_op jit(solution)/shard_map/ppermute | solution.py:47
  66.8 0.8 weigh.5.refs_5_.refs_3_
  67.7 0.8 weigh.7.refs_7_.refs_5_
  68.5 0.8 weigh.6.refs_6_.refs_4_
  69.3 4.5 %partial_gram.3 = (f32[256,512]{1,0:T(8,128)S(1)}, bf16[256,512]{1,0:T(8,128)(2,1)S(1)}, bf16[256,512]{1,0:T(8,128)(2,1)S(1)}, bf16[256,512]{1,0:T(8,128)(2,1)S(1)}) custom-call(bf16[4,6,16,512]{3,2,1,0:T(8,128)(2,1)S(1)} %pad_maximum_fusion.refs_0_, bf16[4,6,16,512]{3,2,1,0:T(8,128)(2,1)S(1)} %collective-permute-done.3.refs_1_, ...), custom_call_target="tpu_custom_call" | custom-call | flops 3221225472 | bytes 4194304 | tf_op jit(solution)/shard_map/partial_gram/pallas_call | solution.py:139
  73.8 3.0 %collective-permute-start.17 = (bf16[256,512]{1,0:T(8,128)(2,1)S(1)}, bf16[256,512]{1,0:T(8,128)(2,1)S(1)}, u32[]{:S(2)}, u32[]{:S(2)}) collective-permute-start(bf16[256,512]{1,0:T(8,128)(2,1)S(1)} %get-tuple-element.15), channel_id=1, source_target_pairs={{0,128},{8,136},{16,144},{24,152},{32,160},{40,168},{48,176},{56,1... | collective-permute-start | bytes 786440 | tf_op jit(solution)/shard_map/ppermute | solution.py:27
  76.8 4.1 %partial_gram.4 = (f32[256,256]{1,0:T(8,128)S(1)}, bf16[256,256]{1,0:T(8,128)(2,1)S(1)}, bf16[256,256]{1,0:T(8,128)(2,1)S(1)}, bf16[256,256]{1,0:T(8,128)(2,1)S(1)}) custom-call(bf16[4,6,16,512]{3,2,1,0:T(8,128)(2,1)S(1)} %collective-permute-done.20.refs_0_, bf16[4,6,16,512]{3,2,1,0:T(8,128)(2,1)S(1)} %collective-permute-done.21.refs_1_, ...), custom_call_target="tpu_custom_call" | custom-call | flops 1610612736 | bytes 4194304 | tf_op jit(solution)/shard_map/partial_gram/pallas_call | solution.py:139
  82.0 1.6 %collective-permute-start.24 = (bf16[256,256]{1,0:T(8,128)(2,1)S(1)}, bf16[256,256]{1,0:T(8,128)(2,1)S(1)}, u32[]{:S(2)}, u32[]{:S(2)}) collective-permute-start(bf16[256,256]{1,0:T(8,128)(2,1)S(1)} %get-tuple-element.21), channel_id=1, source_target_pairs={{0,192},{8,200},{16,208},{24,216},{32,224},{40,232},{48,240},{56,2... | collective-permute-start | bytes 393224 | tf_op jit(solution)/shard_map/ppermute | solution.py:27
  83.6 4.1 %partial_gram.5 = (f32[256,256]{1,0:T(8,128)S(1)}, bf16[256,256]{1,0:T(8,128)(2,1)S(1)}, bf16[256,256]{1,0:T(8,128)(2,1)S(1)}, bf16[256,256]{1,0:T(8,128)(2,1)S(1)}) custom-call(bf16[4,6,16,512]{3,2,1,0:T(8,128)(2,1)S(1)} %collective-permute-done.25.refs_0_, bf16[4,6,16,512]{3,2,1,0:T(8,128)(2,1)S(1)} %collective-permute-done.26.refs_1_, ...), custom_call_target="tpu_custom_call" | custom-call | flops 1610612736 | bytes 4194304 | tf_op jit(solution)/shard_map/partial_gram/pallas_call | solution.py:139
  87.7 3.0 %collective-permute-start.27 = (bf16[256,256]{1,0:T(8,128)(2,1)S(1)}, bf16[256,256]{1,0:T(8,128)(2,1)S(1)}, u32[]{:S(2)}, u32[]{:S(2)}) collective-permute-start(bf16[256,256]{1,0:T(8,128)(2,1)S(1)} %get-tuple-element.23), channel_id=1, source_target_pairs={{0,128},{8,136},{16,144},{24,152},{32,160},{40,168},{48,176},{56,1... | collective-permute-start | bytes 393224 | tf_op jit(solution)/shard_map/ppermute | solution.py:27
  91.4 1.4 %collective-permute-start.19 = (bf16[256,512]{1,0:T(8,128)(2,1)S(1)}, bf16[256,512]{1,0:T(8,128)(2,1)S(1)}, u32[]{:S(2)}, u32[]{:S(2)}) collective-permute-start(bf16[256,512]{1,0:T(8,128)(2,1)S(1)} %get-tuple-element.17), channel_id=1, source_target_pairs={{0,192},{8,200},{16,208},{24,216},{32,224},{40,232},{48,240},{56,2... | collective-permute-start | bytes 786440 | tf_op jit(solution)/shard_map/ppermute | solution.py:27
  93.4 2.4 %collective-permute-done.27.refs_9_ = bf16[256,256]{1,0:T(8,128)(2,1)S(1)} collective-permute-done((bf16[256,256]{1,0:T(8,128)(2,1)S(1)}, bf16[256,256]{1,0:T(8,128)(2,1)S(1)}, u32[]{:S(2)}, u32[]{:S(2)}) %collective-permute-start.27) | collective-permute-done | bytes 131104 | tf_op jit(solution)/shard_map/ppermute | solution.py:27
  95.7 2.1 %collective-permute-start.29 = (bf16[256,256]{1,0:T(8,128)(2,1)S(1)}, bf16[256,256]{1,0:T(8,128)(2,1)S(1)}, u32[]{:S(2)}, u32[]{:S(2)}) collective-permute-start(bf16[256,256]{1,0:T(8,128)(2,1)S(1)} %get-tuple-element.25), channel_id=1, source_target_pairs={{0,192},{8,200},{16,208},{24,216},{32,224},{40,232},{48,240},{56,2... | collective-permute-start | bytes 393224 | tf_op jit(solution)/shard_map/ppermute | solution.py:27
  98.0 2.3 %collective-permute-done.28.refs_10_ = bf16[256,256]{1,0:T(8,128)(2,1)S(1)} collective-permute-done((bf16[256,256]{1,0:T(8,128)(2,1)S(1)}, bf16[256,256]{1,0:T(8,128)(2,1)S(1)}, u32[]{:S(2)}, u32[]{:S(2)}) %collective-permute-start.28) | collective-permute-done | bytes 131104 | tf_op jit(solution)/shard_map/ppermute | solution.py:27
  100.8 1.9 %collect.1 = (f32[2,128,512]{2,1,0:T(8,128)}, f32[2,128,512]{2,1,0:T(8,128)}) custom-call(f32[256,512]{1,0:T(8,128)S(1)} %get-tuple-element.14.refs_0_, bf16[256,512]{1,0:T(8,128)(2,1)S(1)} %collective-permute-done.17.refs_1_, bf16[256,512]{1,0:T(8,128)(2,1)S(1)} %collective-permute-done.18.refs_2_, bf16[256,512]{1,0:T(8,128)(2,1)S(1)} %collective-permute-done.19.refs_3_, ...), custom_call_target="tpu_custom_call" | custom-call | tf_op jit(solution)/shard_map/collect/pallas_call | solution.py:201
  (51 shorter events, 4.2 us)
Async XLA Ops:
  2.0 24.5 %collective-permute-start.6 = (bf16[4,6,16,512]{3,2,1,0:T(8,128)(2,1)S(1)}, bf16[4,6,16,512]{3,2,1,0:T(8,128)(2,1)S(1)}, u32[]{:S(2)}, u32[]{:S(2)}) collective-permute-start(bf16[4,6,16,512]{3,2,1,0:T(8,128)(2,1)S(1)} %bitcast.28), channel_id=1, source_target_pairs={{0,0},{1,32},{2,2},{3,34},{4,4},{5,36},{6,6},{7,38},{8,64},{9,96},... | collective-permute-start | bytes 1179656 | tf_op jit(solution)/shard_map/ppermute | solution.py:47
  5.9 22.7 %collective-permute-start.2 = (bf16[6,16,512]{2,1,0:T(8,128)(2,1)S(1)}, bf16[6,16,512]{2,1,0:T(8,128)(2,1)S(1)}, u32[]{:S(2)}, u32[]{:S(2)}) collective-permute-start(bf16[6,16,512]{2,1,0:T(8,128)(2,1)S(1)} %get-tuple-element.31), channel_id=1, source_target_pairs={{0,192},{8,200},{16,208},{24,216},{32,224},{40,232},{48,240},{56,2... | collective-permute-start | bytes 294920 | tf_op jit(solution)/shard_map/ppermute | solution.py:27
  5.9 22.7 %collective-permute-start.1 = (bf16[6,16,512]{2,1,0:T(8,128)(2,1)S(1)}, bf16[6,16,512]{2,1,0:T(8,128)(2,1)S(1)}, u32[]{:S(2)}, u32[]{:S(2)}) collective-permute-start(bf16[6,16,512]{2,1,0:T(8,128)(2,1)S(1)} %get-tuple-element.32), channel_id=1, source_target_pairs={{0,128},{8,136},{16,144},{24,152},{32,160},{40,168},{48,176},{56,1... | collective-permute-start | bytes 294920 | tf_op jit(solution)/shard_map/ppermute | solution.py:27
  10.8 17.9 %collective-permute-start = (bf16[6,16,512]{2,1,0:T(8,128)(2,1)S(1)}, bf16[6,16,512]{2,1,0:T(8,128)(2,1)S(1)}, u32[]{:S(2)}, u32[]{:S(2)}) collective-permute-start(bf16[6,16,512]{2,1,0:T(8,128)(2,1)S(1)} %get-tuple-element.33), channel_id=1, source_target_pairs={{0,64},{8,72},{16,80},{24,88},{32,96},{40,104},{48,112},{56,120},{... | collective-permute-start | bytes 294920 | tf_op jit(solution)/shard_map/ppermute | solution.py:27
  26.5 33.8 %copy-start = (s32[2048]{0:T(1024)S(1)}, s32[2048]{0:T(1024)}, u32[]{:S(2)}) copy-start(s32[2048]{0:T(1024)} %param.5) | copy-start | bytes 24580
  26.5 33.8 %copy-start.1 = (f32[16]{0:T(128)S(1)}, f32[16]{0:T(128)}, u32[]{:S(2)}) copy-start(f32[16]{0:T(128)} %refs_0_.7) | copy-start | bytes 196
  26.6 9.8 %collective-permute-start.9 = (bf16[6,16,512]{2,1,0:T(8,128)(2,1)S(1)}, bf16[6,16,512]{2,1,0:T(8,128)(2,1)S(1)}, u32[]{:S(2)}, u32[]{:S(2)}) collective-permute-start(bf16[6,16,512]{2,1,0:T(8,128)(2,1)S(1)} %get-tuple-element.27), channel_id=1, source_target_pairs={{0,192},{8,200},{16,208},{24,216},{32,224},{40,232},{48,240},{56,2... | collective-permute-start | bytes 294920 | tf_op jit(solution)/shard_map/ppermute | solution.py:27
  26.7 9.7 %collective-permute-start.8 = (bf16[6,16,512]{2,1,0:T(8,128)(2,1)S(1)}, bf16[6,16,512]{2,1,0:T(8,128)(2,1)S(1)}, u32[]{:S(2)}, u32[]{:S(2)}) collective-permute-start(bf16[6,16,512]{2,1,0:T(8,128)(2,1)S(1)} %get-tuple-element.28), channel_id=1, source_target_pairs={{0,128},{8,136},{16,144},{24,152},{32,160},{40,168},{48,176},{56,1... | collective-permute-start | bytes 294920 | tf_op jit(solution)/shard_map/ppermute | solution.py:27
  28.6 7.8 %collective-permute-start.7 = (bf16[6,16,512]{2,1,0:T(8,128)(2,1)S(1)}, bf16[6,16,512]{2,1,0:T(8,128)(2,1)S(1)}, u32[]{:S(2)}, u32[]{:S(2)}) collective-permute-start(bf16[6,16,512]{2,1,0:T(8,128)(2,1)S(1)} %get-tuple-element.29), channel_id=1, source_target_pairs={{0,64},{8,72},{16,80},{24,88},{32,96},{40,104},{48,112},{56,120},{... | collective-permute-start | bytes 294920 | tf_op jit(solution)/shard_map/ppermute | solution.py:27
  28.7 15.9 %collective-permute-start.3 = (bf16[4,6,16,512]{3,2,1,0:T(8,128)(2,1)S(1)}, bf16[4,6,16,512]{3,2,1,0:T(8,128)(2,1)S(1)}, u32[]{:S(2)}, u32[]{:S(2)}) collective-permute-start(bf16[4,6,16,512]{3,2,1,0:T(8,128)(2,1)S(1)} %pad_maximum_fusion.refs_0_), channel_id=1, source_target_pairs={{0,8},{8,16},{16,24},{24,32},{32,40},{40,48},{48,56},{56,0},{64,72... | collective-permute-start | bytes 1179656 | tf_op jit(solution)/shard_map/ppermute | solution.py:27
  34.5 10.1 %collective-permute-start.4 = (bf16[4,6,16,512]{3,2,1,0:T(8,128)(2,1)S(1)}, bf16[4,6,16,512]{3,2,1,0:T(8,128)(2,1)S(1)}, u32[]{:S(2)}, u32[]{:S(2)}) collective-permute-start(bf16[4,6,16,512]{3,2,1,0:T(8,128)(2,1)S(1)} %pad_maximum_fusion.refs_0_), channel_id=1, source_target_pairs={{0,56},{8,0},{16,8},{24,16},{32,24},{40,32},{48,40},{56,48},{64,12... | collective-permute-start | bytes 1179656 | tf_op jit(solution)/shard_map/ppermute | solution.py:27
  36.4 11.5 %collective-permute-start.11 = (bf16[4,6,16,512]{3,2,1,0:T(8,128)(2,1)S(1)}, bf16[4,6,16,512]{3,2,1,0:T(8,128)(2,1)S(1)}, u32[]{:S(2)}, u32[]{:S(2)}) collective-permute-start(bf16[4,6,16,512]{3,2,1,0:T(8,128)(2,1)S(1)} %pad_maximum_fusion.1.refs_3_), channel_id=1, source_target_pairs={{0,6},{1,7},{2,0},{3,1},{4,2},{5,3},{6,4},{7,5},{8,14},{9,15},{10,... | collective-permute-start | bytes 1179656 | tf_op jit(solution)/shard_map/ppermute | solution.py:36
  39.3 11.9 %collective-permute-start.13 = (bf16[4,6,16,512]{3,2,1,0:T(8,128)(2,1)S(1)}, bf16[4,6,16,512]{3,2,1,0:T(8,128)(2,1)S(1)}, u32[]{:S(2)}, u32[]{:S(2)}) collective-permute-start(bf16[4,6,16,512]{3,2,1,0:T(8,128)(2,1)S(1)} %pad_maximum_fusion.1.refs_3_), channel_id=1, source_target_pairs={{0,2},{1,3},{2,4},{3,5},{4,6},{5,7},{6,0},{7,1},{8,10},{9,11},{10,... | collective-permute-start | bytes 1179656 | tf_op jit(solution)/shard_map/ppermute | solution.py:36
  44.7 10.7 %collective-permute-start.5 = (bf16[4,6,16,512]{3,2,1,0:T(8,128)(2,1)S(1)}, bf16[4,6,16,512]{3,2,1,0:T(8,128)(2,1)S(1)}, u32[]{:S(2)}, u32[]{:S(2)}) collective-permute-start(bf16[4,6,16,512]{3,2,1,0:T(8,128)(2,1)S(1)} %collective-permute-done.3.refs_1_), channel_id=1, source_target_pairs={{0,8},{8,16},{16,24},{24,32},{32,40},{40,48},{48,56},{56,0},{64,72... | collective-permute-start | bytes 1179656 | tf_op jit(solution)/shard_map/ppermute | solution.py:27
  44.7 10.7 %collective-permute-start.20 = (bf16[4,6,16,512]{3,2,1,0:T(8,128)(2,1)S(1)}, bf16[4,6,16,512]{3,2,1,0:T(8,128)(2,1)S(1)}, u32[]{:S(2)}, u32[]{:S(2)}) collective-permute-start(bf16[4,6,16,512]{3,2,1,0:T(8,128)(2,1)S(1)} %collective-permute-done.4.refs_2_), channel_id=1, source_target_pairs={{0,56},{8,0},{16,8},{24,16},{32,24},{40,32},{48,40},{56,48},{64,12... | collective-permute-start | bytes 1179656 | tf_op jit(solution)/shard_map/ppermute | solution.py:27
  47.9 10.7 %collective-permute-start.10 = (bf16[4,6,16,512]{3,2,1,0:T(8,128)(2,1)S(1)}, bf16[4,6,16,512]{3,2,1,0:T(8,128)(2,1)S(1)}, u32[]{:S(2)}, u32[]{:S(2)}) collective-permute-start(bf16[4,6,16,512]{3,2,1,0:T(8,128)(2,1)S(1)} %pad_maximum_fusion.1.refs_3_), channel_id=1, source_target_pairs={{0,1},{1,0},{2,3},{3,2},{4,5},{5,4},{6,7},{7,6},{8,9},{9,8},{10,11... | collective-permute-start | bytes 1179656 | tf_op jit(solution)/shard_map/ppermute | solution.py:36
  51.3 9.1 %collective-permute-start.14 = (bf16[4,6,16,512]{3,2,1,0:T(8,128)(2,1)S(1)}, bf16[4,6,16,512]{3,2,1,0:T(8,128)(2,1)S(1)}, u32[]{:S(2)}, u32[]{:S(2)}) collective-permute-start(bf16[4,6,16,512]{3,2,1,0:T(8,128)(2,1)S(1)} %broadcast_select_fusion.1), channel_id=1, source_target_pairs={{0,2},{1,7},{2,4},{3,1},{4,6},{5,3},{6,0},{7,5},{8,10},{9,15},{10,... | collective-permute-start | bytes 1179656 | tf_op jit(solution)/shard_map/ppermute | solution.py:36
  55.4 9.8 %collective-permute-start.21 = (bf16[4,6,16,512]{3,2,1,0:T(8,128)(2,1)S(1)}, bf16[4,6,16,512]{3,2,1,0:T(8,128)(2,1)S(1)}, u32[]{:S(2)}, u32[]{:S(2)}) collective-permute-start(bf16[4,6,16,512]{3,2,1,0:T(8,128)(2,1)S(1)} %collective-permute-done.5.refs_3_), channel_id=1, source_target_pairs={{0,8},{8,16},{16,24},{24,32},{32,40},{40,48},{48,56},{56,0},{64,72... | collective-permute-start | bytes 1179656 | tf_op jit(solution)/shard_map/ppermute | solution.py:27
  55.4 9.8 %collective-permute-start.25 = (bf16[4,6,16,512]{3,2,1,0:T(8,128)(2,1)S(1)}, bf16[4,6,16,512]{3,2,1,0:T(8,128)(2,1)S(1)}, u32[]{:S(2)}, u32[]{:S(2)}) collective-permute-start(bf16[4,6,16,512]{3,2,1,0:T(8,128)(2,1)S(1)} %collective-permute-done.20.refs_0_), channel_id=1, source_target_pairs={{0,56},{8,0},{16,8},{24,16},{32,24},{40,32},{48,40},{56,48},{64,12... | collective-permute-start | bytes 1179656 | tf_op jit(solution)/shard_map/ppermute | solution.py:27
  58.7 8.2 %collective-permute-start.12 = (bf16[4,6,16,512]{3,2,1,0:T(8,128)(2,1)S(1)}, bf16[4,6,16,512]{3,2,1,0:T(8,128)(2,1)S(1)}, u32[]{:S(2)}, u32[]{:S(2)}) collective-permute-start(bf16[4,6,16,512]{3,2,1,0:T(8,128)(2,1)S(1)} %collective-permute-done.11.refs_3_), channel_id=1, source_target_pairs={{0,1},{1,0},{2,3},{3,2},{4,5},{5,4},{6,7},{7,6},{8,9},{9,8},{10,11... | collective-permute-start | bytes 1179656 | tf_op jit(solution)/shard_map/ppermute | solution.py:36
  58.7 9.0 %collective-permute-start.16 = (bf16[4,6,16,512]{3,2,1,0:T(8,128)(2,1)S(1)}, bf16[4,6,16,512]{3,2,1,0:T(8,128)(2,1)S(1)}, u32[]{:S(2)}, u32[]{:S(2)}) collective-permute-start(bf16[4,6,16,512]{3,2,1,0:T(8,128)(2,1)S(1)} %collective-permute-done.13.refs_3_), channel_id=1, source_target_pairs={{0,1},{1,0},{2,3},{3,2},{4,5},{5,4},{6,7},{7,6},{8,9},{9,8},{10,11... | collective-permute-start | bytes 1179656 | tf_op jit(solution)/shard_map/ppermute | solution.py:36
  60.3 8.1 %collective-permute-start.15 = (bf16[4,6,16,512]{3,2,1,0:T(8,128)(2,1)S(1)}, bf16[4,6,16,512]{3,2,1,0:T(8,128)(2,1)S(1)}, u32[]{:S(2)}, u32[]{:S(2)}) collective-permute-start(bf16[4,6,16,512]{3,2,1,0:T(8,128)(2,1)S(1)} %collective-permute-done.14.refs_3_), channel_id=1, source_target_pairs={{0,1},{1,0},{2,3},{3,2},{4,5},{5,4},{6,7},{7,6},{8,9},{9,8},{10,11... | collective-permute-start | bytes 1179656 | tf_op jit(solution)/shard_map/ppermute | solution.py:36
  65.3 18.4 %collective-permute-start.26 = (bf16[4,6,16,512]{3,2,1,0:T(8,128)(2,1)S(1)}, bf16[4,6,16,512]{3,2,1,0:T(8,128)(2,1)S(1)}, u32[]{:S(2)}, u32[]{:S(2)}) collective-permute-start(bf16[4,6,16,512]{3,2,1,0:T(8,128)(2,1)S(1)} %broadcast_select_fusion), channel_id=1, source_target_pairs={{0,8},{1,57},{2,10},{3,59},{4,12},{5,61},{6,14},{7,63},{8,16},{9,1... | collective-permute-start | bytes 1179656 | tf_op jit(solution)/shard_map/ppermute | solution.py:47
  73.8 26.9 %collective-permute-start.17 = (bf16[256,512]{1,0:T(8,128)(2,1)S(1)}, bf16[256,512]{1,0:T(8,128)(2,1)S(1)}, u32[]{:S(2)}, u32[]{:S(2)}) collective-permute-start(bf16[256,512]{1,0:T(8,128)(2,1)S(1)} %get-tuple-element.15), channel_id=1, source_target_pairs={{0,128},{8,136},{16,144},{24,152},{32,160},{40,168},{48,176},{56,1... | collective-permute-start | bytes 786440 | tf_op jit(solution)/shard_map/ppermute | solution.py:27
  80.9 9.8 %collective-permute-start.22 = (bf16[256,256]{1,0:T(8,128)(2,1)S(1)}, bf16[256,256]{1,0:T(8,128)(2,1)S(1)}, u32[]{:S(2)}, u32[]{:S(2)}) collective-permute-start(bf16[256,256]{1,0:T(8,128)(2,1)S(1)} %get-tuple-element.19), channel_id=1, source_target_pairs={{0,128},{8,136},{16,144},{24,152},{32,160},{40,168},{48,176},{56,1... | collective-permute-start | bytes 393224 | tf_op jit(solution)/shard_map/ppermute | solution.py:27
  81.6 9.8 %collective-permute-start.23 = (bf16[256,256]{1,0:T(8,128)(2,1)S(1)}, bf16[256,256]{1,0:T(8,128)(2,1)S(1)}, u32[]{:S(2)}, u32[]{:S(2)}) collective-permute-start(bf16[256,256]{1,0:T(8,128)(2,1)S(1)} %get-tuple-element.20), channel_id=1, source_target_pairs={{0,64},{8,72},{16,80},{24,88},{32,96},{40,104},{48,112},{56,120},{... | collective-permute-start | bytes 393224 | tf_op jit(solution)/shard_map/ppermute | solution.py:27
  82.0 10.7 %collective-permute-start.24 = (bf16[256,256]{1,0:T(8,128)(2,1)S(1)}, bf16[256,256]{1,0:T(8,128)(2,1)S(1)}, u32[]{:S(2)}, u32[]{:S(2)}) collective-permute-start(bf16[256,256]{1,0:T(8,128)(2,1)S(1)} %get-tuple-element.21), channel_id=1, source_target_pairs={{0,192},{8,200},{16,208},{24,216},{32,224},{40,232},{48,240},{56,2... | collective-permute-start | bytes 393224 | tf_op jit(solution)/shard_map/ppermute | solution.py:27
  87.7 8.0 %collective-permute-start.27 = (bf16[256,256]{1,0:T(8,128)(2,1)S(1)}, bf16[256,256]{1,0:T(8,128)(2,1)S(1)}, u32[]{:S(2)}, u32[]{:S(2)}) collective-permute-start(bf16[256,256]{1,0:T(8,128)(2,1)S(1)} %get-tuple-element.23), channel_id=1, source_target_pairs={{0,128},{8,136},{16,144},{24,152},{32,160},{40,168},{48,176},{56,1... | collective-permute-start | bytes 393224 | tf_op jit(solution)/shard_map/ppermute | solution.py:27
  90.7 10.0 %collective-permute-start.18 = (bf16[256,512]{1,0:T(8,128)(2,1)S(1)}, bf16[256,512]{1,0:T(8,128)(2,1)S(1)}, u32[]{:S(2)}, u32[]{:S(2)}) collective-permute-start(bf16[256,512]{1,0:T(8,128)(2,1)S(1)} %get-tuple-element.16), channel_id=1, source_target_pairs={{0,64},{8,72},{16,80},{24,88},{32,96},{40,104},{48,112},{56,120},{... | collective-permute-start | bytes 786440 | tf_op jit(solution)/shard_map/ppermute | solution.py:27
  91.4 9.4 %collective-permute-start.19 = (bf16[256,512]{1,0:T(8,128)(2,1)S(1)}, bf16[256,512]{1,0:T(8,128)(2,1)S(1)}, u32[]{:S(2)}, u32[]{:S(2)}) collective-permute-start(bf16[256,512]{1,0:T(8,128)(2,1)S(1)} %get-tuple-element.17), channel_id=1, source_target_pairs={{0,192},{8,200},{16,208},{24,216},{32,224},{40,232},{48,240},{56,2... | collective-permute-start | bytes 786440 | tf_op jit(solution)/shard_map/ppermute | solution.py:27
  92.8 7.6 %collective-permute-start.28 = (bf16[256,256]{1,0:T(8,128)(2,1)S(1)}, bf16[256,256]{1,0:T(8,128)(2,1)S(1)}, u32[]{:S(2)}, u32[]{:S(2)}) collective-permute-start(bf16[256,256]{1,0:T(8,128)(2,1)S(1)} %get-tuple-element.24), channel_id=1, source_target_pairs={{0,64},{8,72},{16,80},{24,88},{32,96},{40,104},{48,112},{56,120},{... | collective-permute-start | bytes 393224 | tf_op jit(solution)/shard_map/ppermute | solution.py:27
  95.7 5.0 %collective-permute-start.29 = (bf16[256,256]{1,0:T(8,128)(2,1)S(1)}, bf16[256,256]{1,0:T(8,128)(2,1)S(1)}, u32[]{:S(2)}, u32[]{:S(2)}) collective-permute-start(bf16[256,256]{1,0:T(8,128)(2,1)S(1)} %get-tuple-element.25), channel_id=1, source_target_pairs={{0,192},{8,200},{16,208},{24,216},{32,224},{40,232},{48,240},{56,2... | collective-permute-start | bytes 393224 | tf_op jit(solution)/shard_map/ppermute | solution.py:27
  (1 other events, 33.8 us)

commit v3 on v0

v3 whole, which is shorter than its diff:
```python
import jax
import jax.numpy as jnp
import numpy as np
from jax import lax
from jax.experimental import pallas as pl
from jax.experimental.pallas import tpu as pltpu
from jax.sharding import PartitionSpec as P

NY, NZ, NX, NC = 4, 8, 4, 2
NQ = 512
KQ = 6 * NQ
BF = jnp.bfloat16
F32 = jnp.float32
VMEM_LIMIT = 24 * 1024 * 1024
SCALE = np.float32(1) / np.sqrt(np.float32(6 * 2048))
COST = pl.CostEstimate(flops=1, transcendentals=0, bytes_accessed=1)
SMEM_SPEC = pl.BlockSpec(memory_space=pltpu.SMEM)
VMEM_SPEC = pl.BlockSpec(memory_space=pltpu.VMEM)
PARAMS = pltpu.CompilerParams(vmem_limit_bytes=VMEM_LIMIT)

RING4 = (0, -1, 1, 2)


def place():
    row, col = lax.axis_index("row"), lax.axis_index("col")
    return row // NZ, row % NZ, col // NC, col % NC


def permute(v, move):
    pairs = []
    for y in range(NY):
        for z in range(NZ):
            for x in range(NX):
                for c in range(NC):
                    y2, z2, x2, c2 = move(y, z, x, c)
                    to = ((y2 % NY * NZ + z2 % NZ) * NX + x2 % NX) * NC + c2
                    pairs.append((((y * NZ + z) * NX + x) * NC + c, to))
    return lax.ppermute(v, ("row", "col"), pairs)


def along(axis, step):
    dy, dz, dx = ((step if axis == a else 0) for a in "yzx")
    return lambda y, z, x, c: (y + dy, z + dz, x + dx, c)


def swap(v):
    return permute(v, lambda y, z, x, c: (y, z, x, 1 - c))


def ring4(v, axis):
    half = v.shape[0] // 2
    before = permute(v, along(axis, 1))
    after = permute(v, along(axis, -1))
    far = [permute(before[:half], along(axis, 1)), permute(after[half:], along(axis, -1))]
    return [v], [before], [after], far


def weigh_kernel(count, quarter, tab0_ref, tab1_ref, labels_ref, *refs):
    ins, out_ref = refs[:-1], refs[-1]
    c = place()[3]
    labels = labels_ref[0:1, pl.ds(pl.multiple_of((2 * c + quarter) * NQ, NQ), NQ)]
    weights = []
    for tab in (tab0_ref, tab1_ref):
        w = jnp.zeros((1, NQ), F32)
        for k in range(count):
            w = jnp.where(labels == k, tab[k], w)
        weights.append(w * SCALE)
    off = 0
    for ref in ins:
        for j in range(ref.shape[0]):
            for lane in range(NC):
                for m in range(6):
                    v = ref[j, lane, m].astype(F32)
                    for k in range(2):
                        out_ref[k, off:off + 16, m * NQ:(m + 1) * NQ] = (v * weights[k]).astype(BF)
                off += 16


def weigh(tables, labels, quarter, pieces):
    count = tables[0].shape[0]
    return pl.pallas_call(
        lambda *refs: weigh_kernel(count, quarter, *refs),
        out_shape=pltpu.VMEM((2, 128, KQ), BF),
        in_specs=[SMEM_SPEC] * 2 + [VMEM_SPEC] * (1 + len(pieces)),
        out_specs=VMEM_SPEC,
        compiler_params=PARAMS,
        cost_estimate=COST,
        name="weigh",
    )(*tables, labels, *pieces)


def columns_kernel(plan, *refs):
    outs = refs[-2:]
    z = place()[1]
    for ref, (step, first) in zip(refs, plan):
        base = pl.multiple_of(16 * lax.rem(z + step + NZ, NZ), 16)
        base2 = pl.multiple_of(128 + 16 * lax.rem(z + step + NZ, NZ), 16)
        for j in range(ref.shape[0]):
            out = outs[first + j]
            for q in range(2):
                for m in range(3):
                    re, im = ref[j, q, m], ref[j, q, m + 3]
                    lo = slice(q * KQ + m * NQ, q * KQ + (m + 1) * NQ)
                    hi = slice(q * KQ + (m + 3) * NQ, q * KQ + (m + 4) * NQ)
                    out[pl.ds(base, 16), lo] = re
                    out[pl.ds(base, 16), hi] = im
                    out[pl.ds(base2, 16), lo] = im
                    out[pl.ds(base2, 16), hi] = -re


def columns(pieces, plan):
    return pl.pallas_call(
        lambda *refs: columns_kernel(plan, *refs),
        out_shape=[pltpu.VMEM((256, 2 * KQ), BF)] * NC,
        in_specs=[VMEM_SPEC] * len(pieces),
        out_specs=[VMEM_SPEC] * NC,
        compiler_params=PARAMS,
        cost_estimate=COST,
        name="columns",
    )(*pieces)


def gram_kernel(steps, carried, *refs):
    out_ref = refs[-1]
    rhs = refs[carried]
    lhs = refs[carried + 1:-1]
    y, _, x, c = place()
    out_ref[...] = refs[0][...] if carried else jnp.zeros(out_ref.shape, F32)
    for q in range(2):
        for k, step in enumerate(steps):
            a = lhs[q * len(steps) + k][...].reshape(256, KQ)
            d = lax.dot_general(a, rhs[:, q * KQ:(q + 1) * KQ], (((1,), (1,)), ((), ())), preferred_element_type=F32)
            for j, other in enumerate(RING4):
                dx, dy = (step, other) if q == 0 else (other, step)
                at = 128 * lax.rem(x + dx + NX, NX) + 16 * lax.rem(y + dy + NY, NY)
                for lane in range(NC):
                    off = pl.multiple_of(at + 64 * (c if lane == 0 else 1 - c), 16)
                    lo = 32 * j + 16 * lane
                    for k2 in range(2):
                        out_ref[k2, pl.ds(off, 16), :] += d[128 * k2 + lo:128 * k2 + lo + 16]


def gram(acc, rhs, lhs, steps):
    carried = acc is not None
    args = ([acc] if carried else []) + [rhs] + lhs
    return pl.pallas_call(
        lambda *refs: gram_kernel(steps, int(carried), *refs),
        out_shape=pltpu.VMEM((2, 512, 256), F32),
        in_specs=[VMEM_SPEC] * len(args),
        out_specs=VMEM_SPEC,
        compiler_params=PARAMS,
        cost_estimate=COST,
        name="gram",
    )(*args)


def pack_kernel(a_ref, b_ref, out_ref):
    for k in range(2):
        for f in range(NY * NZ):
            v = (a_ref[k, 16 * f:16 * f + 16] + b_ref[k, 16 * f:16 * f + 16]).astype(BF)
            for e in range(2):
                out_ref[f, 2 * k + e] = v[:, 128 * e:128 * e + 128]


def pack(a, b):
    return pl.pallas_call(
        pack_kernel,
        out_shape=jax.ShapeDtypeStruct((NY * NZ, 4, 16, 128), BF),
        in_specs=[VMEM_SPEC] * 2,
        out_specs=VMEM_SPEC,
        compiler_params=PARAMS,
        cost_estimate=COST,
        name="pack",
    )(a, b)


def assemble_kernel(in_ref, noise_ref, energy_ref):
    for y in range(NY):
        for z in range(NZ):
            for e in range(2):
                for k, out in enumerate((noise_ref, energy_ref)):
                    v = in_ref[y * NZ + z, 2 * k + e].astype(F32)
                    out[e, 16 * z:16 * z + 16, 128 * y:128 * y + 128] = v


def assemble(v):
    shape = jax.ShapeDtypeStruct((2, 128, NQ), F32)
    return pl.pallas_call(
        assemble_kernel,
        out_shape=[shape, shape],
        in_specs=[VMEM_SPEC],
        out_specs=[VMEM_SPEC] * 2,
        compiler_params=PARAMS,
        cost_estimate=COST,
        name="assemble",
    )(v)


def body(responses, labels, conductivity, permittivity):
    c = place()[3]
    tables = (conductivity, permittivity)
    labels = labels.reshape(1, labels.shape[0])
    halves = responses.reshape(16, 2, 3, 4, NQ).transpose(3, 1, 2, 0, 4).reshape(2, 2, 6, 16, NQ)

    theirs = swap(lax.dynamic_index_in_dim(halves, 1 - c, 0, keepdims=False))
    base = jnp.stack([lax.dynamic_index_in_dim(halves, c, 0, keepdims=False), theirs])

    pieces, plan = [base], [(0, 0)]
    up = down = base
    for k in (1, 2, 3):
        up, down = permute(up, along("z", 1)), permute(down, along("z", -1))
        pieces += [up, down]
        plan += [(-k, 0), (k, 0)]
    pieces += [permute(up[:1], along("z", 1)), permute(down[1:], along("z", -1))]
    plan += [(-4, 0), (4, 1)]
    rhs = columns(pieces, plan)

    def two_rings(quarter, first, second):
        ring = ring4(base[:, quarter], first)
        own = jnp.concatenate([v for part in ring for v in part]).reshape(4, NC, 6, 16, NQ)
        return [weigh(tables, labels, quarter, part) for part in ring4(own, second)]

    rows0 = two_rings(0, "y", "x")
    rows1 = two_rings(1, "x", "y")

    sums = []
    for lane in (1, 0):
        acc = gram(None, rhs[lane], rows0[:3] + rows1[:3], RING4[:3])
        acc = gram(acc, rhs[lane], rows0[3:] + rows1[3:], RING4[3:])
        sums.append(swap(acc) if lane else acc)
    packed = pack(sums[1], sums[0])
    moved = lax.all_to_all(packed, "row", 0, 0, tiled=True)
    return tuple(assemble(moved))


def solution(mesh):
    in_specs = (P(("col", "row"), None, None, None), P(), P(), P())
    out_specs = (P(None, "row", "col"), P(None, "row", "col"))
    return jax.shard_map(body, mesh=mesh, in_specs=in_specs, out_specs=out_specs, check_vma=False)
```

time: 241 us -> 97.6 us (0.40)
  waiting for transfers between devices: 196 us -> 15.6 us
  starting transfers between devices: 0.08 us -> 38.8 us
  blocking collectives: 0 us -> 22.9 us
  Pallas kernels: 0 us -> 15.5 us
  matrix products: 13.2 us -> 0 us
  between operations: 14.2 us -> 1.02 us
  other arithmetic: 11.9 us -> 0.12 us
  local copies, waits for them, and re-layouts: 5.42 us -> 1.67 us
    all_gather x1 -> x0, waiting for transfers between devices: 123 us -> none  [body(): columns = lax.all_gather(responses, 'row', axis=0, tiled=True)]
    psum x1 -> x0, waiting for transfers between devices: 72.5 us -> none  [broadcast(): return lax.psum(block, axis)]
    ppermute x0 -> x26, starting transfers between devices: none -> 38.8 us  [permute(): return lax.ppermute(v, ('row', 'col'), pairs)]
    all_to_all x0 -> x1, blocking collectives: none -> 22.9 us  [body(): moved = lax.all_to_all(packed, 'row', 0, 0, tiled=True)]
    ppermute x0 -> x26, waiting for transfers between devices: none -> 15.6 us  [permute(): return lax.ppermute(v, ('row', 'col'), pairs)]
    pallas_call x0 -> x15, Pallas kernels: none -> 15.5 us  [the longest x4 7.56 us: gram(): pl.pallas_call(lambda *refs: gram_kernel(steps, int(carried), *refs), out...]
    dot_general x1 -> x0, matrix products: 13.2 us -> none  [tile_products(): lax.dot_general(left_stack, right_flat, (((1,), (1,)), ((), ())), preferr...]
    mul x2 -> x0, other arithmetic: 6.83 us -> none  [the longest x1 6.83 us: weighted(): scaled = fields * weight_vec[None, None, None, :]]
  transfers between devices with their start and end apart: 2 -> 26, of which waited for: 2 -> 9; matrix products, arithmetic and copies ran while one was open for 0% -> 0% of each run, Pallas kernels for 0% -> 13%
where the time goes in v3:
time: 97.6 us; the launch traced here: 95.7 us
  starting transfers between devices  38.8 us (40%)
  blocking collectives  22.9 us (23%)
  waiting for transfers between devices  15.6 us (16%)
  Pallas kernels  15.5 us (16%)
  local copies, waits for them, and re-layouts  1.67 us (2%)
  between operations  1.02 us (1%)
    ppermute x26, starting transfers between devices, permute(): return lax.ppermute(v, ('row', 'col'), pairs)  38.8 us
    all_to_all x1, blocking collectives, body(): moved = lax.all_to_all(packed, 'row', 0, 0, tiled=True)  22.9 us
    ppermute x26, waiting for transfers between devices, permute(): return lax.ppermute(v, ('row', 'col'), pairs)  15.6 us
    pallas_call x4, Pallas kernels, gram(): pl.pallas_call(lambda *refs: gram_kernel(steps, int(carried), *refs), out...  7.56 us
    pallas_call x8, Pallas kernels, weigh(): pl.pallas_call(lambda *refs: weigh_kernel(count, quarter, *refs), out_sha...  6.33 us
  transfers between devices with their start and end apart: 26, of which 9 were waited for; matrix products, arithmetic and copies ran while one was open for 0% of the time, Pallas kernels for 13%

profile of v3, /device:TPU:8, one launch (start us, length us, event | category | flops | bytes accessed | tf_op | source)
XLA Modules:
  0.0 95.7 jit_solution(11977153536216683387)
XLA Ops:
  0.6 1.2 %reshape.19 = bf16[16,2,3,4,512]{4,3,1,2,0:T(4,128)(2,1)S(1)} reshape(bf16[16,2,3,2048]{3,1,2,0:T(2,128)(2,1)} %param.4) | data formatting | bytes 786432 | tf_op jit(solution)/shard_map/reshape | solution.py:203
  2.2 1.4 %collective-permute-done = bf16[2,6,16,512]{3,2,1,0:T(8,128)(2,1)S(1)} collective-permute-done((bf16[2,6,16,512]{3,2,1,0:T(8,128)(2,1)S(1)}, bf16[2,6,16,512]{3,2,1,0:T(8,128)(2,1)S(1)}, u32[]{:S(2)}, u32[]{:S(2)}) %collective-permute-start) | collective-permute-done | bytes 196640 | tf_op jit(solution)/shard_map/ppermute | solution.py:38
  3.7 1.7 %collective-permute-start.9 = (bf16[2,6,16,512]{3,2,1,0:T(8,128)(2,1)S(1)}, bf16[2,6,16,512]{3,2,1,0:T(8,128)(2,1)S(1)}, u32[]{:S(2)}, u32[]{:S(2)}) collective-permute-start(bf16[2,6,16,512]{3,2,1,0:T(8,128)(2,1)S(1)} %get-tuple-element.11), channel_id=1, source_target_pairs={{0,64},{1,65},{2,66},{3,67},{4,68},{5,69},{6,70},{7,71},{8,72},{9,... | collective-permute-start | bytes 589832 | tf_op jit(solution)/shard_map/ppermute | solution.py:38
  6.0 1.2 %collective-permute-start.15 = (bf16[2,6,16,512]{3,2,1,0:T(8,128)(2,1)S(1)}, bf16[2,6,16,512]{3,2,1,0:T(8,128)(2,1)S(1)}, u32[]{:S(2)}, u32[]{:S(2)}) collective-permute-start(bf16[2,6,16,512]{3,2,1,0:T(8,128)(2,1)S(1)} %get-tuple-element.7), channel_id=1, source_target_pairs={{0,2},{1,3},{2,4},{3,5},{4,6},{5,7},{6,0},{7,1},{8,10},{9,11},{10,... | collective-permute-start | bytes 589832 | tf_op jit(solution)/shard_map/ppermute | solution.py:38
  7.3 2.0 %collective-permute-start.16 = (bf16[2,6,16,512]{3,2,1,0:T(8,128)(2,1)S(1)}, bf16[2,6,16,512]{3,2,1,0:T(8,128)(2,1)S(1)}, u32[]{:S(2)}, u32[]{:S(2)}) collective-permute-start(bf16[2,6,16,512]{3,2,1,0:T(8,128)(2,1)S(1)} %get-tuple-element.7), channel_id=1, source_target_pairs={{0,6},{1,7},{2,0},{3,1},{4,2},{5,3},{6,4},{7,5},{8,14},{9,15},{10,... | collective-permute-start | bytes 589832 | tf_op jit(solution)/shard_map/ppermute | solution.py:38
  9.3 1.7 %collective-permute-start.1 = (bf16[2,2,6,16,512]{4,3,2,1,0:T(8,128)(2,1)S(1)}, bf16[2,2,6,16,512]{4,3,2,1,0:T(8,128)(2,1)S(1)}, u32[]{:S(2)}, u32[]{:S(2)}) collective-permute-start(bf16[2,2,6,16,512]{4,3,2,1,0:T(8,128)(2,1)S(1)} %pad_maximum_fusion.refs_0_), channel_id=1, source_target_pairs={{0,8},{1,9},{2,10},{3,11},{4,12},{5,13},{6,14},{7,15},{8,16},{9,17... | collective-permute-start | bytes 1179656 | tf_op jit(solution)/shard_map/ppermute | solution.py:38
  11.2 5.4 %collective-permute-start.2 = (bf16[2,2,6,16,512]{4,3,2,1,0:T(8,128)(2,1)S(1)}, bf16[2,2,6,16,512]{4,3,2,1,0:T(8,128)(2,1)S(1)}, u32[]{:S(2)}, u32[]{:S(2)}) collective-permute-start(bf16[2,2,6,16,512]{4,3,2,1,0:T(8,128)(2,1)S(1)} %pad_maximum_fusion.refs_0_), channel_id=1, source_target_pairs={{0,56},{1,57},{2,58},{3,59},{4,60},{5,61},{6,62},{7,63},{8,0},{9,1... | collective-permute-start | bytes 1179656 | tf_op jit(solution)/shard_map/ppermute | solution.py:38
  16.6 1.7 %collective-permute-start.11 = (bf16[1,6,16,512]{3,2,1,0:T(8,128)(2,1)S(1)}, bf16[1,6,16,512]{3,2,1,0:T(8,128)(2,1)S(1)}, u32[]{:S(2)}, u32[]{:S(2)}) collective-permute-start(bf16[1,6,16,512]{3,2,1,0:T(8,128)(2,1)S(1)} %slice.52), channel_id=1, source_target_pairs={{0,64},{1,65},{2,66},{3,67},{4,68},{5,69},{6,70},{7,71},{8,72},{9,... | collective-permute-start | bytes 294920 | tf_op jit(solution)/shard_map/ppermute | solution.py:38
  18.8 1.6 %collective-permute-start.17 = (bf16[1,6,16,512]{3,2,1,0:T(8,128)(2,1)S(1)}, bf16[1,6,16,512]{3,2,1,0:T(8,128)(2,1)S(1)}, u32[]{:S(2)}, u32[]{:S(2)}) collective-permute-start(bf16[1,6,16,512]{3,2,1,0:T(8,128)(2,1)S(1)} %slice.56), channel_id=1, source_target_pairs={{0,2},{1,3},{2,4},{3,5},{4,6},{5,7},{6,0},{7,1},{8,10},{9,11},{10,... | collective-permute-start | bytes 294920 | tf_op jit(solution)/shard_map/ppermute | solution.py:38
  20.4 0.9 collective-permute-done.11
  21.3 2.8 %collective-permute-start.18 = (bf16[1,6,16,512]{3,2,1,0:T(8,128)(2,1)S(1)}, bf16[1,6,16,512]{3,2,1,0:T(8,128)(2,1)S(1)}, u32[]{:S(2)}, u32[]{:S(2)}) collective-permute-start(bf16[1,6,16,512]{3,2,1,0:T(8,128)(2,1)S(1)} %slice.57), channel_id=1, source_target_pairs={{0,6},{1,7},{2,0},{3,1},{4,2},{5,3},{6,4},{7,5},{8,14},{9,15},{10,... | collective-permute-start | bytes 294920 | tf_op jit(solution)/shard_map/ppermute | solution.py:38
  24.7 2.8 %collective-permute-start.14 = (bf16[4,2,6,16,512]{4,3,2,1,0:T(8,128)(2,1)S(1)}, bf16[4,2,6,16,512]{4,3,2,1,0:T(8,128)(2,1)S(1)}, u32[]{:S(2)}, u32[]{:S(2)}) collective-permute-start(bf16[4,2,6,16,512]{4,3,2,1,0:T(8,128)(2,1)S(1)} %bitcast.21), channel_id=1, source_target_pairs={{0,6},{1,7},{2,0},{3,1},{4,2},{5,3},{6,4},{7,5},{8,14},{9,15},{10,... | collective-permute-start | bytes 2359304 | tf_op jit(solution)/shard_map/ppermute | solution.py:38
  27.6 3.3 %collective-permute-start.4 = (bf16[2,2,6,16,512]{4,3,2,1,0:T(8,128)(2,1)S(1)}, bf16[2,2,6,16,512]{4,3,2,1,0:T(8,128)(2,1)S(1)}, u32[]{:S(2)}, u32[]{:S(2)}) collective-permute-start(bf16[2,2,6,16,512]{4,3,2,1,0:T(8,128)(2,1)S(1)} %collective-permute-done.2.refs_2_), channel_id=1, source_target_pairs={{0,56},{1,57},{2,58},{3,59},{4,60},{5,61},{6,62},{7,63},{8,0},{9,1... | collective-permute-start | bytes 1179656 | tf_op jit(solution)/shard_map/ppermute | solution.py:38
  30.9 1.8 %collective-permute-start.19 = (bf16[4,2,6,16,512]{4,3,2,1,0:T(8,128)(2,1)S(1)}, bf16[4,2,6,16,512]{4,3,2,1,0:T(8,128)(2,1)S(1)}, u32[]{:S(2)}, u32[]{:S(2)}) collective-permute-start(bf16[4,2,6,16,512]{4,3,2,1,0:T(8,128)(2,1)S(1)} %bitcast.17), channel_id=1, source_target_pairs={{0,64},{1,65},{2,66},{3,67},{4,68},{5,69},{6,70},{7,71},{8,72},{9,... | collective-permute-start | bytes 2359304 | tf_op jit(solution)/shard_map/ppermute | solution.py:38
  32.7 1.7 %collective-permute-done.3.refs_3_ = bf16[2,2,6,16,512]{4,3,2,1,0:T(8,128)(2,1)S(1)} collective-permute-done((bf16[2,2,6,16,512]{4,3,2,1,0:T(8,128)(2,1)S(1)}, bf16[2,2,6,16,512]{4,3,2,1,0:T(8,128)(2,1)S(1)}, u32[]{:S(2)}, u32[]{:S(2)}) %collective-permute-start.3) | collective-permute-done | bytes 393248 | tf_op jit(solution)/shard_map/ppermute | solution.py:38
  34.5 3.0 %collective-permute-start.20 = (bf16[4,2,6,16,512]{4,3,2,1,0:T(8,128)(2,1)S(1)}, bf16[4,2,6,16,512]{4,3,2,1,0:T(8,128)(2,1)S(1)}, u32[]{:S(2)}, u32[]{:S(2)}) collective-permute-start(bf16[4,2,6,16,512]{4,3,2,1,0:T(8,128)(2,1)S(1)} %bitcast.18), channel_id=1, source_target_pairs={{0,192},{1,193},{2,194},{3,195},{4,196},{5,197},{6,198},{7,199},{8... | collective-permute-start | bytes 2359304 | tf_op jit(solution)/shard_map/ppermute | solution.py:38
  37.4 5.4 %collective-permute-done.13.refs_3_ = bf16[4,2,6,16,512]{4,3,2,1,0:T(8,128)(2,1)S(1)} collective-permute-done((bf16[4,2,6,16,512]{4,3,2,1,0:T(8,128)(2,1)S(1)}, bf16[4,2,6,16,512]{4,3,2,1,0:T(8,128)(2,1)S(1)}, u32[]{:S(2)}, u32[]{:S(2)}) %collective-permute-start.13) | collective-permute-done | bytes 786464 | tf_op jit(solution)/shard_map/ppermute | solution.py:38
  42.8 1.1 %collective-permute-start.6 = (bf16[2,2,6,16,512]{4,3,2,1,0:T(8,128)(2,1)S(1)}, bf16[2,2,6,16,512]{4,3,2,1,0:T(8,128)(2,1)S(1)}, u32[]{:S(2)}, u32[]{:S(2)}) collective-permute-start(bf16[2,2,6,16,512]{4,3,2,1,0:T(8,128)(2,1)S(1)} %collective-permute-done.4.refs_4_), channel_id=1, source_target_pairs={{0,56},{1,57},{2,58},{3,59},{4,60},{5,61},{6,62},{7,63},{8,0},{9,1... | collective-permute-start | bytes 1179656 | tf_op jit(solution)/shard_map/ppermute | solution.py:38
  43.9 2.6 %collective-permute-done.5.refs_5_ = bf16[2,2,6,16,512]{4,3,2,1,0:T(8,128)(2,1)S(1)} collective-permute-done((bf16[2,2,6,16,512]{4,3,2,1,0:T(8,128)(2,1)S(1)}, bf16[2,2,6,16,512]{4,3,2,1,0:T(8,128)(2,1)S(1)}, u32[]{:S(2)}, u32[]{:S(2)}) %collective-permute-start.5) | collective-permute-done | bytes 393248 | tf_op jit(solution)/shard_map/ppermute | solution.py:38
  46.6 1.0 %collective-permute-start.21 = (bf16[2,2,6,16,512]{4,3,2,1,0:T(8,128)(2,1)S(1)}, bf16[2,2,6,16,512]{4,3,2,1,0:T(8,128)(2,1)S(1)}, u32[]{:S(2)}, u32[]{:S(2)}) collective-permute-start(bf16[2,2,6,16,512]{4,3,2,1,0:T(8,128)(2,1)S(1)} %slice.58), channel_id=1, source_target_pairs={{0,2},{1,3},{2,4},{3,5},{4,6},{5,7},{6,0},{7,1},{8,10},{9,11},{10,... | collective-permute-start | bytes 1179656 | tf_op jit(solution)/shard_map/ppermute | solution.py:38
  47.7 0.9 collective-permute-done.19.refs_3_
  48.6 1.5 %collective-permute-start.22 = (bf16[2,2,6,16,512]{4,3,2,1,0:T(8,128)(2,1)S(1)}, bf16[2,2,6,16,512]{4,3,2,1,0:T(8,128)(2,1)S(1)}, u32[]{:S(2)}, u32[]{:S(2)}) collective-permute-start(bf16[2,2,6,16,512]{4,3,2,1,0:T(8,128)(2,1)S(1)} %slice.59), channel_id=1, source_target_pairs={{0,6},{1,7},{2,0},{3,1},{4,2},{5,3},{6,4},{7,5},{8,14},{9,15},{10,... | collective-permute-start | bytes 1179656 | tf_op jit(solution)/shard_map/ppermute | solution.py:38
  50.1 2.4 %collective-permute-done.20.refs_3_ = bf16[4,2,6,16,512]{4,3,2,1,0:T(8,128)(2,1)S(1)} collective-permute-done((bf16[4,2,6,16,512]{4,3,2,1,0:T(8,128)(2,1)S(1)}, bf16[4,2,6,16,512]{4,3,2,1,0:T(8,128)(2,1)S(1)}, u32[]{:S(2)}, u32[]{:S(2)}) %collective-permute-start.20) | collective-permute-done | bytes 786464 | tf_op jit(solution)/shard_map/ppermute | solution.py:38
  53.0 2.1 %collective-permute-start.24 = (bf16[2,2,6,16,512]{4,3,2,1,0:T(8,128)(2,1)S(1)}, bf16[2,2,6,16,512]{4,3,2,1,0:T(8,128)(2,1)S(1)}, u32[]{:S(2)}, u32[]{:S(2)}) collective-permute-start(bf16[2,2,6,16,512]{4,3,2,1,0:T(8,128)(2,1)S(1)} %slice.61), channel_id=1, source_target_pairs={{0,192},{1,193},{2,194},{3,195},{4,196},{5,197},{6,198},{7,199},{8... | collective-permute-start | bytes 1179656 | tf_op jit(solution)/shard_map/ppermute | solution.py:38
  55.1 1.8 %collective-permute-start.8 = (bf16[1,2,6,16,512]{4,3,2,1,0:T(8,128)(2,1)S(1)}, bf16[1,2,6,16,512]{4,3,2,1,0:T(8,128)(2,1)S(1)}, u32[]{:S(2)}, u32[]{:S(2)}) collective-permute-start(bf16[1,2,6,16,512]{4,3,2,1,0:T(8,128)(2,1)S(1)} %slice.49), channel_id=1, source_target_pairs={{0,56},{1,57},{2,58},{3,59},{4,60},{5,61},{6,62},{7,63},{8,0},{9,1... | collective-permute-start | bytes 589832 | tf_op jit(solution)/shard_map/ppermute | solution.py:38
  62.2 2.7 %gram.6.refs_0_ = f32[2,512,256]{2,1,0:T(8,128)S(1)} custom-call(bf16[256,6144]{1,0:T(8,128)(2,1)S(1)} %get-tuple-element.5.refs_0_.refs_1_, bf16[2,128,3072]{2,1,0:T(8,128)(2,1)S(1)} %weigh.8.refs_1_, bf16[2,128,3072]{2,1,0:T(8,128)(2,1)S(1)} %weigh.9.refs_2_, bf16[2,128,3072]{2,1,0:T(8,128)(2,1)S(1)} %weigh.10.refs_3_, ...), custom_call_target="tpu_custom_call" | custom-call | flops 1 | bytes 1 | tf_op jit(solution)/shard_map/gram/pallas_call | solution.py:146
  65.8 0.8 weigh.15.refs_3_
  66.6 1.0 %gram.7 = f32[2,512,256]{2,1,0:T(8,128)S(1)} custom-call(f32[2,512,256]{2,1,0:T(8,128)S(1)} %gram.6.refs_0_, bf16[256,6144]{1,0:T(8,128)(2,1)S(1)} %get-tuple-element.5.refs_0_.refs_1_, bf16[2,128,3072]{2,1,0:T(8,128)(2,1)S(1)} %weigh.14.refs_2_, bf16[2,128,3072]{2,1,0:T(8,128)(2,1)S(1)} %weigh.15.refs_3_), custom_call_target="tpu_custom_call" | custom-call | flops 1 | bytes 1 | tf_op jit(solution)/shard_map/gram/pallas_call | solution.py:146
  67.8 2.7 %gram.4.refs_0_ = f32[2,512,256]{2,1,0:T(8,128)S(1)} custom-call(bf16[256,6144]{1,0:T(8,128)(2,1)S(1)} %get-tuple-element.4.refs_0_.refs_1_, bf16[2,128,3072]{2,1,0:T(8,128)(2,1)S(1)} %weigh.8.refs_1_, bf16[2,128,3072]{2,1,0:T(8,128)(2,1)S(1)} %weigh.9.refs_2_, bf16[2,128,3072]{2,1,0:T(8,128)(2,1)S(1)} %weigh.10.refs_3_, ...), custom_call_target="tpu_custom_call" | custom-call | flops 1 | bytes 1 | tf_op jit(solution)/shard_map/gram/pallas_call | solution.py:146
  70.5 1.0 %gram.5.a_ref = f32[2,512,256]{2,1,0:T(8,128)S(1)} custom-call(f32[2,512,256]{2,1,0:T(8,128)S(1)} %gram.4.refs_0_, bf16[256,6144]{1,0:T(8,128)(2,1)S(1)} %get-tuple-element.4.refs_0_.refs_1_, bf16[2,128,3072]{2,1,0:T(8,128)(2,1)S(1)} %weigh.14.refs_2_, bf16[2,128,3072]{2,1,0:T(8,128)(2,1)S(1)} %weigh.15.refs_3_), custom_call_target="tpu_custom_call" | custom-call | flops 1 | bytes 1 | tf_op jit(solution)/shard_map/gram/pallas_call | solution.py:146
  71.7 22.9 %all_to_all.5.in_ref = bf16[32,4,16,128]{3,2,1,0:T(8,128)(2,1)S(1)} all-to-all(bf16[32,4,16,128]{3,2,1,0:T(8,128)(2,1)S(1)} %pack.1), channel_id=1, replica_groups=mesh['row'=32,'col'=8] {'row'}, dimensions={0} | all-to-all | bytes 1048576 | tf_op jit(solution)/shard_map/all_to_all | solution.py:232
  94.6 1.1 %assemble.1 = (f32[2,128,512]{2,1,0:T(8,128)}, f32[2,128,512]{2,1,0:T(8,128)}) custom-call(bf16[32,4,16,128]{3,2,1,0:T(8,128)(2,1)S(1)} %all_to_all.5.in_ref), custom_call_target="tpu_custom_call" | custom-call | flops 1 | bytes 1 | tf_op jit(solution)/shard_map/assemble/pallas_call | solution.py:188
  (65 shorter events, 9.3 us)
Async XLA Ops:
  2.1 1.5 %collective-permute-start = (bf16[2,6,16,512]{3,2,1,0:T(8,128)(2,1)S(1)}, bf16[2,6,16,512]{3,2,1,0:T(8,128)(2,1)S(1)}, u32[]{:S(2)}, u32[]{:S(2)}) collective-permute-start(bf16[2,6,16,512]{3,2,1,0:T(8,128)(2,1)S(1)} %get-tuple-element.13), channel_id=1, source_target_pairs={{0,1},{1,0},{2,3},{3,2},{4,5},{5,4},{6,7},{7,6},{8,9},{9,8},{10,11... | collective-permute-start | bytes 589832 | tf_op jit(solution)/shard_map/ppermute | solution.py:38
  3.7 7.5 %collective-permute-start.9 = (bf16[2,6,16,512]{3,2,1,0:T(8,128)(2,1)S(1)}, bf16[2,6,16,512]{3,2,1,0:T(8,128)(2,1)S(1)}, u32[]{:S(2)}, u32[]{:S(2)}) collective-permute-start(bf16[2,6,16,512]{3,2,1,0:T(8,128)(2,1)S(1)} %get-tuple-element.11), channel_id=1, source_target_pairs={{0,64},{1,65},{2,66},{3,67},{4,68},{5,69},{6,70},{7,71},{8,72},{9,... | collective-permute-start | bytes 589832 | tf_op jit(solution)/shard_map/ppermute | solution.py:38
  5.3 11.3 %collective-permute-start.10 = (bf16[2,6,16,512]{3,2,1,0:T(8,128)(2,1)S(1)}, bf16[2,6,16,512]{3,2,1,0:T(8,128)(2,1)S(1)}, u32[]{:S(2)}, u32[]{:S(2)}) collective-permute-start(bf16[2,6,16,512]{3,2,1,0:T(8,128)(2,1)S(1)} %get-tuple-element.11), channel_id=1, source_target_pairs={{0,192},{1,193},{2,194},{3,195},{4,196},{5,197},{6,198},{7,199},{8... | collective-permute-start | bytes 589832 | tf_op jit(solution)/shard_map/ppermute | solution.py:38
  6.0 12.2 %collective-permute-start.15 = (bf16[2,6,16,512]{3,2,1,0:T(8,128)(2,1)S(1)}, bf16[2,6,16,512]{3,2,1,0:T(8,128)(2,1)S(1)}, u32[]{:S(2)}, u32[]{:S(2)}) collective-permute-start(bf16[2,6,16,512]{3,2,1,0:T(8,128)(2,1)S(1)} %get-tuple-element.7), channel_id=1, source_target_pairs={{0,2},{1,3},{2,4},{3,5},{4,6},{5,7},{6,0},{7,1},{8,10},{9,11},{10,... | collective-permute-start | bytes 589832 | tf_op jit(solution)/shard_map/ppermute | solution.py:38
  7.3 11.5 %collective-permute-start.16 = (bf16[2,6,16,512]{3,2,1,0:T(8,128)(2,1)S(1)}, bf16[2,6,16,512]{3,2,1,0:T(8,128)(2,1)S(1)}, u32[]{:S(2)}, u32[]{:S(2)}) collective-permute-start(bf16[2,6,16,512]{3,2,1,0:T(8,128)(2,1)S(1)} %get-tuple-element.7), channel_id=1, source_target_pairs={{0,6},{1,7},{2,0},{3,1},{4,2},{5,3},{6,4},{7,5},{8,14},{9,15},{10,... | collective-permute-start | bytes 589832 | tf_op jit(solution)/shard_map/ppermute | solution.py:38
  9.3 15.2 %collective-permute-start.1 = (bf16[2,2,6,16,512]{4,3,2,1,0:T(8,128)(2,1)S(1)}, bf16[2,2,6,16,512]{4,3,2,1,0:T(8,128)(2,1)S(1)}, u32[]{:S(2)}, u32[]{:S(2)}) collective-permute-start(bf16[2,2,6,16,512]{4,3,2,1,0:T(8,128)(2,1)S(1)} %pad_maximum_fusion.refs_0_), channel_id=1, source_target_pairs={{0,8},{1,9},{2,10},{3,11},{4,12},{5,13},{6,14},{7,15},{8,16},{9,17... | collective-permute-start | bytes 1179656 | tf_op jit(solution)/shard_map/ppermute | solution.py:38
  11.2 16.4 %collective-permute-start.2 = (bf16[2,2,6,16,512]{4,3,2,1,0:T(8,128)(2,1)S(1)}, bf16[2,2,6,16,512]{4,3,2,1,0:T(8,128)(2,1)S(1)}, u32[]{:S(2)}, u32[]{:S(2)}) collective-permute-start(bf16[2,2,6,16,512]{4,3,2,1,0:T(8,128)(2,1)S(1)} %pad_maximum_fusion.refs_0_), channel_id=1, source_target_pairs={{0,56},{1,57},{2,58},{3,59},{4,60},{5,61},{6,62},{7,63},{8,0},{9,1... | collective-permute-start | bytes 1179656 | tf_op jit(solution)/shard_map/ppermute | solution.py:38
  16.6 4.7 %collective-permute-start.11 = (bf16[1,6,16,512]{3,2,1,0:T(8,128)(2,1)S(1)}, bf16[1,6,16,512]{3,2,1,0:T(8,128)(2,1)S(1)}, u32[]{:S(2)}, u32[]{:S(2)}) collective-permute-start(bf16[1,6,16,512]{3,2,1,0:T(8,128)(2,1)S(1)} %slice.52), channel_id=1, source_target_pairs={{0,64},{1,65},{2,66},{3,67},{4,68},{5,69},{6,70},{7,71},{8,72},{9,... | collective-permute-start | bytes 294920 | tf_op jit(solution)/shard_map/ppermute | solution.py:38
  18.3 5.8 %collective-permute-start.12 = (bf16[1,6,16,512]{3,2,1,0:T(8,128)(2,1)S(1)}, bf16[1,6,16,512]{3,2,1,0:T(8,128)(2,1)S(1)}, u32[]{:S(2)}, u32[]{:S(2)}) collective-permute-start(bf16[1,6,16,512]{3,2,1,0:T(8,128)(2,1)S(1)} %slice.53), channel_id=1, source_target_pairs={{0,192},{1,193},{2,194},{3,195},{4,196},{5,197},{6,198},{7,199},{8... | collective-permute-start | bytes 294920 | tf_op jit(solution)/shard_map/ppermute | solution.py:38
  18.8 5.9 %collective-permute-start.17 = (bf16[1,6,16,512]{3,2,1,0:T(8,128)(2,1)S(1)}, bf16[1,6,16,512]{3,2,1,0:T(8,128)(2,1)S(1)}, u32[]{:S(2)}, u32[]{:S(2)}) collective-permute-start(bf16[1,6,16,512]{3,2,1,0:T(8,128)(2,1)S(1)} %slice.56), channel_id=1, source_target_pairs={{0,2},{1,3},{2,4},{3,5},{4,6},{5,7},{6,0},{7,1},{8,10},{9,11},{10,... | collective-permute-start | bytes 294920 | tf_op jit(solution)/shard_map/ppermute | solution.py:38
  21.3 9.6 %collective-permute-start.18 = (bf16[1,6,16,512]{3,2,1,0:T(8,128)(2,1)S(1)}, bf16[1,6,16,512]{3,2,1,0:T(8,128)(2,1)S(1)}, u32[]{:S(2)}, u32[]{:S(2)}) collective-permute-start(bf16[1,6,16,512]{3,2,1,0:T(8,128)(2,1)S(1)} %slice.57), channel_id=1, source_target_pairs={{0,6},{1,7},{2,0},{3,1},{4,2},{5,3},{6,4},{7,5},{8,14},{9,15},{10,... | collective-permute-start | bytes 294920 | tf_op jit(solution)/shard_map/ppermute | solution.py:38
  24.1 18.7 %collective-permute-start.13 = (bf16[4,2,6,16,512]{4,3,2,1,0:T(8,128)(2,1)S(1)}, bf16[4,2,6,16,512]{4,3,2,1,0:T(8,128)(2,1)S(1)}, u32[]{:S(2)}, u32[]{:S(2)}) collective-permute-start(bf16[4,2,6,16,512]{4,3,2,1,0:T(8,128)(2,1)S(1)} %bitcast.20), channel_id=1, source_target_pairs={{0,2},{1,3},{2,4},{3,5},{4,6},{5,7},{6,0},{7,1},{8,10},{9,11},{10,... | collective-permute-start | bytes 2359304 | tf_op jit(solution)/shard_map/ppermute | solution.py:38
  24.6 9.9 %collective-permute-start.3 = (bf16[2,2,6,16,512]{4,3,2,1,0:T(8,128)(2,1)S(1)}, bf16[2,2,6,16,512]{4,3,2,1,0:T(8,128)(2,1)S(1)}, u32[]{:S(2)}, u32[]{:S(2)}) collective-permute-start(bf16[2,2,6,16,512]{4,3,2,1,0:T(8,128)(2,1)S(1)} %collective-permute-done.1.refs_1_), channel_id=1, source_target_pairs={{0,8},{1,9},{2,10},{3,11},{4,12},{5,13},{6,14},{7,15},{8,16},{9,17... | collective-permute-start | bytes 1179656 | tf_op jit(solution)/shard_map/ppermute | solution.py:38
  24.7 21.9 %collective-permute-start.14 = (bf16[4,2,6,16,512]{4,3,2,1,0:T(8,128)(2,1)S(1)}, bf16[4,2,6,16,512]{4,3,2,1,0:T(8,128)(2,1)S(1)}, u32[]{:S(2)}, u32[]{:S(2)}) collective-permute-start(bf16[4,2,6,16,512]{4,3,2,1,0:T(8,128)(2,1)S(1)} %bitcast.21), channel_id=1, source_target_pairs={{0,6},{1,7},{2,0},{3,1},{4,2},{5,3},{6,4},{7,5},{8,14},{9,15},{10,... | collective-permute-start | bytes 2359304 | tf_op jit(solution)/shard_map/ppermute | solution.py:38
  27.6 9.8 %collective-permute-start.4 = (bf16[2,2,6,16,512]{4,3,2,1,0:T(8,128)(2,1)S(1)}, bf16[2,2,6,16,512]{4,3,2,1,0:T(8,128)(2,1)S(1)}, u32[]{:S(2)}, u32[]{:S(2)}) collective-permute-start(bf16[2,2,6,16,512]{4,3,2,1,0:T(8,128)(2,1)S(1)} %collective-permute-done.2.refs_2_), channel_id=1, source_target_pairs={{0,56},{1,57},{2,58},{3,59},{4,60},{5,61},{6,62},{7,63},{8,0},{9,1... | collective-permute-start | bytes 1179656 | tf_op jit(solution)/shard_map/ppermute | solution.py:38
  30.9 17.7 %collective-permute-start.19 = (bf16[4,2,6,16,512]{4,3,2,1,0:T(8,128)(2,1)S(1)}, bf16[4,2,6,16,512]{4,3,2,1,0:T(8,128)(2,1)S(1)}, u32[]{:S(2)}, u32[]{:S(2)}) collective-permute-start(bf16[4,2,6,16,512]{4,3,2,1,0:T(8,128)(2,1)S(1)} %bitcast.17), channel_id=1, source_target_pairs={{0,64},{1,65},{2,66},{3,67},{4,68},{5,69},{6,70},{7,71},{8,72},{9,... | collective-permute-start | bytes 2359304 | tf_op jit(solution)/shard_map/ppermute | solution.py:38
  34.5 18.1 %collective-permute-start.20 = (bf16[4,2,6,16,512]{4,3,2,1,0:T(8,128)(2,1)S(1)}, bf16[4,2,6,16,512]{4,3,2,1,0:T(8,128)(2,1)S(1)}, u32[]{:S(2)}, u32[]{:S(2)}) collective-permute-start(bf16[4,2,6,16,512]{4,3,2,1,0:T(8,128)(2,1)S(1)} %bitcast.18), channel_id=1, source_target_pairs={{0,192},{1,193},{2,194},{3,195},{4,196},{5,197},{6,198},{7,199},{8... | collective-permute-start | bytes 2359304 | tf_op jit(solution)/shard_map/ppermute | solution.py:38
  37.4 9.1 %collective-permute-start.5 = (bf16[2,2,6,16,512]{4,3,2,1,0:T(8,128)(2,1)S(1)}, bf16[2,2,6,16,512]{4,3,2,1,0:T(8,128)(2,1)S(1)}, u32[]{:S(2)}, u32[]{:S(2)}) collective-permute-start(bf16[2,2,6,16,512]{4,3,2,1,0:T(8,128)(2,1)S(1)} %collective-permute-done.3.refs_3_), channel_id=1, source_target_pairs={{0,8},{1,9},{2,10},{3,11},{4,12},{5,13},{6,14},{7,15},{8,16},{9,17... | collective-permute-start | bytes 1179656 | tf_op jit(solution)/shard_map/ppermute | solution.py:38
  42.8 10.2 %collective-permute-start.6 = (bf16[2,2,6,16,512]{4,3,2,1,0:T(8,128)(2,1)S(1)}, bf16[2,2,6,16,512]{4,3,2,1,0:T(8,128)(2,1)S(1)}, u32[]{:S(2)}, u32[]{:S(2)}) collective-permute-start(bf16[2,2,6,16,512]{4,3,2,1,0:T(8,128)(2,1)S(1)} %collective-permute-done.4.refs_4_), channel_id=1, source_target_pairs={{0,56},{1,57},{2,58},{3,59},{4,60},{5,61},{6,62},{7,63},{8,0},{9,1... | collective-permute-start | bytes 1179656 | tf_op jit(solution)/shard_map/ppermute | solution.py:38
  43.9 13.1 %copy-start = (s32[2048]{0:T(1024)S(1)}, s32[2048]{0:T(1024)}, u32[]{:S(2)}) copy-start(s32[2048]{0:T(1024)} %param.5) | copy-start | bytes 24580
  43.9 13.1 %copy-start.1 = (f32[16]{0:T(128)S(1)}, f32[16]{0:T(128)}, u32[]{:S(2)}) copy-start(f32[16]{0:T(128)} %refs_0_.15) | copy-start | bytes 196
  43.9 13.0 %copy-start.2 = (f32[16]{0:T(128)S(1)}, f32[16]{0:T(128)}, u32[]{:S(2)}) copy-start(f32[16]{0:T(128)} %refs_1_.15) | copy-start | bytes 196
  46.5 8.6 %collective-permute-start.7 = (bf16[1,2,6,16,512]{4,3,2,1,0:T(8,128)(2,1)S(1)}, bf16[1,2,6,16,512]{4,3,2,1,0:T(8,128)(2,1)S(1)}, u32[]{:S(2)}, u32[]{:S(2)}) collective-permute-start(bf16[1,2,6,16,512]{4,3,2,1,0:T(8,128)(2,1)S(1)} %slice.48), channel_id=1, source_target_pairs={{0,8},{1,9},{2,10},{3,11},{4,12},{5,13},{6,14},{7,15},{8,16},{9,17... | collective-permute-start | bytes 589832 | tf_op jit(solution)/shard_map/ppermute | solution.py:38
  46.6 18.3 %collective-permute-start.21 = (bf16[2,2,6,16,512]{4,3,2,1,0:T(8,128)(2,1)S(1)}, bf16[2,2,6,16,512]{4,3,2,1,0:T(8,128)(2,1)S(1)}, u32[]{:S(2)}, u32[]{:S(2)}) collective-permute-start(bf16[2,2,6,16,512]{4,3,2,1,0:T(8,128)(2,1)S(1)} %slice.58), channel_id=1, source_target_pairs={{0,2},{1,3},{2,4},{3,5},{4,6},{5,7},{6,0},{7,1},{8,10},{9,11},{10,... | collective-permute-start | bytes 1179656 | tf_op jit(solution)/shard_map/ppermute | solution.py:38
  48.6 16.4 %collective-permute-start.22 = (bf16[2,2,6,16,512]{4,3,2,1,0:T(8,128)(2,1)S(1)}, bf16[2,2,6,16,512]{4,3,2,1,0:T(8,128)(2,1)S(1)}, u32[]{:S(2)}, u32[]{:S(2)}) collective-permute-start(bf16[2,2,6,16,512]{4,3,2,1,0:T(8,128)(2,1)S(1)} %slice.59), channel_id=1, source_target_pairs={{0,6},{1,7},{2,0},{3,1},{4,2},{5,3},{6,4},{7,5},{8,14},{9,15},{10,... | collective-permute-start | bytes 1179656 | tf_op jit(solution)/shard_map/ppermute | solution.py:38
  52.5 13.3 %collective-permute-start.23 = (bf16[2,2,6,16,512]{4,3,2,1,0:T(8,128)(2,1)S(1)}, bf16[2,2,6,16,512]{4,3,2,1,0:T(8,128)(2,1)S(1)}, u32[]{:S(2)}, u32[]{:S(2)}) collective-permute-start(bf16[2,2,6,16,512]{4,3,2,1,0:T(8,128)(2,1)S(1)} %slice.60), channel_id=1, source_target_pairs={{0,64},{1,65},{2,66},{3,67},{4,68},{5,69},{6,70},{7,71},{8,72},{9,... | collective-permute-start | bytes 1179656 | tf_op jit(solution)/shard_map/ppermute | solution.py:38
  53.0 12.8 %collective-permute-start.24 = (bf16[2,2,6,16,512]{4,3,2,1,0:T(8,128)(2,1)S(1)}, bf16[2,2,6,16,512]{4,3,2,1,0:T(8,128)(2,1)S(1)}, u32[]{:S(2)}, u32[]{:S(2)}) collective-permute-start(bf16[2,2,6,16,512]{4,3,2,1,0:T(8,128)(2,1)S(1)} %slice.61), channel_id=1, source_target_pairs={{0,192},{1,193},{2,194},{3,195},{4,196},{5,197},{6,198},{7,199},{8... | collective-permute-start | bytes 1179656 | tf_op jit(solution)/shard_map/ppermute | solution.py:38
  55.1 6.6 %collective-permute-start.8 = (bf16[1,2,6,16,512]{4,3,2,1,0:T(8,128)(2,1)S(1)}, bf16[1,2,6,16,512]{4,3,2,1,0:T(8,128)(2,1)S(1)}, u32[]{:S(2)}, u32[]{:S(2)}) collective-permute-start(bf16[1,2,6,16,512]{4,3,2,1,0:T(8,128)(2,1)S(1)} %slice.49), channel_id=1, source_target_pairs={{0,56},{1,57},{2,58},{3,59},{4,60},{5,61},{6,62},{7,63},{8,0},{9,1... | collective-permute-start | bytes 589832 | tf_op jit(solution)/shard_map/ppermute | solution.py:38
  67.7 3.9 %collective-permute-start.25 = (f32[2,512,256]{2,1,0:T(8,128)S(1)}, f32[2,512,256]{2,1,0:T(8,128)S(1)}, u32[]{:S(2)}, u32[]{:S(2)}) collective-permute-start(f32[2,512,256]{2,1,0:T(8,128)S(1)} %gram.7), channel_id=1, source_target_pairs={{0,1},{1,0},{2,3},{3,2},{4,5},{5,4},{6,7},{7,6},{8,9},{9,8},{10,11... | collective-permute-start | bytes 3145736 | tf_op jit(solution)/shard_map/ppermute | solution.py:38

commit v4 on v3

--- a/solution.py
+++ b/solution.py
@@ -225,9 +225,11 @@
 
     sums = []
     for lane in (1, 0):
-        acc = gram(None, rhs[lane], rows0[:3] + rows1[:3], RING4[:3])
-        acc = gram(acc, rhs[lane], rows0[3:] + rows1[3:], RING4[3:])
-        sums.append(swap(acc) if lane else acc)
+        if lane:
+            acc = gram(None, rhs[lane], rows0[:3] + rows1[:3], RING4[:3])
+            sums.append(swap(gram(acc, rhs[lane], rows0[3:] + rows1[3:], RING4[3:])))
+        else:
+            sums.append(gram(None, rhs[lane], rows0 + rows1, RING4))
     packed = pack(sums[1], sums[0])
     moved = lax.all_to_all(packed, "row", 0, 0, tiled=True)
     return tuple(assemble(moved))

time: 97.6 us -> 97.3 us (level)
    pallas_call x4 -> x3, Pallas kernels: 7.56 us -> 7.35 us  [gram(): pl.pallas_call(lambda *refs: gram_kernel(steps, int(carried), *refs), out...]
where the time goes in v4:
time: 97.3 us; the launch traced here: 95.4 us
  starting transfers between devices  38.8 us (40%)
  blocking collectives  22.9 us (24%)
  waiting for transfers between devices  15.6 us (16%)
  Pallas kernels  15.3 us (16%)
  local copies, waits for them, and re-layouts  1.67 us (2%)
  between operations  1.01 us (1%)
    ppermute x26, starting transfers between devices, permute(): return lax.ppermute(v, ('row', 'col'), pairs)  38.8 us
    all_to_all x1, blocking collectives, body(): moved = lax.all_to_all(packed, 'row', 0, 0, tiled=True)  22.9 us
    ppermute x26, waiting for transfers between devices, permute(): return lax.ppermute(v, ('row', 'col'), pairs)  15.6 us
    pallas_call x3, Pallas kernels, gram(): pl.pallas_call(lambda *refs: gram_kernel(steps, int(carried), *refs), out...  7.35 us
    pallas_call x8, Pallas kernels, weigh(): pl.pallas_call(lambda *refs: weigh_kernel(count, quarter, *refs), out_sha...  6.33 us
  transfers between devices with their start and end apart: 26, of which 9 were waited for; matrix products, arithmetic and copies ran while one was open for 0% of the time, Pallas kernels for 13%

profile of v4, /device:TPU:8, one launch (start us, length us, event | category | flops | bytes accessed | tf_op | source)
XLA Modules:
  0.0 95.4 jit_solution(14910051474551037826)
XLA Ops:
  0.6 1.2 %reshape.19 = bf16[16,2,3,4,512]{4,3,1,2,0:T(4,128)(2,1)S(1)} reshape(bf16[16,2,3,2048]{3,1,2,0:T(2,128)(2,1)} %param.4) | data formatting | bytes 786432 | tf_op jit(solution)/shard_map/reshape | solution.py:203
  2.2 1.4 %collective-permute-done = bf16[2,6,16,512]{3,2,1,0:T(8,128)(2,1)S(1)} collective-permute-done((bf16[2,6,16,512]{3,2,1,0:T(8,128)(2,1)S(1)}, bf16[2,6,16,512]{3,2,1,0:T(8,128)(2,1)S(1)}, u32[]{:S(2)}, u32[]{:S(2)}) %collective-permute-start) | collective-permute-done | bytes 196640 | tf_op jit(solution)/shard_map/ppermute | solution.py:38
  3.7 1.7 %collective-permute-start.9 = (bf16[2,6,16,512]{3,2,1,0:T(8,128)(2,1)S(1)}, bf16[2,6,16,512]{3,2,1,0:T(8,128)(2,1)S(1)}, u32[]{:S(2)}, u32[]{:S(2)}) collective-permute-start(bf16[2,6,16,512]{3,2,1,0:T(8,128)(2,1)S(1)} %get-tuple-element.11), channel_id=1, source_target_pairs={{0,64},{1,65},{2,66},{3,67},{4,68},{5,69},{6,70},{7,71},{8,72},{9,... | collective-permute-start | bytes 589832 | tf_op jit(solution)/shard_map/ppermute | solution.py:38
  6.0 1.2 %collective-permute-start.17 = (bf16[2,6,16,512]{3,2,1,0:T(8,128)(2,1)S(1)}, bf16[2,6,16,512]{3,2,1,0:T(8,128)(2,1)S(1)}, u32[]{:S(2)}, u32[]{:S(2)}) collective-permute-start(bf16[2,6,16,512]{3,2,1,0:T(8,128)(2,1)S(1)} %get-tuple-element.7), channel_id=1, source_target_pairs={{0,2},{1,3},{2,4},{3,5},{4,6},{5,7},{6,0},{7,1},{8,10},{9,11},{10,... | collective-permute-start | bytes 589832 | tf_op jit(solution)/shard_map/ppermute | solution.py:38
  7.3 2.0 %collective-permute-start.18 = (bf16[2,6,16,512]{3,2,1,0:T(8,128)(2,1)S(1)}, bf16[2,6,16,512]{3,2,1,0:T(8,128)(2,1)S(1)}, u32[]{:S(2)}, u32[]{:S(2)}) collective-permute-start(bf16[2,6,16,512]{3,2,1,0:T(8,128)(2,1)S(1)} %get-tuple-element.7), channel_id=1, source_target_pairs={{0,6},{1,7},{2,0},{3,1},{4,2},{5,3},{6,4},{7,5},{8,14},{9,15},{10,... | collective-permute-start | bytes 589832 | tf_op jit(solution)/shard_map/ppermute | solution.py:38
  9.3 1.7 %collective-permute-start.1 = (bf16[2,2,6,16,512]{4,3,2,1,0:T(8,128)(2,1)S(1)}, bf16[2,2,6,16,512]{4,3,2,1,0:T(8,128)(2,1)S(1)}, u32[]{:S(2)}, u32[]{:S(2)}) collective-permute-start(bf16[2,2,6,16,512]{4,3,2,1,0:T(8,128)(2,1)S(1)} %pad_maximum_fusion.refs_0_), channel_id=1, source_target_pairs={{0,8},{1,9},{2,10},{3,11},{4,12},{5,13},{6,14},{7,15},{8,16},{9,17... | collective-permute-start | bytes 1179656 | tf_op jit(solution)/shard_map/ppermute | solution.py:38
  11.2 5.4 %collective-permute-start.2 = (bf16[2,2,6,16,512]{4,3,2,1,0:T(8,128)(2,1)S(1)}, bf16[2,2,6,16,512]{4,3,2,1,0:T(8,128)(2,1)S(1)}, u32[]{:S(2)}, u32[]{:S(2)}) collective-permute-start(bf16[2,2,6,16,512]{4,3,2,1,0:T(8,128)(2,1)S(1)} %pad_maximum_fusion.refs_0_), channel_id=1, source_target_pairs={{0,56},{1,57},{2,58},{3,59},{4,60},{5,61},{6,62},{7,63},{8,0},{9,1... | collective-permute-start | bytes 1179656 | tf_op jit(solution)/shard_map/ppermute | solution.py:38
  16.6 1.7 %collective-permute-start.11 = (bf16[1,6,16,512]{3,2,1,0:T(8,128)(2,1)S(1)}, bf16[1,6,16,512]{3,2,1,0:T(8,128)(2,1)S(1)}, u32[]{:S(2)}, u32[]{:S(2)}) collective-permute-start(bf16[1,6,16,512]{3,2,1,0:T(8,128)(2,1)S(1)} %slice.52), channel_id=1, source_target_pairs={{0,64},{1,65},{2,66},{3,67},{4,68},{5,69},{6,70},{7,71},{8,72},{9,... | collective-permute-start | bytes 294920 | tf_op jit(solution)/shard_map/ppermute | solution.py:38
  18.8 1.6 %collective-permute-start.19 = (bf16[1,6,16,512]{3,2,1,0:T(8,128)(2,1)S(1)}, bf16[1,6,16,512]{3,2,1,0:T(8,128)(2,1)S(1)}, u32[]{:S(2)}, u32[]{:S(2)}) collective-permute-start(bf16[1,6,16,512]{3,2,1,0:T(8,128)(2,1)S(1)} %slice.58), channel_id=1, source_target_pairs={{0,2},{1,3},{2,4},{3,5},{4,6},{5,7},{6,0},{7,1},{8,10},{9,11},{10,... | collective-permute-start | bytes 294920 | tf_op jit(solution)/shard_map/ppermute | solution.py:38
  20.4 0.9 collective-permute-done.11
  21.3 2.8 %collective-permute-start.20 = (bf16[1,6,16,512]{3,2,1,0:T(8,128)(2,1)S(1)}, bf16[1,6,16,512]{3,2,1,0:T(8,128)(2,1)S(1)}, u32[]{:S(2)}, u32[]{:S(2)}) collective-permute-start(bf16[1,6,16,512]{3,2,1,0:T(8,128)(2,1)S(1)} %slice.59), channel_id=1, source_target_pairs={{0,6},{1,7},{2,0},{3,1},{4,2},{5,3},{6,4},{7,5},{8,14},{9,15},{10,... | collective-permute-start | bytes 294920 | tf_op jit(solution)/shard_map/ppermute | solution.py:38
  24.7 2.8 %collective-permute-start.14 = (bf16[4,2,6,16,512]{4,3,2,1,0:T(8,128)(2,1)S(1)}, bf16[4,2,6,16,512]{4,3,2,1,0:T(8,128)(2,1)S(1)}, u32[]{:S(2)}, u32[]{:S(2)}) collective-permute-start(bf16[4,2,6,16,512]{4,3,2,1,0:T(8,128)(2,1)S(1)} %bitcast.21), channel_id=1, source_target_pairs={{0,6},{1,7},{2,0},{3,1},{4,2},{5,3},{6,4},{7,5},{8,14},{9,15},{10,... | collective-permute-start | bytes 2359304 | tf_op jit(solution)/shard_map/ppermute | solution.py:38
  27.6 3.3 %collective-permute-start.4 = (bf16[2,2,6,16,512]{4,3,2,1,0:T(8,128)(2,1)S(1)}, bf16[2,2,6,16,512]{4,3,2,1,0:T(8,128)(2,1)S(1)}, u32[]{:S(2)}, u32[]{:S(2)}) collective-permute-start(bf16[2,2,6,16,512]{4,3,2,1,0:T(8,128)(2,1)S(1)} %collective-permute-done.2.refs_2_), channel_id=1, source_target_pairs={{0,56},{1,57},{2,58},{3,59},{4,60},{5,61},{6,62},{7,63},{8,0},{9,1... | collective-permute-start | bytes 1179656 | tf_op jit(solution)/shard_map/ppermute | solution.py:38
  30.9 1.8 %collective-permute-start.21 = (bf16[4,2,6,16,512]{4,3,2,1,0:T(8,128)(2,1)S(1)}, bf16[4,2,6,16,512]{4,3,2,1,0:T(8,128)(2,1)S(1)}, u32[]{:S(2)}, u32[]{:S(2)}) collective-permute-start(bf16[4,2,6,16,512]{4,3,2,1,0:T(8,128)(2,1)S(1)} %bitcast.17), channel_id=1, source_target_pairs={{0,64},{1,65},{2,66},{3,67},{4,68},{5,69},{6,70},{7,71},{8,72},{9,... | collective-permute-start | bytes 2359304 | tf_op jit(solution)/shard_map/ppermute | solution.py:38
  32.7 1.7 %collective-permute-done.3.refs_3_ = bf16[2,2,6,16,512]{4,3,2,1,0:T(8,128)(2,1)S(1)} collective-permute-done((bf16[2,2,6,16,512]{4,3,2,1,0:T(8,128)(2,1)S(1)}, bf16[2,2,6,16,512]{4,3,2,1,0:T(8,128)(2,1)S(1)}, u32[]{:S(2)}, u32[]{:S(2)}) %collective-permute-start.3) | collective-permute-done | bytes 393248 | tf_op jit(solution)/shard_map/ppermute | solution.py:38
  34.5 3.0 %collective-permute-start.22 = (bf16[4,2,6,16,512]{4,3,2,1,0:T(8,128)(2,1)S(1)}, bf16[4,2,6,16,512]{4,3,2,1,0:T(8,128)(2,1)S(1)}, u32[]{:S(2)}, u32[]{:S(2)}) collective-permute-start(bf16[4,2,6,16,512]{4,3,2,1,0:T(8,128)(2,1)S(1)} %bitcast.18), channel_id=1, source_target_pairs={{0,192},{1,193},{2,194},{3,195},{4,196},{5,197},{6,198},{7,199},{8... | collective-permute-start | bytes 2359304 | tf_op jit(solution)/shard_map/ppermute | solution.py:38
  37.4 5.4 %collective-permute-done.13.refs_3_ = bf16[4,2,6,16,512]{4,3,2,1,0:T(8,128)(2,1)S(1)} collective-permute-done((bf16[4,2,6,16,512]{4,3,2,1,0:T(8,128)(2,1)S(1)}, bf16[4,2,6,16,512]{4,3,2,1,0:T(8,128)(2,1)S(1)}, u32[]{:S(2)}, u32[]{:S(2)}) %collective-permute-start.13) | collective-permute-done | bytes 786464 | tf_op jit(solution)/shard_map/ppermute | solution.py:38
  42.8 1.1 %collective-permute-start.6 = (bf16[2,2,6,16,512]{4,3,2,1,0:T(8,128)(2,1)S(1)}, bf16[2,2,6,16,512]{4,3,2,1,0:T(8,128)(2,1)S(1)}, u32[]{:S(2)}, u32[]{:S(2)}) collective-permute-start(bf16[2,2,6,16,512]{4,3,2,1,0:T(8,128)(2,1)S(1)} %collective-permute-done.4.refs_4_), channel_id=1, source_target_pairs={{0,56},{1,57},{2,58},{3,59},{4,60},{5,61},{6,62},{7,63},{8,0},{9,1... | collective-permute-start | bytes 1179656 | tf_op jit(solution)/shard_map/ppermute | solution.py:38
  43.9 2.6 %collective-permute-done.5.refs_5_ = bf16[2,2,6,16,512]{4,3,2,1,0:T(8,128)(2,1)S(1)} collective-permute-done((bf16[2,2,6,16,512]{4,3,2,1,0:T(8,128)(2,1)S(1)}, bf16[2,2,6,16,512]{4,3,2,1,0:T(8,128)(2,1)S(1)}, u32[]{:S(2)}, u32[]{:S(2)}) %collective-permute-start.5) | collective-permute-done | bytes 393248 | tf_op jit(solution)/shard_map/ppermute | solution.py:38
  46.6 1.0 %collective-permute-start.15 = (bf16[2,2,6,16,512]{4,3,2,1,0:T(8,128)(2,1)S(1)}, bf16[2,2,6,16,512]{4,3,2,1,0:T(8,128)(2,1)S(1)}, u32[]{:S(2)}, u32[]{:S(2)}) collective-permute-start(bf16[2,2,6,16,512]{4,3,2,1,0:T(8,128)(2,1)S(1)} %slice.54), channel_id=1, source_target_pairs={{0,2},{1,3},{2,4},{3,5},{4,6},{5,7},{6,0},{7,1},{8,10},{9,11},{10,... | collective-permute-start | bytes 1179656 | tf_op jit(solution)/shard_map/ppermute | solution.py:38
  47.7 0.9 collective-permute-done.21.refs_3_
  48.6 1.5 %collective-permute-start.16 = (bf16[2,2,6,16,512]{4,3,2,1,0:T(8,128)(2,1)S(1)}, bf16[2,2,6,16,512]{4,3,2,1,0:T(8,128)(2,1)S(1)}, u32[]{:S(2)}, u32[]{:S(2)}) collective-permute-start(bf16[2,2,6,16,512]{4,3,2,1,0:T(8,128)(2,1)S(1)} %slice.55), channel_id=1, source_target_pairs={{0,6},{1,7},{2,0},{3,1},{4,2},{5,3},{6,4},{7,5},{8,14},{9,15},{10,... | collective-permute-start | bytes 1179656 | tf_op jit(solution)/shard_map/ppermute | solution.py:38
  50.1 2.4 %collective-permute-done.22.refs_3_ = bf16[4,2,6,16,512]{4,3,2,1,0:T(8,128)(2,1)S(1)} collective-permute-done((bf16[4,2,6,16,512]{4,3,2,1,0:T(8,128)(2,1)S(1)}, bf16[4,2,6,16,512]{4,3,2,1,0:T(8,128)(2,1)S(1)}, u32[]{:S(2)}, u32[]{:S(2)}) %collective-permute-start.22) | collective-permute-done | bytes 786464 | tf_op jit(solution)/shard_map/ppermute | solution.py:38
  53.0 2.1 %collective-permute-start.24 = (bf16[2,2,6,16,512]{4,3,2,1,0:T(8,128)(2,1)S(1)}, bf16[2,2,6,16,512]{4,3,2,1,0:T(8,128)(2,1)S(1)}, u32[]{:S(2)}, u32[]{:S(2)}) collective-permute-start(bf16[2,2,6,16,512]{4,3,2,1,0:T(8,128)(2,1)S(1)} %slice.61), channel_id=1, source_target_pairs={{0,192},{1,193},{2,194},{3,195},{4,196},{5,197},{6,198},{7,199},{8... | collective-permute-start | bytes 1179656 | tf_op jit(solution)/shard_map/ppermute | solution.py:38
  55.1 1.8 %collective-permute-start.8 = (bf16[1,2,6,16,512]{4,3,2,1,0:T(8,128)(2,1)S(1)}, bf16[1,2,6,16,512]{4,3,2,1,0:T(8,128)(2,1)S(1)}, u32[]{:S(2)}, u32[]{:S(2)}) collective-permute-start(bf16[1,2,6,16,512]{4,3,2,1,0:T(8,128)(2,1)S(1)} %slice.49), channel_id=1, source_target_pairs={{0,56},{1,57},{2,58},{3,59},{4,60},{5,61},{6,62},{7,63},{8,0},{9,1... | collective-permute-start | bytes 589832 | tf_op jit(solution)/shard_map/ppermute | solution.py:38
  57.8 0.8 weigh.12.refs_5_.refs_4_
  62.2 2.7 %gram.4.refs_0_ = f32[2,512,256]{2,1,0:T(8,128)S(1)} custom-call(bf16[256,6144]{1,0:T(8,128)(2,1)S(1)} %get-tuple-element.5.refs_0_.refs_1_, bf16[2,128,3072]{2,1,0:T(8,128)(2,1)S(1)} %weigh.8.refs_1_, bf16[2,128,3072]{2,1,0:T(8,128)(2,1)S(1)} %weigh.9.refs_2_, bf16[2,128,3072]{2,1,0:T(8,128)(2,1)S(1)} %weigh.10.refs_3_, ...), custom_call_target="tpu_custom_call" | custom-call | flops 1 | bytes 1 | tf_op jit(solution)/shard_map/gram/pallas_call | solution.py:146
  65.8 0.8 weigh.15.refs_8_.refs_3_
  66.6 1.0 %gram.5 = f32[2,512,256]{2,1,0:T(8,128)S(1)} custom-call(f32[2,512,256]{2,1,0:T(8,128)S(1)} %gram.4.refs_0_, bf16[256,6144]{1,0:T(8,128)(2,1)S(1)} %get-tuple-element.5.refs_0_.refs_1_, bf16[2,128,3072]{2,1,0:T(8,128)(2,1)S(1)} %weigh.11.refs_4_.refs_2_, bf16[2,128,3072]{2,1,0:T(8,128)(2,1)S(1)} %weigh.15.refs_8_.refs_3_), custom_call_target="tpu_custom_call" | custom-call | flops 1 | bytes 1 | tf_op jit(solution)/shard_map/gram/pallas_call | solution.py:146
  67.8 3.6 %gram.3.a_ref = f32[2,512,256]{2,1,0:T(8,128)S(1)} custom-call(bf16[256,6144]{1,0:T(8,128)(2,1)S(1)} %get-tuple-element.4.refs_0_, bf16[2,128,3072]{2,1,0:T(8,128)(2,1)S(1)} %weigh.8.refs_1_, bf16[2,128,3072]{2,1,0:T(8,128)(2,1)S(1)} %weigh.9.refs_2_, bf16[2,128,3072]{2,1,0:T(8,128)(2,1)S(1)} %weigh.10.refs_3_, ...), custom_call_target="tpu_custom_call" | custom-call | flops 1 | bytes 1 | tf_op jit(solution)/shard_map/gram/pallas_call | solution.py:146
  71.5 22.9 %all_to_all.5.in_ref = bf16[32,4,16,128]{3,2,1,0:T(8,128)(2,1)S(1)} all-to-all(bf16[32,4,16,128]{3,2,1,0:T(8,128)(2,1)S(1)} %pack.1), channel_id=1, replica_groups=mesh['row'=32,'col'=8] {'row'}, dimensions={0} | all-to-all | bytes 1048576 | tf_op jit(solution)/shard_map/all_to_all | solution.py:234
  94.3 1.1 %assemble.1 = (f32[2,128,512]{2,1,0:T(8,128)}, f32[2,128,512]{2,1,0:T(8,128)}) custom-call(bf16[32,4,16,128]{3,2,1,0:T(8,128)(2,1)S(1)} %all_to_all.5.in_ref), custom_call_target="tpu_custom_call" | custom-call | flops 1 | bytes 1 | tf_op jit(solution)/shard_map/assemble/pallas_call | solution.py:188
  (64 shorter events, 8.5 us)
Async XLA Ops:
  2.1 1.5 %collective-permute-start = (bf16[2,6,16,512]{3,2,1,0:T(8,128)(2,1)S(1)}, bf16[2,6,16,512]{3,2,1,0:T(8,128)(2,1)S(1)}, u32[]{:S(2)}, u32[]{:S(2)}) collective-permute-start(bf16[2,6,16,512]{3,2,1,0:T(8,128)(2,1)S(1)} %get-tuple-element.13), channel_id=1, source_target_pairs={{0,1},{1,0},{2,3},{3,2},{4,5},{5,4},{6,7},{7,6},{8,9},{9,8},{10,11... | collective-permute-start | bytes 589832 | tf_op jit(solution)/shard_map/ppermute | solution.py:38
  3.7 7.5 %collective-permute-start.9 = (bf16[2,6,16,512]{3,2,1,0:T(8,128)(2,1)S(1)}, bf16[2,6,16,512]{3,2,1,0:T(8,128)(2,1)S(1)}, u32[]{:S(2)}, u32[]{:S(2)}) collective-permute-start(bf16[2,6,16,512]{3,2,1,0:T(8,128)(2,1)S(1)} %get-tuple-element.11), channel_id=1, source_target_pairs={{0,64},{1,65},{2,66},{3,67},{4,68},{5,69},{6,70},{7,71},{8,72},{9,... | collective-permute-start | bytes 589832 | tf_op jit(solution)/shard_map/ppermute | solution.py:38
  5.3 11.3 %collective-permute-start.10 = (bf16[2,6,16,512]{3,2,1,0:T(8,128)(2,1)S(1)}, bf16[2,6,16,512]{3,2,1,0:T(8,128)(2,1)S(1)}, u32[]{:S(2)}, u32[]{:S(2)}) collective-permute-start(bf16[2,6,16,512]{3,2,1,0:T(8,128)(2,1)S(1)} %get-tuple-element.11), channel_id=1, source_target_pairs={{0,192},{1,193},{2,194},{3,195},{4,196},{5,197},{6,198},{7,199},{8... | collective-permute-start | bytes 589832 | tf_op jit(solution)/shard_map/ppermute | solution.py:38
  6.0 12.2 %collective-permute-start.17 = (bf16[2,6,16,512]{3,2,1,0:T(8,128)(2,1)S(1)}, bf16[2,6,16,512]{3,2,1,0:T(8,128)(2,1)S(1)}, u32[]{:S(2)}, u32[]{:S(2)}) collective-permute-start(bf16[2,6,16,512]{3,2,1,0:T(8,128)(2,1)S(1)} %get-tuple-element.7), channel_id=1, source_target_pairs={{0,2},{1,3},{2,4},{3,5},{4,6},{5,7},{6,0},{7,1},{8,10},{9,11},{10,... | collective-permute-start | bytes 589832 | tf_op jit(solution)/shard_map/ppermute | solution.py:38
  7.3 11.5 %collective-permute-start.18 = (bf16[2,6,16,512]{3,2,1,0:T(8,128)(2,1)S(1)}, bf16[2,6,16,512]{3,2,1,0:T(8,128)(2,1)S(1)}, u32[]{:S(2)}, u32[]{:S(2)}) collective-permute-start(bf16[2,6,16,512]{3,2,1,0:T(8,128)(2,1)S(1)} %get-tuple-element.7), channel_id=1, source_target_pairs={{0,6},{1,7},{2,0},{3,1},{4,2},{5,3},{6,4},{7,5},{8,14},{9,15},{10,... | collective-permute-start | bytes 589832 | tf_op jit(solution)/shard_map/ppermute | solution.py:38
  9.3 15.2 %collective-permute-start.1 = (bf16[2,2,6,16,512]{4,3,2,1,0:T(8,128)(2,1)S(1)}, bf16[2,2,6,16,512]{4,3,2,1,0:T(8,128)(2,1)S(1)}, u32[]{:S(2)}, u32[]{:S(2)}) collective-permute-start(bf16[2,2,6,16,512]{4,3,2,1,0:T(8,128)(2,1)S(1)} %pad_maximum_fusion.refs_0_), channel_id=1, source_target_pairs={{0,8},{1,9},{2,10},{3,11},{4,12},{5,13},{6,14},{7,15},{8,16},{9,17... | collective-permute-start | bytes 1179656 | tf_op jit(solution)/shard_map/ppermute | solution.py:38
  11.2 16.4 %collective-permute-start.2 = (bf16[2,2,6,16,512]{4,3,2,1,0:T(8,128)(2,1)S(1)}, bf16[2,2,6,16,512]{4,3,2,1,0:T(8,128)(2,1)S(1)}, u32[]{:S(2)}, u32[]{:S(2)}) collective-permute-start(bf16[2,2,6,16,512]{4,3,2,1,0:T(8,128)(2,1)S(1)} %pad_maximum_fusion.refs_0_), channel_id=1, source_target_pairs={{0,56},{1,57},{2,58},{3,59},{4,60},{5,61},{6,62},{7,63},{8,0},{9,1... | collective-permute-start | bytes 1179656 | tf_op jit(solution)/shard_map/ppermute | solution.py:38
  16.6 4.7 %collective-permute-start.11 = (bf16[1,6,16,512]{3,2,1,0:T(8,128)(2,1)S(1)}, bf16[1,6,16,512]{3,2,1,0:T(8,128)(2,1)S(1)}, u32[]{:S(2)}, u32[]{:S(2)}) collective-permute-start(bf16[1,6,16,512]{3,2,1,0:T(8,128)(2,1)S(1)} %slice.52), channel_id=1, source_target_pairs={{0,64},{1,65},{2,66},{3,67},{4,68},{5,69},{6,70},{7,71},{8,72},{9,... | collective-permute-start | bytes 294920 | tf_op jit(solution)/shard_map/ppermute | solution.py:38
  18.3 5.8 %collective-permute-start.12 = (bf16[1,6,16,512]{3,2,1,0:T(8,128)(2,1)S(1)}, bf16[1,6,16,512]{3,2,1,0:T(8,128)(2,1)S(1)}, u32[]{:S(2)}, u32[]{:S(2)}) collective-permute-start(bf16[1,6,16,512]{3,2,1,0:T(8,128)(2,1)S(1)} %slice.53), channel_id=1, source_target_pairs={{0,192},{1,193},{2,194},{3,195},{4,196},{5,197},{6,198},{7,199},{8... | collective-permute-start | bytes 294920 | tf_op jit(solution)/shard_map/ppermute | solution.py:38
  18.8 5.9 %collective-permute-start.19 = (bf16[1,6,16,512]{3,2,1,0:T(8,128)(2,1)S(1)}, bf16[1,6,16,512]{3,2,1,0:T(8,128)(2,1)S(1)}, u32[]{:S(2)}, u32[]{:S(2)}) collective-permute-start(bf16[1,6,16,512]{3,2,1,0:T(8,128)(2,1)S(1)} %slice.58), channel_id=1, source_target_pairs={{0,2},{1,3},{2,4},{3,5},{4,6},{5,7},{6,0},{7,1},{8,10},{9,11},{10,... | collective-permute-start | bytes 294920 | tf_op jit(solution)/shard_map/ppermute | solution.py:38
  21.3 9.6 %collective-permute-start.20 = (bf16[1,6,16,512]{3,2,1,0:T(8,128)(2,1)S(1)}, bf16[1,6,16,512]{3,2,1,0:T(8,128)(2,1)S(1)}, u32[]{:S(2)}, u32[]{:S(2)}) collective-permute-start(bf16[1,6,16,512]{3,2,1,0:T(8,128)(2,1)S(1)} %slice.59), channel_id=1, source_target_pairs={{0,6},{1,7},{2,0},{3,1},{4,2},{5,3},{6,4},{7,5},{8,14},{9,15},{10,... | collective-permute-start | bytes 294920 | tf_op jit(solution)/shard_map/ppermute | solution.py:38
  24.1 18.7 %collective-permute-start.13 = (bf16[4,2,6,16,512]{4,3,2,1,0:T(8,128)(2,1)S(1)}, bf16[4,2,6,16,512]{4,3,2,1,0:T(8,128)(2,1)S(1)}, u32[]{:S(2)}, u32[]{:S(2)}) collective-permute-start(bf16[4,2,6,16,512]{4,3,2,1,0:T(8,128)(2,1)S(1)} %bitcast.20), channel_id=1, source_target_pairs={{0,2},{1,3},{2,4},{3,5},{4,6},{5,7},{6,0},{7,1},{8,10},{9,11},{10,... | collective-permute-start | bytes 2359304 | tf_op jit(solution)/shard_map/ppermute | solution.py:38
  24.6 9.9 %collective-permute-start.3 = (bf16[2,2,6,16,512]{4,3,2,1,0:T(8,128)(2,1)S(1)}, bf16[2,2,6,16,512]{4,3,2,1,0:T(8,128)(2,1)S(1)}, u32[]{:S(2)}, u32[]{:S(2)}) collective-permute-start(bf16[2,2,6,16,512]{4,3,2,1,0:T(8,128)(2,1)S(1)} %collective-permute-done.1.refs_1_), channel_id=1, source_target_pairs={{0,8},{1,9},{2,10},{3,11},{4,12},{5,13},{6,14},{7,15},{8,16},{9,17... | collective-permute-start | bytes 1179656 | tf_op jit(solution)/shard_map/ppermute | solution.py:38
  24.7 21.9 %collective-permute-start.14 = (bf16[4,2,6,16,512]{4,3,2,1,0:T(8,128)(2,1)S(1)}, bf16[4,2,6,16,512]{4,3,2,1,0:T(8,128)(2,1)S(1)}, u32[]{:S(2)}, u32[]{:S(2)}) collective-permute-start(bf16[4,2,6,16,512]{4,3,2,1,0:T(8,128)(2,1)S(1)} %bitcast.21), channel_id=1, source_target_pairs={{0,6},{1,7},{2,0},{3,1},{4,2},{5,3},{6,4},{7,5},{8,14},{9,15},{10,... | collective-permute-start | bytes 2359304 | tf_op jit(solution)/shard_map/ppermute | solution.py:38
  27.6 9.8 %collective-permute-start.4 = (bf16[2,2,6,16,512]{4,3,2,1,0:T(8,128)(2,1)S(1)}, bf16[2,2,6,16,512]{4,3,2,1,0:T(8,128)(2,1)S(1)}, u32[]{:S(2)}, u32[]{:S(2)}) collective-permute-start(bf16[2,2,6,16,512]{4,3,2,1,0:T(8,128)(2,1)S(1)} %collective-permute-done.2.refs_2_), channel_id=1, source_target_pairs={{0,56},{1,57},{2,58},{3,59},{4,60},{5,61},{6,62},{7,63},{8,0},{9,1... | collective-permute-start | bytes 1179656 | tf_op jit(solution)/shard_map/ppermute | solution.py:38
  30.9 17.7 %collective-permute-start.21 = (bf16[4,2,6,16,512]{4,3,2,1,0:T(8,128)(2,1)S(1)}, bf16[4,2,6,16,512]{4,3,2,1,0:T(8,128)(2,1)S(1)}, u32[]{:S(2)}, u32[]{:S(2)}) collective-permute-start(bf16[4,2,6,16,512]{4,3,2,1,0:T(8,128)(2,1)S(1)} %bitcast.17), channel_id=1, source_target_pairs={{0,64},{1,65},{2,66},{3,67},{4,68},{5,69},{6,70},{7,71},{8,72},{9,... | collective-permute-start | bytes 2359304 | tf_op jit(solution)/shard_map/ppermute | solution.py:38
  34.5 18.1 %collective-permute-start.22 = (bf16[4,2,6,16,512]{4,3,2,1,0:T(8,128)(2,1)S(1)}, bf16[4,2,6,16,512]{4,3,2,1,0:T(8,128)(2,1)S(1)}, u32[]{:S(2)}, u32[]{:S(2)}) collective-permute-start(bf16[4,2,6,16,512]{4,3,2,1,0:T(8,128)(2,1)S(1)} %bitcast.18), channel_id=1, source_target_pairs={{0,192},{1,193},{2,194},{3,195},{4,196},{5,197},{6,198},{7,199},{8... | collective-permute-start | bytes 2359304 | tf_op jit(solution)/shard_map/ppermute | solution.py:38
  37.4 9.1 %collective-permute-start.5 = (bf16[2,2,6,16,512]{4,3,2,1,0:T(8,128)(2,1)S(1)}, bf16[2,2,6,16,512]{4,3,2,1,0:T(8,128)(2,1)S(1)}, u32[]{:S(2)}, u32[]{:S(2)}) collective-permute-start(bf16[2,2,6,16,512]{4,3,2,1,0:T(8,128)(2,1)S(1)} %collective-permute-done.3.refs_3_), channel_id=1, source_target_pairs={{0,8},{1,9},{2,10},{3,11},{4,12},{5,13},{6,14},{7,15},{8,16},{9,17... | collective-permute-start | bytes 1179656 | tf_op jit(solution)/shard_map/ppermute | solution.py:38
  42.8 10.2 %collective-permute-start.6 = (bf16[2,2,6,16,512]{4,3,2,1,0:T(8,128)(2,1)S(1)}, bf16[2,2,6,16,512]{4,3,2,1,0:T(8,128)(2,1)S(1)}, u32[]{:S(2)}, u32[]{:S(2)}) collective-permute-start(bf16[2,2,6,16,512]{4,3,2,1,0:T(8,128)(2,1)S(1)} %collective-permute-done.4.refs_4_), channel_id=1, source_target_pairs={{0,56},{1,57},{2,58},{3,59},{4,60},{5,61},{6,62},{7,63},{8,0},{9,1... | collective-permute-start | bytes 1179656 | tf_op jit(solution)/shard_map/ppermute | solution.py:38
  43.9 13.1 %copy-start = (s32[2048]{0:T(1024)S(1)}, s32[2048]{0:T(1024)}, u32[]{:S(2)}) copy-start(s32[2048]{0:T(1024)} %param.5) | copy-start | bytes 24580
  43.9 13.1 %copy-start.1 = (f32[16]{0:T(128)S(1)}, f32[16]{0:T(128)}, u32[]{:S(2)}) copy-start(f32[16]{0:T(128)} %refs_0_.15) | copy-start | bytes 196
  43.9 13.0 %copy-start.2 = (f32[16]{0:T(128)S(1)}, f32[16]{0:T(128)}, u32[]{:S(2)}) copy-start(f32[16]{0:T(128)} %refs_1_.15) | copy-start | bytes 196
  46.5 8.6 %collective-permute-start.7 = (bf16[1,2,6,16,512]{4,3,2,1,0:T(8,128)(2,1)S(1)}, bf16[1,2,6,16,512]{4,3,2,1,0:T(8,128)(2,1)S(1)}, u32[]{:S(2)}, u32[]{:S(2)}) collective-permute-start(bf16[1,2,6,16,512]{4,3,2,1,0:T(8,128)(2,1)S(1)} %slice.48), channel_id=1, source_target_pairs={{0,8},{1,9},{2,10},{3,11},{4,12},{5,13},{6,14},{7,15},{8,16},{9,17... | collective-permute-start | bytes 589832 | tf_op jit(solution)/shard_map/ppermute | solution.py:38
  46.6 18.3 %collective-permute-start.15 = (bf16[2,2,6,16,512]{4,3,2,1,0:T(8,128)(2,1)S(1)}, bf16[2,2,6,16,512]{4,3,2,1,0:T(8,128)(2,1)S(1)}, u32[]{:S(2)}, u32[]{:S(2)}) collective-permute-start(bf16[2,2,6,16,512]{4,3,2,1,0:T(8,128)(2,1)S(1)} %slice.54), channel_id=1, source_target_pairs={{0,2},{1,3},{2,4},{3,5},{4,6},{5,7},{6,0},{7,1},{8,10},{9,11},{10,... | collective-permute-start | bytes 1179656 | tf_op jit(solution)/shard_map/ppermute | solution.py:38
  48.6 16.4 %collective-permute-start.16 = (bf16[2,2,6,16,512]{4,3,2,1,0:T(8,128)(2,1)S(1)}, bf16[2,2,6,16,512]{4,3,2,1,0:T(8,128)(2,1)S(1)}, u32[]{:S(2)}, u32[]{:S(2)}) collective-permute-start(bf16[2,2,6,16,512]{4,3,2,1,0:T(8,128)(2,1)S(1)} %slice.55), channel_id=1, source_target_pairs={{0,6},{1,7},{2,0},{3,1},{4,2},{5,3},{6,4},{7,5},{8,14},{9,15},{10,... | collective-permute-start | bytes 1179656 | tf_op jit(solution)/shard_map/ppermute | solution.py:38
  52.5 13.3 %collective-permute-start.23 = (bf16[2,2,6,16,512]{4,3,2,1,0:T(8,128)(2,1)S(1)}, bf16[2,2,6,16,512]{4,3,2,1,0:T(8,128)(2,1)S(1)}, u32[]{:S(2)}, u32[]{:S(2)}) collective-permute-start(bf16[2,2,6,16,512]{4,3,2,1,0:T(8,128)(2,1)S(1)} %slice.60), channel_id=1, source_target_pairs={{0,64},{1,65},{2,66},{3,67},{4,68},{5,69},{6,70},{7,71},{8,72},{9,... | collective-permute-start | bytes 1179656 | tf_op jit(solution)/shard_map/ppermute | solution.py:38
  53.0 12.8 %collective-permute-start.24 = (bf16[2,2,6,16,512]{4,3,2,1,0:T(8,128)(2,1)S(1)}, bf16[2,2,6,16,512]{4,3,2,1,0:T(8,128)(2,1)S(1)}, u32[]{:S(2)}, u32[]{:S(2)}) collective-permute-start(bf16[2,2,6,16,512]{4,3,2,1,0:T(8,128)(2,1)S(1)} %slice.61), channel_id=1, source_target_pairs={{0,192},{1,193},{2,194},{3,195},{4,196},{5,197},{6,198},{7,199},{8... | collective-permute-start | bytes 1179656 | tf_op jit(solution)/shard_map/ppermute | solution.py:38
  55.1 6.6 %collective-permute-start.8 = (bf16[1,2,6,16,512]{4,3,2,1,0:T(8,128)(2,1)S(1)}, bf16[1,2,6,16,512]{4,3,2,1,0:T(8,128)(2,1)S(1)}, u32[]{:S(2)}, u32[]{:S(2)}) collective-permute-start(bf16[1,2,6,16,512]{4,3,2,1,0:T(8,128)(2,1)S(1)} %slice.49), channel_id=1, source_target_pairs={{0,56},{1,57},{2,58},{3,59},{4,60},{5,61},{6,62},{7,63},{8,0},{9,1... | collective-permute-start | bytes 589832 | tf_op jit(solution)/shard_map/ppermute | solution.py:38
  67.7 3.7 %collective-permute-start.25 = (f32[2,512,256]{2,1,0:T(8,128)S(1)}, f32[2,512,256]{2,1,0:T(8,128)S(1)}, u32[]{:S(2)}, u32[]{:S(2)}) collective-permute-start(f32[2,512,256]{2,1,0:T(8,128)S(1)} %gram.5), channel_id=1, source_target_pairs={{0,1},{1,0},{2,3},{3,2},{4,5},{5,4},{6,7},{7,6},{8,9},{9,8},{10,11... | collective-permute-start | bytes 3145736 | tf_op jit(solution)/shard_map/ppermute | solution.py:38
